TPU v7x, 512 devices: a whole 4x8x8 slice. The times are simulated.
512 devices in a mesh: image: 16 (over z_hi, x), space: 32 (over z_lo, y, core).
Axes of the slice: x: 4, y: 8, z: 8 (z_hi: 4, z_lo: 2; z = z_hi * 2 + z_lo), core: 2. Of those that a mesh axis runs over, the one named last changes fastest.
Arguments:
- displacement: float32 [16, 3, 32768], P('image', None, 'space'), may hold values from -0.5 to 0.5
- end_states: float32 [2, 3, 32768], P(None, None, 'space'), may hold values from -0.5 to 0.5
- atom_live: int32 [32768], P('space'), may hold values 0 or 1
- partner_cells: int32 [256, 5], P('space'), may hold values from 0 to 11, as said below
- partner_live: int32 [256, 5], P('space'), may hold values from 0 to 1
- spring_const: float32 [16], P('image'), may hold values from 2 to 20
Outputs:
- band_force: float32 [16, 3, 32768], P('image', None, 'space')
- path_stats: float32 [16, 3], P('image')
Inputs may be any that keep to these rules, and one draw needn't show every extreme that they name: `partner_cells`: each cell's live entries name the cell itself (index c + 2), the cells c + 1 and c + 3, and for some cells c or c + 4; the live entries are symmetric between cells of the image (counting cells modulo 256); entries come in any order and dead entries name arbitrary cells.
All inputs are finite; a program needn't handle non-finite values. No bound on the sum of `atom_live` on one device may be relied on, other than what follows from the above.
Results may differ from a plain program's by a relative error of at most 0.0003.
Values sent between devices are 32-bit elements; how exact they have to be, the bound alone decides.
No kernel may reach another device: no remote copies, remote signals or barrier semaphores. Data moves between devices by JAX's collectives and lax.ppermute only.
A program may use at most 64 MiB of HBM per device.

v0:
```python
import jax
import jax.numpy as jnp
from jax import lax
from jax.sharding import PartitionSpec as P

SLOTS = 128
GHOST = 2
ITERATIONS = 6


cutoff_sq = 9.0
pair_strength = 0.4
step_size = 0.02
epsilon = 1e-06
tile_block = 2


def extended_2(cells, sides, width, closed):
    for axis, dim in sides:
        count = lax.axis_size(axis)
        ends = count if closed else count - 1
        head = lax.slice_in_dim(cells, 0, width, axis=dim)
        tail = lax.slice_in_dim(cells, cells.shape[dim] - width, cells.shape[dim], axis=dim)
        cells = jnp.concatenate(
            [
                lax.ppermute(tail, axis, [(i, (i + 1) % count) for i in range(ends)]),
                cells,
                lax.ppermute(head, axis, [((i + 1) % count, i) for i in range(ends)]),
            ],
            axis=dim,
        )
    return cells


def from_everyone(shard, axis):
    length = lax.axis_size(axis)
    return lax.all_to_all(
        jnp.broadcast_to(shard[None], (length, *shard.shape)), axis, 0, 0, tiled=True
    )


def of_everyone(shard, axis):
    return from_everyone(shard, axis).sum(axis=0)


def in_one(arrays, axis):
    ends = [0]
    for a in arrays:
        ends.append(ends[-1] + a.size)
    so_far = of_everyone(jnp.concatenate([a.ravel() for a in arrays]), axis)
    return tuple((so_far[b:e].reshape(a.shape) for a, b, e in zip(arrays, ends, ends[1:])))


def site_table():
    slot_ids = jnp.arange(SLOTS, dtype=jnp.int32)
    return jnp.stack([slot_ids // 64, slot_ids // 8 % 8, slot_ids % 8]).astype(jnp.float32)


def tile_weight(own_live, partner_atoms, tile_live, self_tile, partner):
    diagonal = (
        jnp.arange(SLOTS, dtype=jnp.int32)[:, None] == jnp.arange(SLOTS, dtype=jnp.int32)[None, :]
    )
    weight = (
        own_live[:, :, None]
        * partner_atoms[:, partner, None, :]
        * tile_live[:, partner, None, None]
    )
    return jnp.where(self_tile[:, partner, None, None] & diagonal[None], jnp.float32(0.0), weight)


def pair_geometry(own_sites, partner_sites, partner):
    separation = own_sites[:, :, :, None] - partner_sites[:, partner, :, None, :]
    scaled = jnp.sum(separation * separation, axis=1) / cutoff_sq
    remain = jnp.where(scaled < 1.0, 1.0 - scaled, jnp.float32(0.0))
    return (separation, remain)


def density_cells(own_sites, partner_sites, own_live, partner_atoms, tile_live, self_tile):
    density = jnp.zeros(own_live.shape, jnp.float32)
    for partner in range(partner_sites.shape[1]):
        separation, remain = pair_geometry(own_sites, partner_sites, partner)
        weight = tile_weight(own_live, partner_atoms, tile_live, self_tile, partner)
        density = density + jnp.sum(weight * remain**4, axis=-1)
    return density


def force_cells(
    own_sites,
    partner_sites,
    own_live,
    partner_atoms,
    tile_live,
    self_tile,
    own_slope,
    partner_slope,
):
    total = jnp.zeros(own_sites.shape, jnp.float32)
    for partner in range(partner_sites.shape[1]):
        separation, remain = pair_geometry(own_sites, partner_sites, partner)
        weight = tile_weight(own_live, partner_atoms, tile_live, self_tile, partner)
        slopes = own_slope[:, :, None] + partner_slope[:, partner, None, :]
        coefficient = slopes * (-4.0 * remain**3) + pair_strength * (-3.0 * remain**2)
        total = total + jnp.sum((weight * coefficient)[:, None] * separation, axis=-1)
    return -(2.0 / cutoff_sq) * total


def blocked(function, block_cells, *arrays):
    total_rows = arrays[0].shape[0]
    shaped = tuple(
        (item.reshape((total_rows // block_cells, block_cells) + item.shape[1:]) for item in arrays)
    )
    result = lax.map(lambda group: function(*group), shaped)
    return result.reshape((total_rows,) + result.shape[2:])


def body(displacement, end_states, atom_live, partner_cells, partner_live, spring_const):
    cell_count = partner_cells.shape[0]
    tile_count = partner_cells.shape[1]
    extended_cells = cell_count + 2 * GHOST
    deep_cells = cell_count + 4 * GHOST
    live_flat = atom_live.astype(jnp.float32)
    own_live = live_flat.reshape(cell_count, SLOTS)
    tile_live = partner_live.astype(jnp.float32)
    self_tile = partner_cells == (GHOST + jnp.arange(cell_count, dtype=jnp.int32))[:, None]
    site = site_table()
    axis_unit = jnp.array([1.0, 0.0, 0.0], jnp.float32)
    cell_offsets = (2 * jnp.arange(extended_cells, dtype=jnp.int32)).astype(jnp.float32)
    deep_offsets = (2 * jnp.arange(deep_cells, dtype=jnp.int32)).astype(jnp.float32)
    tables = jnp.concatenate([partner_cells, partner_live], axis=1)
    wide_tables = extended_2(tables, (("space", 0),), GHOST, True)
    wide_cells = wide_tables[:, :tile_count]
    wide_tlive = wide_tables[:, tile_count:].astype(jnp.float32)
    wide_pos = GHOST + jnp.arange(extended_cells, dtype=jnp.int32)
    wide_local = (wide_pos - 2 * GHOST) % cell_count
    wide_index = jnp.clip(
        wide_pos[:, None] + wide_cells - GHOST - wide_local[:, None], 0, deep_cells - 1
    )
    wide_self = wide_cells == (wide_local + GHOST)[:, None]
    image_index = lax.axis_index("image")
    image_count = lax.axis_size("image")
    moved = displacement
    for iteration in range(ITERATIONS):
        both = extended_2(moved, (("image", 0),), 1, False)
        upstream = both[0:1]
        downstream = both[2:3]
        upstream = jnp.where(image_index == 0, end_states[0:1], upstream)
        downstream = jnp.where(image_index == image_count - 1, end_states[1:2], downstream)
        forward_gap = (downstream - moved)[0] * live_flat
        backward_gap = (moved - upstream)[0] * live_flat
        packed = jnp.concatenate([moved[0], live_flat[None]], axis=0)
        deep = extended_2(packed, (("space", 1),), 2 * GHOST * SLOTS, True)
        deep = deep.reshape(4, deep_cells, SLOTS)
        deep_placed = (
            deep[:3] + site[:, None, :] + deep_offsets[None, :, None] * axis_unit[:, None, None]
        )
        wide_own = deep_placed[:, GHOST : GHOST + extended_cells].transpose(1, 0, 2)
        wide_partner = deep_placed[:, wide_index].transpose(1, 2, 0, 3)
        wide_atoms = deep[3][wide_index]
        wide_live = deep[3][GHOST : GHOST + extended_cells]
        wide_density = blocked(
            density_cells,
            tile_block,
            wide_own,
            wide_partner,
            wide_live,
            wide_atoms,
            wide_tlive,
            wide_self,
        )
        slope_all = -0.5 / jnp.sqrt(1.0 + wide_density) * wide_live
        slope = slope_all[GHOST : GHOST + cell_count]
        extended = deep[:, GHOST : GHOST + extended_cells]
        placed = (
            extended[:3] + site[:, None, :] + cell_offsets[None, :, None] * axis_unit[:, None, None]
        )
        own_sites = placed[:, GHOST : GHOST + cell_count].transpose(1, 0, 2)
        partner_sites = placed[:, partner_cells].transpose(1, 2, 0, 3)
        partner_atoms = extended[3][partner_cells]
        partner_slope = slope_all[partner_cells]
        force = blocked(
            force_cells,
            tile_block,
            own_sites,
            partner_sites,
            own_live,
            partner_atoms,
            tile_live,
            self_tile,
            slope,
            partner_slope,
        )
        force = force.transpose(1, 0, 2).reshape(3, -1)
        forward_sq, backward_sq, cross_sum, force_ahead, force_behind = in_one(
            (
                jnp.sum(forward_gap * forward_gap),
                jnp.sum(backward_gap * backward_gap),
                jnp.sum(forward_gap * backward_gap),
                jnp.sum(force * forward_gap),
                jnp.sum(force * backward_gap),
            ),
            "space",
        )
        length_ahead = jnp.sqrt(forward_sq + epsilon)
        length_behind = jnp.sqrt(backward_sq + epsilon)
        tangent_sq = (
            forward_sq / length_ahead**2
            + backward_sq / length_behind**2
            + 2.0 * cross_sum / (length_ahead * length_behind)
        )
        tangent_len = jnp.sqrt(jnp.maximum(tangent_sq, 1.0))
        tangent = (forward_gap / length_ahead + backward_gap / length_behind) / tangent_len
        parallel = (force_ahead / length_ahead + force_behind / length_behind) / tangent_len
        cosine = cross_sum / (length_ahead * length_behind)
        spring_term = spring_const[0] * (length_ahead - length_behind)
        band_force = force + (spring_term - parallel) * tangent
        path_stats = jnp.stack([parallel, spring_term, cosine])
        moved = moved + step_size * band_force[None]
    return (band_force[None], path_stats[None])


def solution(mesh):
    return jax.shard_map(
        body,
        mesh=mesh,
        in_specs=(
            P("image", None, "space"),
            P(None, None, "space"),
            P("space"),
            P("space", None),
            P("space", None),
            P("image"),
        ),
        out_specs=(P("image", None, "space"), P("image", None)),
        check_vma=False,
    )
```

profile of v0, /device:TPU:134, one launch (start us, length us, event | category | flops | bytes accessed | tf_op | source)
XLA Modules:
  0.0 384.0 jit_solution(12861890882926459524)
XLA Ops:
  1.4 2.7 collective-permute-start.4
  4.1 7.3 %collective-permute-start.5 = (f32[1,3,1024]{2,1,0:T(4,128)S(1)}, f32[1,3,1024]{2,1,0:T(4,128)S(1)}, u32[]{:S(2)}, u32[]{:S(2)}) collective-permute-start(f32[1,3,1024]{2,1,0:T(4,128)S(1)} %copy.577), channel_id=1, source_target_pairs={{0,32},{32,64},{64,96},{96,128},{128,160},{160,192},{192,224},{224... | collective-permute-start | bytes 36872 | tf_op jit(solution)/shard_map/ppermute | solution.py:26
  11.5 6.1 %collective-permute-start.1 = (f32[4,512]{1,0:T(4,128)S(1)}, f32[4,512]{1,0:T(4,128)S(1)}, u32[]{:S(2)}, u32[]{:S(2)}) collective-permute-start(f32[4,512]{1,0:T(4,128)S(1)} %get-tuple-element.2425), channel_id=1, source_target_pairs={{1,0},{2,1},{3,2},{4,3},{5,4},{6,5},{7,6},{8,7},{9,8},{10,9},{11,1... | collective-permute-start | bytes 24584 | tf_op jit(solution)/shard_map/ppermute | solution.py:28
  17.7 3.1 collective-permute-start.3
  20.8 1.9 collective-permute-start.2
  23.9 1.9 collective-permute-start
  25.8 2.0 collective-permute-done.2
  28.2 2.8 collective-permute-done
  33.9 9.0 %while.138 = (s32[]{:T(128)}, f32[6,2,128]{2,1,0:T(2,128)S(1)}, pred[6,2,5]{2,1,0:T(4,128)(4,1)S(1)}, f32[6,2,128]{2,1,0:T(2,128)S(1)}, f32[6,2,5,128]{3,1,2,0:T...) while((s32[]{:T(128)}, f32[6,2,128]{2,1,0:T(2,128)S(1)}, ...), condition=%wide.region_11.12_spmd, body=%wide.region_0.11_spmd.sunk | while | flops 3292930 | bytes 1492347 | solution.py:112
  44.8 9.5 %while.139 = (s32[]{:T(128)}, f32[4,2,3,128]{3,1,0,2:T(2,128)S(1)}, pred[4,2,5]{2,1,0:T(4,128)(4,1)S(1)}, f32[4,2,128]{2,1,0:T(2,128)S(1)}, f32[4,2,5,128]{3,1,2...) while((s32[]{:T(128)}, f32[4,2,3,128]{3,1,0,2:T(2,128)S(1)}, ...), condition=%wide.region_23.24_spmd, body=%wide.region_12.23_spmd.sunk | while | flops 5423106 | bytes 2890123 | solution.py:112
  55.6 3.2 concatenate.68
  59.5 3.9 %all-to-all-start = ((f32[32,1,5]{2,1,0:T(1,128)}), f32[32,1,5]{2,1,0:T(1,128)S(1)}, u32[]{:S(2)}, u32[]{:S(2)}) async-start(f32[32,1,5]{2,1,0:T(1,128)} %broadcast_in_dim.303), calls=%async_computation | async-start | bytes 32768 | tf_op jit(solution)/shard_map/all_to_all | solution.py:37
  64.0 7.8 %all-to-all-done = f32[32,1,5]{2,1,0:T(1,128)S(1)} async-done(((f32[32,1,5]{2,1,0:T(1,128)}), f32[32,1,5]{2,1,0:T(1,128)S(1)}, u32[]{:S(2)}, u32[]{:S(2)}) %all-to-all-start) | async-done | bytes 672 | tf_op jit(solution)/shard_map/all_to_all | solution.py:37
  79.1 2.4 collective-permute-start.6
  83.4 8.1 %collective-permute-start.9 = (f32[1,3,1024]{2,1,0:T(4,128)S(1)}, f32[1,3,1024]{2,1,0:T(4,128)S(1)}, u32[]{:S(2)}, u32[]{:S(2)}) collective-permute-start(f32[1,3,1024]{2,1,0:T(4,128)S(1)} %multiply_add_fusion.5), channel_id=1, source_target_pairs={{0,32},{32,64},{64,96},{96,128},{128,160},{160,192},{192,224},{224... | collective-permute-start | bytes 36872 | tf_op jit(solution)/shard_map/ppermute | solution.py:26
  93.8 9.0 %while.140 = (s32[]{:T(128)}, f32[6,2,128]{2,1,0:T(2,128)S(1)}, pred[6,2,5]{2,1,0:T(4,128)(4,1)S(1)}, f32[6,2,128]{2,1,0:T(2,128)S(1)}, f32[6,2,5,128]{3,1,2,0:T...) while((s32[]{:T(128)}, f32[6,2,128]{2,1,0:T(2,128)S(1)}, ...), condition=%wide.region_41.42_spmd, body=%wide.region_30.41_spmd.sunk | while | flops 3292930 | bytes 1492347 | solution.py:112
  104.8 9.5 %while.141 = (s32[]{:T(128)}, f32[4,2,3,128]{3,1,0,2:T(2,128)S(1)}, pred[4,2,5]{2,1,0:T(4,128)(4,1)S(1)}, f32[4,2,128]{2,1,0:T(2,128)S(1)}, f32[4,2,5,128]{3,1,2...) while((s32[]{:T(128)}, f32[4,2,3,128]{3,1,0,2:T(2,128)S(1)}, ...), condition=%wide.region_53.54_spmd, body=%wide.region_42.53_spmd.sunk | while | flops 5423106 | bytes 2890123 | solution.py:112
  115.7 3.2 concatenate.71
  119.5 4.5 %all-to-all-start.1 = ((f32[32,1,5]{2,1,0:T(1,128)}), f32[32,1,5]{2,1,0:T(1,128)S(1)}, u32[]{:S(2)}, u32[]{:S(2)}) async-start(f32[32,1,5]{2,1,0:T(1,128)} %broadcast_in_dim.304), calls=%async_computation.1 | async-start | bytes 32768 | tf_op jit(solution)/shard_map/all_to_all | solution.py:37
  124.0 8.4 %all-to-all-done.1 = f32[32,1,5]{2,1,0:T(1,128)S(1)} async-done(((f32[32,1,5]{2,1,0:T(1,128)}), f32[32,1,5]{2,1,0:T(1,128)S(1)}, u32[]{:S(2)}, u32[]{:S(2)}) %all-to-all-start.1) | async-done | bytes 672 | tf_op jit(solution)/shard_map/all_to_all | solution.py:37
  139.7 2.4 collective-permute-start.10
  144.0 8.3 %collective-permute-start.13 = (f32[1,3,1024]{2,1,0:T(4,128)S(1)}, f32[1,3,1024]{2,1,0:T(4,128)S(1)}, u32[]{:S(2)}, u32[]{:S(2)}) collective-permute-start(f32[1,3,1024]{2,1,0:T(4,128)S(1)} %multiply_add_fusion.4), channel_id=1, source_target_pairs={{0,32},{32,64},{64,96},{96,128},{128,160},{160,192},{192,224},{224... | collective-permute-start | bytes 36872 | tf_op jit(solution)/shard_map/ppermute | solution.py:26
  155.1 9.0 %while.142 = (s32[]{:T(128)}, f32[6,2,128]{2,1,0:T(2,128)S(1)}, pred[6,2,5]{2,1,0:T(4,128)(4,1)S(1)}, f32[6,2,128]{2,1,0:T(2,128)S(1)}, f32[6,2,5,128]{3,1,2,0:T...) while((s32[]{:T(128)}, f32[6,2,128]{2,1,0:T(2,128)S(1)}, ...), condition=%wide.region_71.72_spmd, body=%wide.region_60.71_spmd.sunk | while | flops 3292930 | bytes 1492347 | solution.py:112
  166.2 9.5 %while.143 = (s32[]{:T(128)}, f32[4,2,3,128]{3,1,0,2:T(2,128)S(1)}, pred[4,2,5]{2,1,0:T(4,128)(4,1)S(1)}, f32[4,2,128]{2,1,0:T(2,128)S(1)}, f32[4,2,5,128]{3,1,2...) while((s32[]{:T(128)}, f32[4,2,3,128]{3,1,0,2:T(2,128)S(1)}, ...), condition=%wide.region_83.84_spmd, body=%wide.region_72.83_spmd.sunk | while | flops 5423106 | bytes 2890123 | solution.py:112
  177.0 3.2 concatenate.74
  180.8 4.5 %all-to-all-start.2 = ((f32[32,1,5]{2,1,0:T(1,128)}), f32[32,1,5]{2,1,0:T(1,128)S(1)}, u32[]{:S(2)}, u32[]{:S(2)}) async-start(f32[32,1,5]{2,1,0:T(1,128)} %broadcast_in_dim.305), calls=%async_computation.2 | async-start | bytes 32768 | tf_op jit(solution)/shard_map/all_to_all | solution.py:37
  185.3 8.4 %all-to-all-done.2 = f32[32,1,5]{2,1,0:T(1,128)S(1)} async-done(((f32[32,1,5]{2,1,0:T(1,128)}), f32[32,1,5]{2,1,0:T(1,128)S(1)}, u32[]{:S(2)}, u32[]{:S(2)}) %all-to-all-start.2) | async-done | bytes 672 | tf_op jit(solution)/shard_map/all_to_all | solution.py:37
  201.1 2.4 collective-permute-start.14
  205.4 8.1 %collective-permute-start.17 = (f32[1,3,1024]{2,1,0:T(4,128)S(1)}, f32[1,3,1024]{2,1,0:T(4,128)S(1)}, u32[]{:S(2)}, u32[]{:S(2)}) collective-permute-start(f32[1,3,1024]{2,1,0:T(4,128)S(1)} %multiply_add_fusion.3), channel_id=1, source_target_pairs={{0,32},{32,64},{64,96},{96,128},{128,160},{160,192},{192,224},{224... | collective-permute-start | bytes 36872 | tf_op jit(solution)/shard_map/ppermute | solution.py:26
  216.3 9.0 %while.144 = (s32[]{:T(128)}, f32[6,2,128]{2,1,0:T(2,128)S(1)}, pred[6,2,5]{2,1,0:T(4,128)(4,1)S(1)}, f32[6,2,128]{2,1,0:T(2,128)S(1)}, f32[6,2,5,128]{3,1,2,0:T...) while((s32[]{:T(128)}, f32[6,2,128]{2,1,0:T(2,128)S(1)}, ...), condition=%wide.region_101.102_spmd, body=%wide.region_90.101_spmd.sunk | while | flops 3292930 | bytes 1492347 | solution.py:112
  227.3 9.5 %while.145 = (s32[]{:T(128)}, f32[4,2,3,128]{3,1,0,2:T(2,128)S(1)}, pred[4,2,5]{2,1,0:T(4,128)(4,1)S(1)}, f32[4,2,128]{2,1,0:T(2,128)S(1)}, f32[4,2,5,128]{3,1,2...) while((s32[]{:T(128)}, f32[4,2,3,128]{3,1,0,2:T(2,128)S(1)}, ...), condition=%wide.region_113.114_spmd, body=%wide.region_102.113_spmd.sunk | while | flops 5423106 | bytes 2890123 | solution.py:112
  238.2 3.2 concatenate.77
  242.0 4.5 %all-to-all-start.3 = ((f32[32,1,5]{2,1,0:T(1,128)}), f32[32,1,5]{2,1,0:T(1,128)S(1)}, u32[]{:S(2)}, u32[]{:S(2)}) async-start(f32[32,1,5]{2,1,0:T(1,128)} %broadcast_in_dim.306), calls=%async_computation.3 | async-start | bytes 32768 | tf_op jit(solution)/shard_map/all_to_all | solution.py:37
  246.5 8.4 %all-to-all-done.3 = f32[32,1,5]{2,1,0:T(1,128)S(1)} async-done(((f32[32,1,5]{2,1,0:T(1,128)}), f32[32,1,5]{2,1,0:T(1,128)S(1)}, u32[]{:S(2)}, u32[]{:S(2)}) %all-to-all-start.3) | async-done | bytes 672 | tf_op jit(solution)/shard_map/all_to_all | solution.py:37
  262.2 2.4 collective-permute-start.18
  266.6 8.1 %collective-permute-start.21 = (f32[1,3,1024]{2,1,0:T(4,128)S(1)}, f32[1,3,1024]{2,1,0:T(4,128)S(1)}, u32[]{:S(2)}, u32[]{:S(2)}) collective-permute-start(f32[1,3,1024]{2,1,0:T(4,128)S(1)} %multiply_add_fusion.2), channel_id=1, source_target_pairs={{0,32},{32,64},{64,96},{96,128},{128,160},{160,192},{192,224},{224... | collective-permute-start | bytes 36872 | tf_op jit(solution)/shard_map/ppermute | solution.py:26
  277.5 9.0 %while.146 = (s32[]{:T(128)}, f32[6,2,128]{2,1,0:T(2,128)S(1)}, pred[6,2,5]{2,1,0:T(4,128)(4,1)S(1)}, f32[6,2,128]{2,1,0:T(2,128)S(1)}, f32[6,2,5,128]{3,1,2,0:T...) while((s32[]{:T(128)}, f32[6,2,128]{2,1,0:T(2,128)S(1)}, ...), condition=%wide.region_131.132_spmd, body=%wide.region_120.131_spmd.sunk | while | flops 3292930 | bytes 1492347 | solution.py:112
  288.5 9.5 %while.147 = (s32[]{:T(128)}, f32[4,2,3,128]{3,1,0,2:T(2,128)S(1)}, pred[4,2,5]{2,1,0:T(4,128)(4,1)S(1)}, f32[4,2,128]{2,1,0:T(2,128)S(1)}, f32[4,2,5,128]{3,1,2...) while((s32[]{:T(128)}, f32[4,2,3,128]{3,1,0,2:T(2,128)S(1)}, ...), condition=%wide.region_143.144_spmd, body=%wide.region_132.143_spmd.sunk | while | flops 5423106 | bytes 2890123 | solution.py:112
  299.4 3.2 concatenate.80
  303.2 4.5 %all-to-all-start.4 = ((f32[32,1,5]{2,1,0:T(1,128)}), f32[32,1,5]{2,1,0:T(1,128)S(1)}, u32[]{:S(2)}, u32[]{:S(2)}) async-start(f32[32,1,5]{2,1,0:T(1,128)} %broadcast_in_dim.307), calls=%async_computation.4 | async-start | bytes 32768 | tf_op jit(solution)/shard_map/all_to_all | solution.py:37
  307.7 8.4 %all-to-all-done.4 = f32[32,1,5]{2,1,0:T(1,128)S(1)} async-done(((f32[32,1,5]{2,1,0:T(1,128)}), f32[32,1,5]{2,1,0:T(1,128)S(1)}, u32[]{:S(2)}, u32[]{:S(2)}) %all-to-all-start.4) | async-done | bytes 672 | tf_op jit(solution)/shard_map/all_to_all | solution.py:37
  323.4 2.4 collective-permute-start.22
  327.8 8.1 %collective-permute-start.25 = (f32[1,3,1024]{2,1,0:T(4,128)S(1)}, f32[1,3,1024]{2,1,0:T(4,128)S(1)}, u32[]{:S(2)}, u32[]{:S(2)}) collective-permute-start(f32[1,3,1024]{2,1,0:T(4,128)S(1)} %multiply_add_fusion.1), channel_id=1, source_target_pairs={{0,32},{32,64},{64,96},{96,128},{128,160},{160,192},{192,224},{224... | collective-permute-start | bytes 36872 | tf_op jit(solution)/shard_map/ppermute | solution.py:26
  338.1 8.9 %while.148 = (s32[]{:T(128)}, f32[6,2,128]{2,1,0:T(2,128)S(1)}, pred[6,2,5]{2,1,0:T(4,128)(4,1)S(1)}, f32[6,2,128]{2,1,0:T(2,128)S(1)}, f32[6,2,5,128]{3,1,2,0:T...) while((s32[]{:T(128)}, f32[6,2,128]{2,1,0:T(2,128)S(1)}, ...), condition=%wide.region_161.162_spmd, body=%wide.region_150.161_spmd.sunk | while | flops 3292930 | bytes 1492347 | solution.py:112
  349.1 9.5 %while.149 = (s32[]{:T(128)}, f32[4,2,3,128]{3,1,0,2:T(2,128)S(1)}, pred[4,2,5]{2,1,0:T(4,128)(4,1)S(1)}, f32[4,2,128]{2,1,0:T(2,128)S(1)}, f32[4,2,5,128]{3,1,2...) while((s32[]{:T(128)}, f32[4,2,3,128]{3,1,0,2:T(2,128)S(1)}, ...), condition=%wide.region_173.174_spmd, body=%wide.region_162.173_spmd.sunk | while | flops 5423106 | bytes 2890123 | solution.py:112
  360.0 3.3 concatenate.83
  363.8 4.5 %all-to-all-start.5 = ((f32[32,1,5]{2,1,0:T(1,128)}), f32[32,1,5]{2,1,0:T(1,128)S(1)}, u32[]{:S(2)}, u32[]{:S(2)}) async-start(f32[32,1,5]{2,1,0:T(1,128)} %broadcast_in_dim.308), calls=%async_computation.5 | async-start | bytes 32768 | tf_op jit(solution)/shard_map/all_to_all | solution.py:37
  368.3 8.4 %all-to-all-done.5 = f32[32,1,5]{2,1,0:T(1,128)S(1)} async-done(((f32[32,1,5]{2,1,0:T(1,128)}), f32[32,1,5]{2,1,0:T(1,128)S(1)}, u32[]{:S(2)}, u32[]{:S(2)}) %all-to-all-start.5) | async-done | bytes 672 | tf_op jit(solution)/shard_map/all_to_all | solution.py:37
  (1330 shorter events, 169.8 us)
Async XLA Ops:
  0.6 10.8 %copy-start.10 = (s32[1024]{0:T(1024)S(1)}, s32[1024]{0:T(1024)}, u32[]{:S(2)}) copy-start(s32[1024]{0:T(1024)} %param.33) | copy-start | bytes 12292
  1.4 52.9 %collective-permute-start.4 = (f32[1,3,1024]{2,1,0:T(4,128)S(1)}, f32[1,3,1024]{2,1,0:T(4,128)S(1)}, u32[]{:S(2)}, u32[]{:S(2)}) collective-permute-start(f32[1,3,1024]{2,1,0:T(4,128)S(1)} %copy.577), channel_id=1, source_target_pairs={{32,0},{64,32},{96,64},{128,96},{160,128},{192,160},{224,192},{256... | collective-permute-start | bytes 36872 | tf_op jit(solution)/shard_map/ppermute | solution.py:28
  4.1 50.2 %collective-permute-start.5 = (f32[1,3,1024]{2,1,0:T(4,128)S(1)}, f32[1,3,1024]{2,1,0:T(4,128)S(1)}, u32[]{:S(2)}, u32[]{:S(2)}) collective-permute-start(f32[1,3,1024]{2,1,0:T(4,128)S(1)} %copy.577), channel_id=1, source_target_pairs={{0,32},{32,64},{64,96},{96,128},{128,160},{160,192},{192,224},{224... | collective-permute-start | bytes 36872 | tf_op jit(solution)/shard_map/ppermute | solution.py:26
  11.4 6.1 %copy-start.7 = (s32[8,5]{1,0:T(8,128)S(1)}, s32[8,5]{1,0:T(8,128)}, u32[]{:S(2)}) copy-start(s32[8,5]{1,0:T(8,128)} %param.34) | copy-start | bytes 484
  11.5 6.1 %copy-start.8 = (s32[8,5]{1,0:T(8,128)S(1)}, s32[8,5]{1,0:T(8,128)}, u32[]{:S(2)}) copy-start(s32[8,5]{1,0:T(8,128)} %param.35) | copy-start | bytes 484
  11.5 16.7 %collective-permute-start.1 = (f32[4,512]{1,0:T(4,128)S(1)}, f32[4,512]{1,0:T(4,128)S(1)}, u32[]{:S(2)}, u32[]{:S(2)}) collective-permute-start(f32[4,512]{1,0:T(4,128)S(1)} %get-tuple-element.2425), channel_id=1, source_target_pairs={{1,0},{2,1},{3,2},{4,3},{5,4},{6,5},{7,6},{8,7},{9,8},{10,9},{11,1... | collective-permute-start | bytes 24584 | tf_op jit(solution)/shard_map/ppermute | solution.py:28
  17.7 6.2 %collective-permute-start.3 = (s32[2,10]{1,0:T(2,128)S(1)}, s32[2,10]{1,0:T(2,128)S(1)}, u32[]{:S(2)}, u32[]{:S(2)}) collective-permute-start(s32[2,10]{1,0:T(2,128)S(1)} %get-tuple-element.2433), channel_id=1, source_target_pairs={{1,0},{2,1},{3,2},{4,3},{5,4},{6,5},{7,6},{8,7},{9,8},{10,9},{11,1... | collective-permute-start | bytes 248 | tf_op jit(solution)/shard_map/ppermute | solution.py:28
  20.8 7.0 %collective-permute-start.2 = (s32[2,10]{1,0:T(2,128)S(1)}, s32[2,10]{1,0:T(2,128)S(1)}, u32[]{:S(2)}, u32[]{:S(2)}) collective-permute-start(s32[2,10]{1,0:T(2,128)S(1)} %get-tuple-element.2432), channel_id=1, source_target_pairs={{0,1},{1,2},{2,3},{3,4},{4,5},{5,6},{6,7},{7,8},{8,9},{9,10},{10,1... | collective-permute-start | bytes 248 | tf_op jit(solution)/shard_map/ppermute | solution.py:26
  22.8 1.1 copy-start.9
  23.0 0.7 copy-start.11
  23.9 7.1 %collective-permute-start = (f32[4,512]{1,0:T(4,128)S(1)}, f32[4,512]{1,0:T(4,128)S(1)}, u32[]{:S(2)}, u32[]{:S(2)}) collective-permute-start(f32[4,512]{1,0:T(4,128)S(1)} %get-tuple-element.2424), channel_id=1, source_target_pairs={{0,1},{1,2},{2,3},{3,4},{4,5},{5,6},{6,7},{7,8},{8,9},{9,10},{10,1... | collective-permute-start | bytes 24584 | tf_op jit(solution)/shard_map/ppermute | solution.py:26
  31.3 0.6 copy-start.1
  33.1 0.7 slice-start.1
  44.8 9.5 %copy-start.6 = (f32[1,3,1024]{2,0,1:T(1,128)S(1)}, f32[1,3,1024]{2,0,1:T(1,128)}, u32[]{:S(2)}) copy-start(f32[1,3,1024]{2,0,1:T(1,128)} %param.31) | copy-start | bytes 36868
  59.5 12.3 %all-to-all-start = ((f32[32,1,5]{2,1,0:T(1,128)}), f32[32,1,5]{2,1,0:T(1,128)S(1)}, u32[]{:S(2)}, u32[]{:S(2)}) async-start(f32[32,1,5]{2,1,0:T(1,128)} %broadcast_in_dim.303), calls=%async_computation | async-start | bytes 32768 | tf_op jit(solution)/shard_map/all_to_all | solution.py:37
  77.2 14.4 %collective-permute-start.7 = (f32[4,512]{1,0:T(4,128)S(1)}, f32[4,512]{1,0:T(4,128)S(1)}, u32[]{:S(2)}, u32[]{:S(2)}) collective-permute-start(f32[4,512]{1,0:T(4,128)S(1)} %get-tuple-element.2423), channel_id=1, source_target_pairs={{1,0},{2,1},{3,2},{4,3},{5,4},{6,5},{7,6},{8,7},{9,8},{10,9},{11,1... | collective-permute-start | bytes 24584 | tf_op jit(solution)/shard_map/ppermute | solution.py:28
  79.1 12.5 %collective-permute-start.6 = (f32[4,512]{1,0:T(4,128)S(1)}, f32[4,512]{1,0:T(4,128)S(1)}, u32[]{:S(2)}, u32[]{:S(2)}) collective-permute-start(f32[4,512]{1,0:T(4,128)S(1)} %get-tuple-element.2422), channel_id=1, source_target_pairs={{0,1},{1,2},{2,3},{3,4},{4,5},{5,6},{6,7},{7,8},{8,9},{9,10},{10,1... | collective-permute-start | bytes 24584 | tf_op jit(solution)/shard_map/ppermute | solution.py:26
  81.5 32.8 %collective-permute-start.8 = (f32[1,3,1024]{2,1,0:T(4,128)S(1)}, f32[1,3,1024]{2,1,0:T(4,128)S(1)}, u32[]{:S(2)}, u32[]{:S(2)}) collective-permute-start(f32[1,3,1024]{2,1,0:T(4,128)S(1)} %multiply_add_fusion.5), channel_id=1, source_target_pairs={{32,0},{64,32},{96,64},{128,96},{160,128},{192,160},{224,192},{256... | collective-permute-start | bytes 36872 | tf_op jit(solution)/shard_map/ppermute | solution.py:28
  83.4 30.9 %collective-permute-start.9 = (f32[1,3,1024]{2,1,0:T(4,128)S(1)}, f32[1,3,1024]{2,1,0:T(4,128)S(1)}, u32[]{:S(2)}, u32[]{:S(2)}) collective-permute-start(f32[1,3,1024]{2,1,0:T(4,128)S(1)} %multiply_add_fusion.5), channel_id=1, source_target_pairs={{0,32},{32,64},{64,96},{96,128},{128,160},{160,192},{192,224},{224... | collective-permute-start | bytes 36872 | tf_op jit(solution)/shard_map/ppermute | solution.py:26
  91.8 0.7 copy-start.2
  93.0 0.7 slice-start.2
  119.5 12.9 %all-to-all-start.1 = ((f32[32,1,5]{2,1,0:T(1,128)}), f32[32,1,5]{2,1,0:T(1,128)S(1)}, u32[]{:S(2)}, u32[]{:S(2)}) async-start(f32[32,1,5]{2,1,0:T(1,128)} %broadcast_in_dim.304), calls=%async_computation.1 | async-start | bytes 32768 | tf_op jit(solution)/shard_map/all_to_all | solution.py:37
  137.8 14.6 %collective-permute-start.11 = (f32[4,512]{1,0:T(4,128)S(1)}, f32[4,512]{1,0:T(4,128)S(1)}, u32[]{:S(2)}, u32[]{:S(2)}) collective-permute-start(f32[4,512]{1,0:T(4,128)S(1)} %get-tuple-element.2421), channel_id=1, source_target_pairs={{1,0},{2,1},{3,2},{4,3},{5,4},{6,5},{7,6},{8,7},{9,8},{10,9},{11,1... | collective-permute-start | bytes 24584 | tf_op jit(solution)/shard_map/ppermute | solution.py:28
  139.7 12.7 %collective-permute-start.10 = (f32[4,512]{1,0:T(4,128)S(1)}, f32[4,512]{1,0:T(4,128)S(1)}, u32[]{:S(2)}, u32[]{:S(2)}) collective-permute-start(f32[4,512]{1,0:T(4,128)S(1)} %get-tuple-element.2420), channel_id=1, source_target_pairs={{0,1},{1,2},{2,3},{3,4},{4,5},{5,6},{6,7},{7,8},{8,9},{9,10},{10,1... | collective-permute-start | bytes 24584 | tf_op jit(solution)/shard_map/ppermute | solution.py:26
  142.1 33.5 %collective-permute-start.12 = (f32[1,3,1024]{2,1,0:T(4,128)S(1)}, f32[1,3,1024]{2,1,0:T(4,128)S(1)}, u32[]{:S(2)}, u32[]{:S(2)}) collective-permute-start(f32[1,3,1024]{2,1,0:T(4,128)S(1)} %multiply_add_fusion.4), channel_id=1, source_target_pairs={{32,0},{64,32},{96,64},{128,96},{160,128},{192,160},{224,192},{256... | collective-permute-start | bytes 36872 | tf_op jit(solution)/shard_map/ppermute | solution.py:28
  144.0 31.6 %collective-permute-start.13 = (f32[1,3,1024]{2,1,0:T(4,128)S(1)}, f32[1,3,1024]{2,1,0:T(4,128)S(1)}, u32[]{:S(2)}, u32[]{:S(2)}) collective-permute-start(f32[1,3,1024]{2,1,0:T(4,128)S(1)} %multiply_add_fusion.4), channel_id=1, source_target_pairs={{0,32},{32,64},{64,96},{96,128},{128,160},{160,192},{192,224},{224... | collective-permute-start | bytes 36872 | tf_op jit(solution)/shard_map/ppermute | solution.py:26
  152.5 0.6 copy-start.3
  154.4 0.7 slice-start.3
  180.8 12.9 %all-to-all-start.2 = ((f32[32,1,5]{2,1,0:T(1,128)}), f32[32,1,5]{2,1,0:T(1,128)S(1)}, u32[]{:S(2)}, u32[]{:S(2)}) async-start(f32[32,1,5]{2,1,0:T(1,128)} %broadcast_in_dim.305), calls=%async_computation.2 | async-start | bytes 32768 | tf_op jit(solution)/shard_map/all_to_all | solution.py:37
  199.1 14.4 %collective-permute-start.15 = (f32[4,512]{1,0:T(4,128)S(1)}, f32[4,512]{1,0:T(4,128)S(1)}, u32[]{:S(2)}, u32[]{:S(2)}) collective-permute-start(f32[4,512]{1,0:T(4,128)S(1)} %get-tuple-element.2419), channel_id=1, source_target_pairs={{1,0},{2,1},{3,2},{4,3},{5,4},{6,5},{7,6},{8,7},{9,8},{10,9},{11,1... | collective-permute-start | bytes 24584 | tf_op jit(solution)/shard_map/ppermute | solution.py:28
  201.1 12.5 %collective-permute-start.14 = (f32[4,512]{1,0:T(4,128)S(1)}, f32[4,512]{1,0:T(4,128)S(1)}, u32[]{:S(2)}, u32[]{:S(2)}) collective-permute-start(f32[4,512]{1,0:T(4,128)S(1)} %get-tuple-element.2418), channel_id=1, source_target_pairs={{0,1},{1,2},{2,3},{3,4},{4,5},{5,6},{6,7},{7,8},{8,9},{9,10},{10,1... | collective-permute-start | bytes 24584 | tf_op jit(solution)/shard_map/ppermute | solution.py:26
  203.5 33.4 %collective-permute-start.16 = (f32[1,3,1024]{2,1,0:T(4,128)S(1)}, f32[1,3,1024]{2,1,0:T(4,128)S(1)}, u32[]{:S(2)}, u32[]{:S(2)}) collective-permute-start(f32[1,3,1024]{2,1,0:T(4,128)S(1)} %multiply_add_fusion.3), channel_id=1, source_target_pairs={{32,0},{64,32},{96,64},{128,96},{160,128},{192,160},{224,192},{256... | collective-permute-start | bytes 36872 | tf_op jit(solution)/shard_map/ppermute | solution.py:28
  205.4 31.4 %collective-permute-start.17 = (f32[1,3,1024]{2,1,0:T(4,128)S(1)}, f32[1,3,1024]{2,1,0:T(4,128)S(1)}, u32[]{:S(2)}, u32[]{:S(2)}) collective-permute-start(f32[1,3,1024]{2,1,0:T(4,128)S(1)} %multiply_add_fusion.3), channel_id=1, source_target_pairs={{0,32},{32,64},{64,96},{96,128},{128,160},{160,192},{192,224},{224... | collective-permute-start | bytes 36872 | tf_op jit(solution)/shard_map/ppermute | solution.py:26
  215.6 0.7 slice-start.4
  242.0 12.9 %all-to-all-start.3 = ((f32[32,1,5]{2,1,0:T(1,128)}), f32[32,1,5]{2,1,0:T(1,128)S(1)}, u32[]{:S(2)}, u32[]{:S(2)}) async-start(f32[32,1,5]{2,1,0:T(1,128)} %broadcast_in_dim.306), calls=%async_computation.3 | async-start | bytes 32768 | tf_op jit(solution)/shard_map/all_to_all | solution.py:37
  260.3 14.4 %collective-permute-start.19 = (f32[4,512]{1,0:T(4,128)S(1)}, f32[4,512]{1,0:T(4,128)S(1)}, u32[]{:S(2)}, u32[]{:S(2)}) collective-permute-start(f32[4,512]{1,0:T(4,128)S(1)} %get-tuple-element.2417), channel_id=1, source_target_pairs={{1,0},{2,1},{3,2},{4,3},{5,4},{6,5},{7,6},{8,7},{9,8},{10,9},{11,1... | collective-permute-start | bytes 24584 | tf_op jit(solution)/shard_map/ppermute | solution.py:28
  262.2 12.5 %collective-permute-start.18 = (f32[4,512]{1,0:T(4,128)S(1)}, f32[4,512]{1,0:T(4,128)S(1)}, u32[]{:S(2)}, u32[]{:S(2)}) collective-permute-start(f32[4,512]{1,0:T(4,128)S(1)} %get-tuple-element.2416), channel_id=1, source_target_pairs={{0,1},{1,2},{2,3},{3,4},{4,5},{5,6},{6,7},{7,8},{8,9},{9,10},{10,1... | collective-permute-start | bytes 24584 | tf_op jit(solution)/shard_map/ppermute | solution.py:26
  264.7 33.4 %collective-permute-start.20 = (f32[1,3,1024]{2,1,0:T(4,128)S(1)}, f32[1,3,1024]{2,1,0:T(4,128)S(1)}, u32[]{:S(2)}, u32[]{:S(2)}) collective-permute-start(f32[1,3,1024]{2,1,0:T(4,128)S(1)} %multiply_add_fusion.2), channel_id=1, source_target_pairs={{32,0},{64,32},{96,64},{128,96},{160,128},{192,160},{224,192},{256... | collective-permute-start | bytes 36872 | tf_op jit(solution)/shard_map/ppermute | solution.py:28
  266.6 31.4 %collective-permute-start.21 = (f32[1,3,1024]{2,1,0:T(4,128)S(1)}, f32[1,3,1024]{2,1,0:T(4,128)S(1)}, u32[]{:S(2)}, u32[]{:S(2)}) collective-permute-start(f32[1,3,1024]{2,1,0:T(4,128)S(1)} %multiply_add_fusion.2), channel_id=1, source_target_pairs={{0,32},{32,64},{64,96},{96,128},{128,160},{160,192},{192,224},{224... | collective-permute-start | bytes 36872 | tf_op jit(solution)/shard_map/ppermute | solution.py:26
  276.8 0.7 slice-start.5
  303.2 12.9 %all-to-all-start.4 = ((f32[32,1,5]{2,1,0:T(1,128)}), f32[32,1,5]{2,1,0:T(1,128)S(1)}, u32[]{:S(2)}, u32[]{:S(2)}) async-start(f32[32,1,5]{2,1,0:T(1,128)} %broadcast_in_dim.307), calls=%async_computation.4 | async-start | bytes 32768 | tf_op jit(solution)/shard_map/all_to_all | solution.py:37
  321.5 14.4 %collective-permute-start.23 = (f32[4,512]{1,0:T(4,128)S(1)}, f32[4,512]{1,0:T(4,128)S(1)}, u32[]{:S(2)}, u32[]{:S(2)}) collective-permute-start(f32[4,512]{1,0:T(4,128)S(1)} %get-tuple-element.2415), channel_id=1, source_target_pairs={{1,0},{2,1},{3,2},{4,3},{5,4},{6,5},{7,6},{8,7},{9,8},{10,9},{11,1... | collective-permute-start | bytes 24584 | tf_op jit(solution)/shard_map/ppermute | solution.py:28
  323.4 12.5 %collective-permute-start.22 = (f32[4,512]{1,0:T(4,128)S(1)}, f32[4,512]{1,0:T(4,128)S(1)}, u32[]{:S(2)}, u32[]{:S(2)}) collective-permute-start(f32[4,512]{1,0:T(4,128)S(1)} %get-tuple-element.2414), channel_id=1, source_target_pairs={{0,1},{1,2},{2,3},{3,4},{4,5},{5,6},{6,7},{7,8},{8,9},{9,10},{10,1... | collective-permute-start | bytes 24584 | tf_op jit(solution)/shard_map/ppermute | solution.py:26
  325.8 32.7 %collective-permute-start.24 = (f32[1,3,1024]{2,1,0:T(4,128)S(1)}, f32[1,3,1024]{2,1,0:T(4,128)S(1)}, u32[]{:S(2)}, u32[]{:S(2)}) collective-permute-start(f32[1,3,1024]{2,1,0:T(4,128)S(1)} %multiply_add_fusion.1), channel_id=1, source_target_pairs={{32,0},{64,32},{96,64},{128,96},{160,128},{192,160},{224,192},{256... | collective-permute-start | bytes 36872 | tf_op jit(solution)/shard_map/ppermute | solution.py:28
  327.8 30.8 %collective-permute-start.25 = (f32[1,3,1024]{2,1,0:T(4,128)S(1)}, f32[1,3,1024]{2,1,0:T(4,128)S(1)}, u32[]{:S(2)}, u32[]{:S(2)}) collective-permute-start(f32[1,3,1024]{2,1,0:T(4,128)S(1)} %multiply_add_fusion.1), channel_id=1, source_target_pairs={{0,32},{32,64},{64,96},{96,128},{128,160},{160,192},{192,224},{224... | collective-permute-start | bytes 36872 | tf_op jit(solution)/shard_map/ppermute | solution.py:26
  336.1 0.7 copy-start
  337.4 0.7 slice-start
  363.8 12.9 %all-to-all-start.5 = ((f32[32,1,5]{2,1,0:T(1,128)}), f32[32,1,5]{2,1,0:T(1,128)S(1)}, u32[]{:S(2)}, u32[]{:S(2)}) async-start(f32[32,1,5]{2,1,0:T(1,128)} %broadcast_in_dim.308), calls=%async_computation.5 | async-start | bytes 32768 | tf_op jit(solution)/shard_map/all_to_all | solution.py:37
  (2 other events, 1.2 us)
where the time goes:
time: 386 us; the launch traced here: 384 us
  starting transfers between devices  121 us (31%)
  local copies, waits for them, and re-layouts  89.8 us (23%)
  other arithmetic  80.1 us (21%)
  waiting for transfers between devices  54.7 us (14%)
  between operations  31.5 us (8%)
  loops' own time  6.62 us (2%)
    ppermute x13, starting transfers between devices, extended_2(): lax.ppermute(tail, axis, [(i, (i + 1) % count) for i in range(ends)])  64.1 us
    all_to_all x6, waiting for transfers between devices, from_everyone(): lax.all_to_all(jnp.broadcast_to(shard[None], (length, *shard.shape)), axi...  49.8 us
    ppermute x13, starting transfers between devices, extended_2(): lax.ppermute(head, axis, [((i + 1) % count, i) for i in range(ends)])  31.1 us
    all_to_all x6, starting transfers between devices, from_everyone(): lax.all_to_all(jnp.broadcast_to(shard[None], (length, *shard.shape)), axi...  26.2 us
    reduce_sum x48, other arithmetic, force_cells(): jnp.sum((weight * coefficient)[:, None] * separation, axis=-1)  23.9 us
    concatenate x6, local copies, waits for them, and re-layouts, in_one(): so_far = of_everyone(jnp.concatenate([a.ravel() for a in arrays]), axis)  19.3 us
    reduce_sum x72, other arithmetic, density_cells(): density = density + jnp.sum(weight * remain ** 4, axis=-1)  19.2 us
    slice x60, local copies, waits for them, and re-layouts, tile_weight(): self_tile[:, partner, None, None] & diagonal[None]  15.2 us
  transfers between devices with their start and end apart: 32, of which 8 were waited for; matrix products, arithmetic and copies ran while one was open for 33% of the time, Pallas kernels for 0%

commit v1 on v0

v1 whole, which is shorter than its diff:
```python
import functools

import jax
import jax.numpy as jnp
from jax import lax
from jax.experimental import pallas as pl
from jax.experimental.pallas import tpu as pltpu
from jax.sharding import PartitionSpec as P


SLOTS = 128
ITERATIONS = 6
CELLS = 8
HALO = 4
WIDE = CELLS + 2 * HALO
OFFSETS = (-2, -1, 0, 1, 2)
DENSE = range(2, WIDE - 2)

cutoff_sq = 9.0
pair_strength = 0.4
step_size = 0.02
epsilon = 1e-06
penalty = 10000.0

f32 = jnp.float32
bf16 = jnp.bfloat16


def vmem(n):
    return [pl.BlockSpec(memory_space=pltpu.VMEM) for _ in range(n)]


def smem():
    return pl.BlockSpec(memory_space=pltpu.SMEM)


def shape(*dims):
    return jax.ShapeDtypeStruct(dims, f32)


def rows_iota():
    return lax.broadcasted_iota(jnp.int32, (8, SLOTS), 0)


def lanes_iota(rows=8):
    return lax.broadcasted_iota(jnp.int32, (rows, SLOTS), 1)


def centred_sites():
    row, lane = rows_iota(), lanes_iota()
    x = (lane // 64).astype(f32) - 0.5
    y = (lane // 8 % 8).astype(f32) - 3.5
    z = (lane % 8).astype(f32) - 3.5
    return jnp.where(row == 0, x, jnp.where(row == 1, y, jnp.where(row == 2, z, 0.0)))


def three_parts(v):
    high = v.astype(bf16).astype(f32)
    rest = v - high
    mid = rest.astype(bf16).astype(f32)
    low = (rest - mid).astype(bf16).astype(f32)
    return high, mid, low


def space_even():
    return 1 - (lax.axis_index("space") & 1)


def pack_kernel(disp, live, cells, used, own, image_out, near_out, far_out):
    even = space_even()
    row = rows_iota()
    lane = lanes_iota()
    cell_id = lax.broadcasted_iota(jnp.int32, cells.shape, 0)
    weight = jnp.zeros((CELLS, SLOTS), f32)
    for n, _ in enumerate(OFFSETS):
        hit = jnp.where(cells[...] == cell_id + n, used[...].astype(f32), 0.0)
        weight = jnp.where(lane == n, jnp.sum(hit, axis=1, keepdims=True), weight)
    for c in range(CELLS):
        part = slice(c * SLOTS, (c + 1) * SLOTS)
        state = jnp.where(row == 3, live[:, part].astype(f32), 0.0)
        state = jnp.where(row == 4, weight[c : c + 1], state)
        for a in range(3):
            state = jnp.where(row == a, disp[a, 0:1, part], state)
        own[c] = state
        image_out[c] = state[0:4]
    near_out[...] = own[pl.ds(even * HALO, HALO)]
    far_out[...] = own[pl.ds((1 - even) * HALO, HALO)]


def join_kernel(own, near, far, wide):
    even = space_even()
    wide[pl.ds(HALO, CELLS)] = own[...]
    wide[pl.ds(even * (HALO + CELLS), HALO)] = near[...]
    wide[pl.ds((1 - even) * (HALO + CELLS), HALO)] = far[...]


def force_kernel(first, *refs):
    if first:
        wide, force, left, right, sums, slope_sums, powers, density = refs
    else:
        base, own, near, far, force = refs[:5]
        left, right, sums, slope_sums, powers, density, wide = refs[5:]
        even = space_even()
        wide[pl.ds(HALO, CELLS)] = own[...]
        wide[pl.ds((1 - even) * (HALO + CELLS), HALO)] = far[...]
        for c in range(HALO):
            at = even * (HALO + CELLS) + c
            wide[at] = jnp.concatenate([near[c], base[at, 4:8]], axis=0)
    row = rows_iota()
    site = centred_sites()

    def placed(c):
        return jnp.where(row < 3, wide[c] + site, 0.0)

    def tall(blocks):
        return jnp.concatenate(blocks, axis=0)

    def squares(p):
        return jnp.sum(p * p, axis=0, keepdims=True) * (1.0 / cutoff_sq)

    def weight_of(c, n):
        return jnp.broadcast_to(wide[c, 4:5, n : n + 1], (1, SLOTS))

    def partner_rows(c):
        p = placed(c)
        alive = wide[c, 3:4, :]
        norm = -squares(p) - penalty * (1.0 - alive)
        rows = p * (2.0 / cutoff_sq)
        rows = jnp.where(row == 3, norm, rows)
        return jnp.where((row == 4) | (row == 6), 1.0, rows)

    def prepare_left(c, _):
        h, m, l = three_parts(partner_rows(c))
        left[c] = tall([h, h, m, m, h, l]).T.astype(bf16)
        sums[c] = tall([h, m, l, jnp.zeros_like(h)]).astype(bf16)
        return 0

    lax.fori_loop(0, WIDE, prepare_left, 0, unroll=8)

    def prepare_right(c, _):
        p = placed(c)
        for n, o in enumerate(OFFSETS):
            q = jnp.where(row == 0, p - 2.0 * o, p)
            rows = jnp.where(row == 3, 1.0, q)
            rows = jnp.where(row == 4, 1.0 - squares(q), rows)
            rows = jnp.where(row == 6, 0.0, rows)
            h, m, l = three_parts(rows)
            right[c, n] = tall([h, m, h, m, l, h]).astype(bf16)
        return 0

    lax.fori_loop(DENSE.start, DENSE.stop, prepare_right, 0, unroll=4)

    def folded(t):
        return jnp.sum(t.reshape(SLOTS // 8, 8, SLOTS), axis=0)

    def two_parts(v):
        high = v.astype(bf16)
        return high, (v - high.astype(f32)).astype(bf16)

    def cell_pair(c, owned):
        total = [jnp.zeros((8, SLOTS), f32), jnp.zeros((8, SLOTS), f32)]
        for dh in range(-2, 4):
            sides = [(i, dh - i + 2) for i in (0, 1) if 0 <= dh - i + 2 < 5]
            blocks = [right[c + i, n] for i, n in sides]
            rhs = blocks[0] if len(blocks) == 1 else jnp.concatenate(blocks, axis=1)
            near = jnp.dot(left[c + dh], rhs, preferred_element_type=f32)
            for b, (i, n) in enumerate(sides):
                t = jnp.maximum(near[:, b * SLOTS : (b + 1) * SLOTS], 0.0)
                square = t * t
                if owned:
                    for k, v in enumerate((square * t, square)):
                        columns = slice(k * SLOTS, (k + 1) * SLOTS)
                        high, low = two_parts(v)
                        at = 2 * n * SLOTS
                        powers[c - HALO + i, at : at + SLOTS, columns] = high
                        powers[c - HALO + i, at + SLOTS : at + 2 * SLOTS, columns] = low
                total[i] = total[i] + weight_of(c + i, n) * folded(square * square)
        for i in (0, 1):
            value = jnp.sum(total[i], axis=0, keepdims=True) - weight_of(c + i, 2)
            alive = wide[c + i, 3:4, :]
            density[c + i] = -0.5 * alive * lax.rsqrt(1.0 + value * alive)

    def rim_pair(k, _):
        cell_pair(2 + 10 * k, False)
        return 0

    def own_pair(k, _):
        cell_pair(HALO + 2 * k, True)
        return 0

    lax.fori_loop(0, 2, rim_pair, 0, unroll=2)
    lax.fori_loop(0, CELLS // 2, own_pair, 0)

    def prepare_slopes(c, _):
        h, m, l = three_parts(partner_rows(c) * density[c])
        slope_sums[c] = tall([h, m, l, jnp.zeros_like(h)]).astype(bf16)
        return 0

    lax.fori_loop(DENSE.start, DENSE.stop, prepare_slopes, 0, unroll=6)

    tilt_row = lax.broadcasted_iota(jnp.int32, (64, SLOTS), 0) % 8 == 6

    def force_cell(k, _):
        c = HALO + k
        parts = []
        for n, o in enumerate(OFFSETS):
            weight = weight_of(c, n)
            factor = jnp.where(tilt_row, o * weight, weight).astype(bf16)
            rows = tall([sums[c + o], slope_sums[c + o]]) * factor
            parts += [rows, rows]
        got = jnp.dot(
            jnp.concatenate(parts, axis=1), powers[k], preferred_element_type=f32
        )

        def joined(at, columns):
            x = got[at : at + 24, columns]
            return x[0:8] + x[8:16] + x[16:24]

        cubes, squared = slice(0, SLOTS), slice(SLOTS, 2 * SLOTS)
        total = (
            -4.0 * (density[c] * joined(0, cubes) + joined(32, cubes))
            - 3.0 * pair_strength * joined(0, squared)
        )
        value = total - (2.0 / cutoff_sq) * placed(c) * total[4:5]
        value = jnp.where(row == 0, value + (4.0 / cutoff_sq) * total[6:7], value)
        force[k] = jnp.where(row < 3, value * wide[c, 3:4, :], 0.0)
        return 0

    lax.fori_loop(0, CELLS, force_cell, 0, unroll=4)


def gaps_kernel(own, force, from_a, from_b, ends, packed, far_out, sums):
    even = space_even()
    image = lax.axis_index("image")
    image_even = 1 - (image & 1)
    edge = (image == 0) | (image == lax.axis_size("image") - 1)
    row = rows_iota()
    kept = row < 3
    blank = jnp.zeros((4, SLOTS), f32)
    totals = [jnp.zeros((8, SLOTS), f32) for _ in range(5)]
    for c in range(CELLS):
        state = own[c]
        alive = state[3:4]
        part = slice(c * SLOTS, (c + 1) * SLOTS)
        both = [jnp.concatenate([ends[a, n : n + 1, part] for a in range(3)], axis=0) for n in (0, 1)]
        fixed = jnp.where(image > 0, both[1], both[0])
        fixed = jnp.concatenate([fixed, blank, blank[0:1]], axis=0)
        one = jnp.concatenate([from_a[c], blank], axis=0)
        other = jnp.concatenate([from_b[c], blank], axis=0)
        other = jnp.where(edge, fixed, other)
        following = jnp.where(image_even == 1, one, other)
        previous = jnp.where(image_even == 1, other, one)
        forward = jnp.where(kept, (following - state) * alive, 0.0)
        backward = jnp.where(kept, (state - previous) * alive, 0.0)
        f = force[c]
        packed[c, 0:8] = f
        packed[c, 8:16] = forward
        packed[c, 16:24] = backward
        pairs = ((forward, forward), (backward, backward), (forward, backward), (f, forward), (f, backward))
        totals = [t + a * b for t, (a, b) in zip(totals, pairs)]
    lane = lanes_iota(1)
    line = jnp.zeros((1, SLOTS), f32)
    for n, t in enumerate(totals):
        value = jnp.sum(jnp.sum(t, axis=0, keepdims=True), axis=1, keepdims=True)
        line = jnp.where(lane == n, value, line)
    sums[...] = jnp.broadcast_to(line[None], sums.shape)
    far_out[...] = packed[pl.ds((1 - even) * HALO, HALO)]


def band_terms(sums, spring):
    total = sums[0]
    for d in range(1, sums.shape[0]):
        total = total + sums[d]

    def value(n):
        return jnp.broadcast_to(total[:, n : n + 1], (1, SLOTS))

    forward_sq, backward_sq, cross, ahead, behind = [value(n) for n in range(5)]
    length_ahead = jnp.sqrt(forward_sq + epsilon)
    length_behind = jnp.sqrt(backward_sq + epsilon)
    both = length_ahead * length_behind
    cosine = cross / both
    tangent_sq = (
        forward_sq / (length_ahead * length_ahead)
        + backward_sq / (length_behind * length_behind)
        + 2.0 * cosine
    )
    tangent_len = jnp.sqrt(jnp.maximum(tangent_sq, 1.0))
    parallel = (ahead / length_ahead + behind / length_behind) / tangent_len
    spring_term = spring * (length_ahead - length_behind)
    pull = (spring_term - parallel) / tangent_len
    return parallel, spring_term, cosine, pull / length_ahead, pull / length_behind


def moved_kernel(spring, sums, old, old_far, packed, far_packed, own, far, image_out, near_out):
    even = space_even()
    _, _, _, ahead, behind = band_terms(sums, spring[0])

    def shifted(state, g):
        return state + step_size * (g[0:8] + ahead * g[8:16] + behind * g[16:24])

    for c in range(CELLS):
        state = shifted(old[c], packed[c])
        own[c] = state
        image_out[c] = state[0:4]
    near_out[...] = image_out[pl.ds(even * HALO, HALO)]
    for c in range(HALO):
        far[c] = shifted(old_far[c], far_packed[c])


def final_kernel(spring, sums, packed, band, stats):
    parallel, spring_term, cosine, ahead, behind = band_terms(sums, spring[0])
    for c in range(CELLS):
        value = packed[c, 0:8] + ahead * packed[c, 8:16] + behind * packed[c, 16:24]
        for a in range(3):
            band[a, 0:1, c * SLOTS : (c + 1) * SLOTS] = value[a : a + 1]
    lane = lanes_iota(1)
    line = jnp.where(lane == 0, parallel, jnp.where(lane == 1, spring_term, cosine))
    stats[...] = line[:, 0:3]


def call(kernel, outs, scalars, arrays, room=2, **more):
    ins = [smem()] * scalars + vmem(arrays)
    return pl.pallas_call(
        kernel,
        out_shape=outs,
        in_specs=ins,
        out_specs=jax.tree.map(lambda _: pl.BlockSpec(memory_space=pltpu.VMEM), outs),
        compiler_params=pltpu.CompilerParams(vmem_limit_bytes=room << 20),
        **more,
    )


def swap_pairs(axis, closed):
    count = lax.axis_size(axis)
    first = [(i, i ^ 1) for i in range(count)]
    second = []
    for i in range(count):
        j = i + 1 if i % 2 else i - 1
        if closed or 0 <= j < count:
            second.append((i, j % count))
    return first, second


def body(displacement, end_states, atom_live, partner_cells, partner_live, spring_const):
    parts = lax.axis_size("space")
    end_states = end_states.transpose(1, 0, 2)
    image_a, image_b = swap_pairs("image", False)
    space_a, space_b = swap_pairs("space", True)

    own, image_out, near, far = call(
        pack_kernel,
        (shape(CELLS, 8, SLOTS), shape(CELLS, 4, SLOTS), shape(HALO, 8, SLOTS), shape(HALO, 8, SLOTS)),
        0,
        4,
    )(displacement.transpose(1, 0, 2), atom_live[None], partner_cells, partner_live)
    near = lax.ppermute(near, "space", space_a)
    far = lax.ppermute(far, "space", space_b)
    base = call(join_kernel, shape(WIDE, 8, SLOTS), 0, 3)(own, near, far)

    def forces(*operands):
        first = len(operands) == 1
        scratch = [
            pltpu.VMEM((WIDE, SLOTS, 48), bf16),
            pltpu.VMEM((WIDE, 5, 48, SLOTS), bf16),
            pltpu.VMEM((WIDE, 32, SLOTS), bf16),
            pltpu.VMEM((WIDE, 32, SLOTS), bf16),
            pltpu.VMEM((CELLS, 10 * SLOTS, 2 * SLOTS), bf16),
            pltpu.VMEM((WIDE, 1, SLOTS), f32),
        ]
        if not first:
            scratch.append(pltpu.VMEM((WIDE, 8, SLOTS), f32))
        return call(
            functools.partial(force_kernel, first),
            shape(CELLS, 8, SLOTS),
            0,
            1 if first else 4,
            room=12,
            scratch_shapes=scratch,
            cost_estimate=pl.CostEstimate(
                flops=20000000, bytes_accessed=200000, transcendentals=2000
            ),
        )(*operands)

    operands = (base,)
    for iteration in range(ITERATIONS):
        from_a = lax.ppermute(image_out, "image", image_a)
        from_b = lax.ppermute(image_out, "image", image_b)
        force = forces(*operands)
        packed, far_packed, sums = call(
            gaps_kernel,
            (shape(CELLS, 24, SLOTS), shape(HALO, 24, SLOTS), shape(parts, 1, SLOTS)),
            0,
            5,
        )(own, force, from_a, from_b, end_states)
        sums = lax.all_to_all(sums, "space", 0, 0, tiled=True)
        if iteration < ITERATIONS - 1:
            far_packed = lax.ppermute(far_packed, "space", space_b)
        if iteration < ITERATIONS - 1:
            own, far, image_out, near = call(
                moved_kernel,
                (
                    shape(CELLS, 8, SLOTS),
                    shape(HALO, 8, SLOTS),
                    shape(CELLS, 4, SLOTS),
                    shape(HALO, 4, SLOTS),
                ),
                1,
                5,
            )(spring_const, sums, own, far, packed, far_packed)
            near = lax.ppermute(near, "space", space_a)
            operands = (base, own, near, far)
    band, stats = call(final_kernel, (shape(3, 1, CELLS * SLOTS), shape(1, 3)), 1, 2)(
        spring_const, sums, packed
    )
    return band.transpose(1, 0, 2), stats


def solution(mesh):
    return jax.shard_map(
        body,
        mesh=mesh,
        in_specs=(
            P("image", None, "space"),
            P(None, None, "space"),
            P("space"),
            P("space", None),
            P("space", None),
            P("image"),
        ),
        out_specs=(P("image", None, "space"), P("image", None)),
        check_vma=False,
    )
```

time: 386 us -> 196 us (0.51)
  the two profiles are of different devices: /device:TPU:134 before, /device:TPU:1 now
where the time goes in v1:
time: 196 us; the launch traced here: 194 us
  starting transfers between devices  87.8 us (45%)
  blocking collectives  61.9 us (32%)
  Pallas kernels  28.4 us (14%)
  waiting for transfers between devices  11.8 us (6%)
  local copies, waits for them, and re-layouts  2.76 us (1%)
    all_to_all x5, blocking collectives, body(): sums = lax.all_to_all(sums, 'space', 0, 0, tiled=True)  61.9 us
    ppermute x6, starting transfers between devices, body(): from_a = lax.ppermute(image_out, 'image', image_a)  35.3 us
    ppermute x6, starting transfers between devices, body(): near = lax.ppermute(near, 'space', space_a)  25.1 us
    pallas_call x6, Pallas kernels, forces(): call(functools.partial(force_kernel, first), shape(CELLS, 8, SLOTS), 0, 1...  24.8 us
    ppermute x5, starting transfers between devices, body(): far_packed = lax.ppermute(far_packed, 'space', space_b)  12.9 us
    all_to_all x1, starting transfers between devices, body(): sums = lax.all_to_all(sums, 'space', 0, 0, tiled=True)  8.6 us
    all_to_all x1, waiting for transfers between devices, body(): sums = lax.all_to_all(sums, 'space', 0, 0, tiled=True)  7.24 us
    ppermute x6, waiting for transfers between devices, body(): near = lax.ppermute(near, 'space', space_a)  4.03 us
  transfers between devices with their start and end apart: 25, of which 7 were waited for; matrix products, arithmetic and copies ran while one was open for 0% of the time, Pallas kernels for 13%

profile of v1, /device:TPU:1, one launch (start us, length us, event | category | flops | bytes accessed | tf_op | source)
XLA Modules:
  0.0 194.5 jit_solution(7282769392815941862)
XLA Ops:
  0.6 0.7 copy-done.1
  1.3 0.7 copy-done.2
  2.0 0.7 copy-done.3
  2.7 0.7 copy-done.4
  3.5 8.7 %collective-permute-start = (f32[4,8,128]{2,1,0:T(8,128)S(1)}, f32[4,8,128]{2,1,0:T(8,128)S(1)}, u32[]{:S(2)}, u32[]{:S(2)}) collective-permute-start(f32[4,8,128]{2,1,0:T(8,128)S(1)} %get-tuple-element.46), channel_id=1, source_target_pairs={{0,1},{1,0},{2,3},{3,2},{4,5},{5,4},{6,7},{7,6},{8,9},{9,8},{10,11... | collective-permute-start | bytes 49160 | tf_op jit(solution)/shard_map/ppermute | solution.py:357
  12.3 1.9 collective-permute-start.1
  14.2 0.7 collective-permute-start.3
  14.9 1.9 collective-permute-start.2
  17.3 4.1 %shard_map.79.force = f32[8,8,128]{2,1,0:T(8,128)S(1)} custom-call(f32[16,8,128]{2,1,0:T(8,128)S(1)} %shard_map.78.refs_0_), custom_call_target="tpu_custom_call" | custom-call | flops 20000000 | bytes 200000 | tf_op jit(solution)/shard_map/pallas_call | solution.py:373
  21.5 0.7 shard_map.80
  22.2 3.1 %collective-permute-start.4 = (f32[4,24,128]{2,1,0:T(8,128)S(1)}, f32[4,24,128]{2,1,0:T(8,128)S(1)}, u32[]{:S(2)}, u32[]{:S(2)}) collective-permute-start(f32[4,24,128]{2,1,0:T(8,128)S(1)} %get-tuple-element.51), channel_id=1, source_target_pairs={{0,31},{1,2},{2,1},{3,4},{4,3},{5,6},{6,5},{7,8},{8,7},{9,10},{10,... | collective-permute-start | bytes 147464 | tf_op jit(solution)/shard_map/ppermute | solution.py:398
  25.4 8.6 %all-to-all-start = ((f32[32,1,128]{2,1,0:T(1,128)}), f32[32,1,128]{2,1,0:T(1,128)S(1)}, u32[]{:S(2)}, u32[]{:S(2)}) async-start(f32[32,1,128]{2,1,0:T(1,128)} %get-tuple-element.49), calls=%async_computation | async-start | bytes 32768 | tf_op jit(solution)/shard_map/all_to_all | solution.py:396
  34.6 7.2 %all-to-all-done.sums = f32[32,1,128]{2,1,0:T(1,128)S(1)} async-done(((f32[32,1,128]{2,1,0:T(1,128)}), f32[32,1,128]{2,1,0:T(1,128)S(1)}, u32[]{:S(2)}, u32[]{:S(2)}) %all-to-all-start) | async-done | bytes 16416 | tf_op jit(solution)/shard_map/all_to_all | solution.py:396
  42.0 0.7 collective-permute-start.7
  42.7 7.9 %collective-permute-start.6 = (f32[8,4,128]{2,1,0:T(4,128)S(1)}, f32[8,4,128]{2,1,0:T(4,128)S(1)}, u32[]{:S(2)}, u32[]{:S(2)}) collective-permute-start(f32[8,4,128]{2,1,0:T(4,128)S(1)} %get-tuple-element.55), channel_id=1, source_target_pairs={{0,32},{32,0},{64,96},{96,64},{128,160},{160,128},{192,224},{224,1... | collective-permute-start | bytes 49160 | tf_op jit(solution)/shard_map/ppermute | solution.py:387
  50.6 3.3 %collective-permute-start.5 = (f32[4,4,128]{2,1,0:T(4,128)S(1)}, f32[4,4,128]{2,1,0:T(4,128)S(1)}, u32[]{:S(2)}, u32[]{:S(2)}) collective-permute-start(f32[4,4,128]{2,1,0:T(4,128)S(1)} %get-tuple-element.53), channel_id=1, source_target_pairs={{0,1},{1,0},{2,3},{3,2},{4,5},{5,4},{6,7},{7,6},{8,9},{9,8},{10,11... | collective-permute-start | bytes 24584 | tf_op jit(solution)/shard_map/ppermute | solution.py:411
  53.9 0.8 collective-permute-done.5.refs_2_
  54.7 4.1 %shard_map.82.force = f32[8,8,128]{2,1,0:T(8,128)S(1)} custom-call(f32[16,8,128]{2,1,0:T(8,128)S(1)} %shard_map.78.refs_0_, f32[8,8,128]{2,1,0:T(8,128)S(1)} %get-tuple-element.52.refs_1_.own.old, f32[4,4,128]{2,1,0:T(4,128)S(1)} %collective-permute-done.5.refs_2_, f32[4,8,128]{2,1,0:T(8,128)S(1)} %get-tuple-element.54.refs_3_.old_far), custom_call_target="tpu_custom_call" | custom-call | flops 20000000 | bytes 200000 | tf_op jit(solution)/shard_map/pallas_call | solution.py:373
  59.0 2.4 %collective-permute-start.8 = (f32[4,24,128]{2,1,0:T(8,128)S(1)}, f32[4,24,128]{2,1,0:T(8,128)S(1)}, u32[]{:S(2)}, u32[]{:S(2)}) collective-permute-start(f32[4,24,128]{2,1,0:T(8,128)S(1)} %get-tuple-element.58), channel_id=1, source_target_pairs={{0,31},{1,2},{2,1},{3,4},{4,3},{5,6},{6,5},{7,8},{8,7},{9,10},{10,... | collective-permute-start | bytes 147464 | tf_op jit(solution)/shard_map/ppermute | solution.py:398
  61.4 12.8 %all_to_all.30.sums = f32[32,1,128]{2,1,0:T(1,128)S(1)} all-to-all(f32[32,1,128]{2,1,0:T(1,128)S(1)} %get-tuple-element.56), channel_id=1, replica_groups=mesh['image'=16,'space'=32] {'space'}, dimensions={0} | all-to-all | bytes 32768 | tf_op jit(solution)/shard_map/all_to_all | solution.py:396
  74.4 0.7 collective-permute-start.11
  75.0 5.6 %collective-permute-start.10 = (f32[8,4,128]{2,1,0:T(4,128)S(1)}, f32[8,4,128]{2,1,0:T(4,128)S(1)}, u32[]{:S(2)}, u32[]{:S(2)}) collective-permute-start(f32[8,4,128]{2,1,0:T(4,128)S(1)} %get-tuple-element.62), channel_id=1, source_target_pairs={{0,32},{32,0},{64,96},{96,64},{128,160},{160,128},{192,224},{224,1... | collective-permute-start | bytes 49160 | tf_op jit(solution)/shard_map/ppermute | solution.py:387
  80.6 3.3 %collective-permute-start.9 = (f32[4,4,128]{2,1,0:T(4,128)S(1)}, f32[4,4,128]{2,1,0:T(4,128)S(1)}, u32[]{:S(2)}, u32[]{:S(2)}) collective-permute-start(f32[4,4,128]{2,1,0:T(4,128)S(1)} %get-tuple-element.60), channel_id=1, source_target_pairs={{0,1},{1,0},{2,3},{3,2},{4,5},{5,4},{6,7},{7,6},{8,9},{9,8},{10,11... | collective-permute-start | bytes 24584 | tf_op jit(solution)/shard_map/ppermute | solution.py:411
  83.9 0.8 collective-permute-done.9.refs_2_
  84.7 4.1 %shard_map.85.force = f32[8,8,128]{2,1,0:T(8,128)S(1)} custom-call(f32[16,8,128]{2,1,0:T(8,128)S(1)} %shard_map.78.refs_0_, f32[8,8,128]{2,1,0:T(8,128)S(1)} %get-tuple-element.59.refs_1_.own.old, f32[4,4,128]{2,1,0:T(4,128)S(1)} %collective-permute-done.9.refs_2_, f32[4,8,128]{2,1,0:T(8,128)S(1)} %get-tuple-element.61.refs_3_.old_far), custom_call_target="tpu_custom_call" | custom-call | flops 20000000 | bytes 200000 | tf_op jit(solution)/shard_map/pallas_call | solution.py:373
  89.0 2.4 %collective-permute-start.12 = (f32[4,24,128]{2,1,0:T(8,128)S(1)}, f32[4,24,128]{2,1,0:T(8,128)S(1)}, u32[]{:S(2)}, u32[]{:S(2)}) collective-permute-start(f32[4,24,128]{2,1,0:T(8,128)S(1)} %get-tuple-element.65), channel_id=1, source_target_pairs={{0,31},{1,2},{2,1},{3,4},{4,3},{5,6},{6,5},{7,8},{8,7},{9,10},{10,... | collective-permute-start | bytes 147464 | tf_op jit(solution)/shard_map/ppermute | solution.py:398
  91.4 12.7 %all_to_all.31.sums = f32[32,1,128]{2,1,0:T(1,128)S(1)} all-to-all(f32[32,1,128]{2,1,0:T(1,128)S(1)} %get-tuple-element.63), channel_id=1, replica_groups=mesh['image'=16,'space'=32] {'space'}, dimensions={0} | all-to-all | bytes 32768 | tf_op jit(solution)/shard_map/all_to_all | solution.py:396
  104.3 0.7 collective-permute-start.15
  105.0 8.2 %collective-permute-start.14 = (f32[8,4,128]{2,1,0:T(4,128)S(1)}, f32[8,4,128]{2,1,0:T(4,128)S(1)}, u32[]{:S(2)}, u32[]{:S(2)}) collective-permute-start(f32[8,4,128]{2,1,0:T(4,128)S(1)} %get-tuple-element.69), channel_id=1, source_target_pairs={{0,32},{32,0},{64,96},{96,64},{128,160},{160,128},{192,224},{224,1... | collective-permute-start | bytes 49160 | tf_op jit(solution)/shard_map/ppermute | solution.py:387
  113.2 3.3 %collective-permute-start.13 = (f32[4,4,128]{2,1,0:T(4,128)S(1)}, f32[4,4,128]{2,1,0:T(4,128)S(1)}, u32[]{:S(2)}, u32[]{:S(2)}) collective-permute-start(f32[4,4,128]{2,1,0:T(4,128)S(1)} %get-tuple-element.67), channel_id=1, source_target_pairs={{0,1},{1,0},{2,3},{3,2},{4,5},{5,4},{6,7},{7,6},{8,9},{9,8},{10,11... | collective-permute-start | bytes 24584 | tf_op jit(solution)/shard_map/ppermute | solution.py:411
  116.5 0.8 collective-permute-done.13.refs_2_
  117.3 4.1 %shard_map.88.force = f32[8,8,128]{2,1,0:T(8,128)S(1)} custom-call(f32[16,8,128]{2,1,0:T(8,128)S(1)} %shard_map.78.refs_0_, f32[8,8,128]{2,1,0:T(8,128)S(1)} %get-tuple-element.66.refs_1_.own.old, f32[4,4,128]{2,1,0:T(4,128)S(1)} %collective-permute-done.13.refs_2_, f32[4,8,128]{2,1,0:T(8,128)S(1)} %get-tuple-element.68.refs_3_.old_far), custom_call_target="tpu_custom_call" | custom-call | flops 20000000 | bytes 200000 | tf_op jit(solution)/shard_map/pallas_call | solution.py:373
  121.6 2.4 %collective-permute-start.16 = (f32[4,24,128]{2,1,0:T(8,128)S(1)}, f32[4,24,128]{2,1,0:T(8,128)S(1)}, u32[]{:S(2)}, u32[]{:S(2)}) collective-permute-start(f32[4,24,128]{2,1,0:T(8,128)S(1)} %get-tuple-element.72), channel_id=1, source_target_pairs={{0,31},{1,2},{2,1},{3,4},{4,3},{5,6},{6,5},{7,8},{8,7},{9,10},{10,... | collective-permute-start | bytes 147464 | tf_op jit(solution)/shard_map/ppermute | solution.py:398
  124.1 12.7 %all_to_all.32.sums = f32[32,1,128]{2,1,0:T(1,128)S(1)} all-to-all(f32[32,1,128]{2,1,0:T(1,128)S(1)} %get-tuple-element.70), channel_id=1, replica_groups=mesh['image'=16,'space'=32] {'space'}, dimensions={0} | all-to-all | bytes 32768 | tf_op jit(solution)/shard_map/all_to_all | solution.py:396
  137.0 0.7 collective-permute-start.19
  137.7 5.6 %collective-permute-start.18 = (f32[8,4,128]{2,1,0:T(4,128)S(1)}, f32[8,4,128]{2,1,0:T(4,128)S(1)}, u32[]{:S(2)}, u32[]{:S(2)}) collective-permute-start(f32[8,4,128]{2,1,0:T(4,128)S(1)} %get-tuple-element.76), channel_id=1, source_target_pairs={{0,32},{32,0},{64,96},{96,64},{128,160},{160,128},{192,224},{224,1... | collective-permute-start | bytes 49160 | tf_op jit(solution)/shard_map/ppermute | solution.py:387
  143.2 3.3 %collective-permute-start.17 = (f32[4,4,128]{2,1,0:T(4,128)S(1)}, f32[4,4,128]{2,1,0:T(4,128)S(1)}, u32[]{:S(2)}, u32[]{:S(2)}) collective-permute-start(f32[4,4,128]{2,1,0:T(4,128)S(1)} %get-tuple-element.74), channel_id=1, source_target_pairs={{0,1},{1,0},{2,3},{3,2},{4,5},{5,4},{6,7},{7,6},{8,9},{9,8},{10,11... | collective-permute-start | bytes 24584 | tf_op jit(solution)/shard_map/ppermute | solution.py:411
  146.5 0.8 collective-permute-done.17.refs_2_
  147.3 4.1 %shard_map.91.force = f32[8,8,128]{2,1,0:T(8,128)S(1)} custom-call(f32[16,8,128]{2,1,0:T(8,128)S(1)} %shard_map.78.refs_0_, f32[8,8,128]{2,1,0:T(8,128)S(1)} %get-tuple-element.73.refs_1_.own.old, f32[4,4,128]{2,1,0:T(4,128)S(1)} %collective-permute-done.17.refs_2_, f32[4,8,128]{2,1,0:T(8,128)S(1)} %get-tuple-element.75.refs_3_.old_far), custom_call_target="tpu_custom_call" | custom-call | flops 20000000 | bytes 200000 | tf_op jit(solution)/shard_map/pallas_call | solution.py:373
  151.6 2.4 %collective-permute-start.20 = (f32[4,24,128]{2,1,0:T(8,128)S(1)}, f32[4,24,128]{2,1,0:T(8,128)S(1)}, u32[]{:S(2)}, u32[]{:S(2)}) collective-permute-start(f32[4,24,128]{2,1,0:T(8,128)S(1)} %get-tuple-element.79), channel_id=1, source_target_pairs={{0,31},{1,2},{2,1},{3,4},{4,3},{5,6},{6,5},{7,8},{8,7},{9,10},{10,... | collective-permute-start | bytes 147464 | tf_op jit(solution)/shard_map/ppermute | solution.py:398
  154.1 12.7 %all_to_all.33.sums = f32[32,1,128]{2,1,0:T(1,128)S(1)} all-to-all(f32[32,1,128]{2,1,0:T(1,128)S(1)} %get-tuple-element.77), channel_id=1, replica_groups=mesh['image'=16,'space'=32] {'space'}, dimensions={0} | all-to-all | bytes 32768 | tf_op jit(solution)/shard_map/all_to_all | solution.py:396
  167.7 6.2 %collective-permute-start.22 = (f32[8,4,128]{2,1,0:T(4,128)S(1)}, f32[8,4,128]{2,1,0:T(4,128)S(1)}, u32[]{:S(2)}, u32[]{:S(2)}) collective-permute-start(f32[8,4,128]{2,1,0:T(4,128)S(1)} %get-tuple-element.83), channel_id=1, source_target_pairs={{0,32},{32,0},{64,96},{96,64},{128,160},{160,128},{192,224},{224,1... | collective-permute-start | bytes 49160 | tf_op jit(solution)/shard_map/ppermute | solution.py:387
  173.8 3.3 %collective-permute-start.21 = (f32[4,4,128]{2,1,0:T(4,128)S(1)}, f32[4,4,128]{2,1,0:T(4,128)S(1)}, u32[]{:S(2)}, u32[]{:S(2)}) collective-permute-start(f32[4,4,128]{2,1,0:T(4,128)S(1)} %get-tuple-element.81), channel_id=1, source_target_pairs={{0,1},{1,0},{2,3},{3,2},{4,5},{5,4},{6,7},{7,6},{8,9},{9,8},{10,11... | collective-permute-start | bytes 24584 | tf_op jit(solution)/shard_map/ppermute | solution.py:411
  177.1 0.8 collective-permute-done.21.refs_2_
  177.9 4.1 %shard_map.94.force = f32[8,8,128]{2,1,0:T(8,128)S(1)} custom-call(f32[16,8,128]{2,1,0:T(8,128)S(1)} %shard_map.78.refs_0_, f32[8,8,128]{2,1,0:T(8,128)S(1)} %get-tuple-element.80.refs_1_.own, f32[4,4,128]{2,1,0:T(4,128)S(1)} %collective-permute-done.21.refs_2_, f32[4,8,128]{2,1,0:T(8,128)S(1)} %get-tuple-element.82.refs_3_), custom_call_target="tpu_custom_call" | custom-call | flops 20000000 | bytes 200000 | tf_op jit(solution)/shard_map/pallas_call | solution.py:373
  182.1 0.7 shard_map.95
  182.8 10.9 %all_to_all.34.sums = f32[32,1,128]{2,1,0:T(1,128)S(1)} all-to-all(f32[32,1,128]{2,1,0:T(1,128)S(1)} %get-tuple-element.84), channel_id=1, replica_groups=mesh['image'=16,'space'=32] {'space'}, dimensions={0} | all-to-all | bytes 32768 | tf_op jit(solution)/shard_map/all_to_all | solution.py:396
  193.7 0.8 shard_map.96
  (37 shorter events, 2.7 us)
Async XLA Ops:
  0.6 0.7 copy-start.1
  1.3 0.7 copy-start.2
  2.0 0.7 copy-start.3
  2.7 0.7 copy-start.4
  3.5 13.3 %collective-permute-start = (f32[4,8,128]{2,1,0:T(8,128)S(1)}, f32[4,8,128]{2,1,0:T(8,128)S(1)}, u32[]{:S(2)}, u32[]{:S(2)}) collective-permute-start(f32[4,8,128]{2,1,0:T(8,128)S(1)} %get-tuple-element.46), channel_id=1, source_target_pairs={{0,1},{1,0},{2,3},{3,2},{4,5},{5,4},{6,7},{7,6},{8,9},{9,8},{10,11... | collective-permute-start | bytes 49160 | tf_op jit(solution)/shard_map/ppermute | solution.py:357
  12.3 5.1 %collective-permute-start.1 = (f32[4,8,128]{2,1,0:T(8,128)S(1)}, f32[4,8,128]{2,1,0:T(8,128)S(1)}, u32[]{:S(2)}, u32[]{:S(2)}) collective-permute-start(f32[4,8,128]{2,1,0:T(8,128)S(1)} %get-tuple-element.47), channel_id=1, source_target_pairs={{0,31},{1,2},{2,1},{3,4},{4,3},{5,6},{6,5},{7,8},{8,7},{9,10},{10,... | collective-permute-start | bytes 49160 | tf_op jit(solution)/shard_map/ppermute | solution.py:358
  14.2 7.3 %collective-permute-start.3 = (f32[8,4,128]{2,1,0:T(4,128)S(1)}, f32[8,4,128]{2,1,0:T(4,128)S(1)}, u32[]{:S(2)}, u32[]{:S(2)}) collective-permute-start(f32[8,4,128]{2,1,0:T(4,128)S(1)} %get-tuple-element.48), channel_id=1, source_target_pairs={{32,64},{64,32},{96,128},{128,96},{160,192},{192,160},{224,256},{2... | collective-permute-start | bytes 49160 | tf_op jit(solution)/shard_map/ppermute | solution.py:388
  14.9 6.6 %collective-permute-start.2 = (f32[8,4,128]{2,1,0:T(4,128)S(1)}, f32[8,4,128]{2,1,0:T(4,128)S(1)}, u32[]{:S(2)}, u32[]{:S(2)}) collective-permute-start(f32[8,4,128]{2,1,0:T(4,128)S(1)} %get-tuple-element.48), channel_id=1, source_target_pairs={{0,32},{32,0},{64,96},{96,64},{128,160},{160,128},{192,224},{224,1... | collective-permute-start | bytes 49160 | tf_op jit(solution)/shard_map/ppermute | solution.py:387
  17.3 4.2 %copy-start = (f32[2,3,1024]{2,0,1:T(2,128)S(1)}, f32[2,3,1024]{2,0,1:T(2,128)}, u32[]{:S(2)}) copy-start(f32[2,3,1024]{2,0,1:T(2,128)} %param.7) | copy-start | bytes 73732
  22.2 19.6 %collective-permute-start.4 = (f32[4,24,128]{2,1,0:T(8,128)S(1)}, f32[4,24,128]{2,1,0:T(8,128)S(1)}, u32[]{:S(2)}, u32[]{:S(2)}) collective-permute-start(f32[4,24,128]{2,1,0:T(8,128)S(1)} %get-tuple-element.51), channel_id=1, source_target_pairs={{0,31},{1,2},{2,1},{3,4},{4,3},{5,6},{6,5},{7,8},{8,7},{9,10},{10,... | collective-permute-start | bytes 147464 | tf_op jit(solution)/shard_map/ppermute | solution.py:398
  25.4 16.5 %all-to-all-start = ((f32[32,1,128]{2,1,0:T(1,128)}), f32[32,1,128]{2,1,0:T(1,128)S(1)}, u32[]{:S(2)}, u32[]{:S(2)}) async-start(f32[32,1,128]{2,1,0:T(1,128)} %get-tuple-element.49), calls=%async_computation | async-start | bytes 32768 | tf_op jit(solution)/shard_map/all_to_all | solution.py:396
  42.0 16.8 %collective-permute-start.7 = (f32[8,4,128]{2,1,0:T(4,128)S(1)}, f32[8,4,128]{2,1,0:T(4,128)S(1)}, u32[]{:S(2)}, u32[]{:S(2)}) collective-permute-start(f32[8,4,128]{2,1,0:T(4,128)S(1)} %get-tuple-element.55), channel_id=1, source_target_pairs={{32,64},{64,32},{96,128},{128,96},{160,192},{192,160},{224,256},{2... | collective-permute-start | bytes 49160 | tf_op jit(solution)/shard_map/ppermute | solution.py:388
  42.7 16.1 %collective-permute-start.6 = (f32[8,4,128]{2,1,0:T(4,128)S(1)}, f32[8,4,128]{2,1,0:T(4,128)S(1)}, u32[]{:S(2)}, u32[]{:S(2)}) collective-permute-start(f32[8,4,128]{2,1,0:T(4,128)S(1)} %get-tuple-element.55), channel_id=1, source_target_pairs={{0,32},{32,0},{64,96},{96,64},{128,160},{160,128},{192,224},{224,1... | collective-permute-start | bytes 49160 | tf_op jit(solution)/shard_map/ppermute | solution.py:387
  50.6 4.1 %collective-permute-start.5 = (f32[4,4,128]{2,1,0:T(4,128)S(1)}, f32[4,4,128]{2,1,0:T(4,128)S(1)}, u32[]{:S(2)}, u32[]{:S(2)}) collective-permute-start(f32[4,4,128]{2,1,0:T(4,128)S(1)} %get-tuple-element.53), channel_id=1, source_target_pairs={{0,1},{1,0},{2,3},{3,2},{4,5},{5,4},{6,7},{7,6},{8,9},{9,8},{10,11... | collective-permute-start | bytes 24584 | tf_op jit(solution)/shard_map/ppermute | solution.py:411
  59.0 15.2 %collective-permute-start.8 = (f32[4,24,128]{2,1,0:T(8,128)S(1)}, f32[4,24,128]{2,1,0:T(8,128)S(1)}, u32[]{:S(2)}, u32[]{:S(2)}) collective-permute-start(f32[4,24,128]{2,1,0:T(8,128)S(1)} %get-tuple-element.58), channel_id=1, source_target_pairs={{0,31},{1,2},{2,1},{3,4},{4,3},{5,6},{6,5},{7,8},{8,7},{9,10},{10,... | collective-permute-start | bytes 147464 | tf_op jit(solution)/shard_map/ppermute | solution.py:398
  74.4 14.5 %collective-permute-start.11 = (f32[8,4,128]{2,1,0:T(4,128)S(1)}, f32[8,4,128]{2,1,0:T(4,128)S(1)}, u32[]{:S(2)}, u32[]{:S(2)}) collective-permute-start(f32[8,4,128]{2,1,0:T(4,128)S(1)} %get-tuple-element.62), channel_id=1, source_target_pairs={{32,64},{64,32},{96,128},{128,96},{160,192},{192,160},{224,256},{2... | collective-permute-start | bytes 49160 | tf_op jit(solution)/shard_map/ppermute | solution.py:388
  75.0 13.8 %collective-permute-start.10 = (f32[8,4,128]{2,1,0:T(4,128)S(1)}, f32[8,4,128]{2,1,0:T(4,128)S(1)}, u32[]{:S(2)}, u32[]{:S(2)}) collective-permute-start(f32[8,4,128]{2,1,0:T(4,128)S(1)} %get-tuple-element.62), channel_id=1, source_target_pairs={{0,32},{32,0},{64,96},{96,64},{128,160},{160,128},{192,224},{224,1... | collective-permute-start | bytes 49160 | tf_op jit(solution)/shard_map/ppermute | solution.py:387
  80.6 4.1 %collective-permute-start.9 = (f32[4,4,128]{2,1,0:T(4,128)S(1)}, f32[4,4,128]{2,1,0:T(4,128)S(1)}, u32[]{:S(2)}, u32[]{:S(2)}) collective-permute-start(f32[4,4,128]{2,1,0:T(4,128)S(1)} %get-tuple-element.60), channel_id=1, source_target_pairs={{0,1},{1,0},{2,3},{3,2},{4,5},{5,4},{6,7},{7,6},{8,9},{9,8},{10,11... | collective-permute-start | bytes 24584 | tf_op jit(solution)/shard_map/ppermute | solution.py:411
  89.0 15.2 %collective-permute-start.12 = (f32[4,24,128]{2,1,0:T(8,128)S(1)}, f32[4,24,128]{2,1,0:T(8,128)S(1)}, u32[]{:S(2)}, u32[]{:S(2)}) collective-permute-start(f32[4,24,128]{2,1,0:T(8,128)S(1)} %get-tuple-element.65), channel_id=1, source_target_pairs={{0,31},{1,2},{2,1},{3,4},{4,3},{5,6},{6,5},{7,8},{8,7},{9,10},{10,... | collective-permute-start | bytes 147464 | tf_op jit(solution)/shard_map/ppermute | solution.py:398
  104.3 17.1 %collective-permute-start.15 = (f32[8,4,128]{2,1,0:T(4,128)S(1)}, f32[8,4,128]{2,1,0:T(4,128)S(1)}, u32[]{:S(2)}, u32[]{:S(2)}) collective-permute-start(f32[8,4,128]{2,1,0:T(4,128)S(1)} %get-tuple-element.69), channel_id=1, source_target_pairs={{32,64},{64,32},{96,128},{128,96},{160,192},{192,160},{224,256},{2... | collective-permute-start | bytes 49160 | tf_op jit(solution)/shard_map/ppermute | solution.py:388
  105.0 16.5 %collective-permute-start.14 = (f32[8,4,128]{2,1,0:T(4,128)S(1)}, f32[8,4,128]{2,1,0:T(4,128)S(1)}, u32[]{:S(2)}, u32[]{:S(2)}) collective-permute-start(f32[8,4,128]{2,1,0:T(4,128)S(1)} %get-tuple-element.69), channel_id=1, source_target_pairs={{0,32},{32,0},{64,96},{96,64},{128,160},{160,128},{192,224},{224,1... | collective-permute-start | bytes 49160 | tf_op jit(solution)/shard_map/ppermute | solution.py:387
  113.2 4.1 %collective-permute-start.13 = (f32[4,4,128]{2,1,0:T(4,128)S(1)}, f32[4,4,128]{2,1,0:T(4,128)S(1)}, u32[]{:S(2)}, u32[]{:S(2)}) collective-permute-start(f32[4,4,128]{2,1,0:T(4,128)S(1)} %get-tuple-element.67), channel_id=1, source_target_pairs={{0,1},{1,0},{2,3},{3,2},{4,5},{5,4},{6,7},{7,6},{8,9},{9,8},{10,11... | collective-permute-start | bytes 24584 | tf_op jit(solution)/shard_map/ppermute | solution.py:411
  121.6 15.2 %collective-permute-start.16 = (f32[4,24,128]{2,1,0:T(8,128)S(1)}, f32[4,24,128]{2,1,0:T(8,128)S(1)}, u32[]{:S(2)}, u32[]{:S(2)}) collective-permute-start(f32[4,24,128]{2,1,0:T(8,128)S(1)} %get-tuple-element.72), channel_id=1, source_target_pairs={{0,31},{1,2},{2,1},{3,4},{4,3},{5,6},{6,5},{7,8},{8,7},{9,10},{10,... | collective-permute-start | bytes 147464 | tf_op jit(solution)/shard_map/ppermute | solution.py:398
  137.0 14.5 %collective-permute-start.19 = (f32[8,4,128]{2,1,0:T(4,128)S(1)}, f32[8,4,128]{2,1,0:T(4,128)S(1)}, u32[]{:S(2)}, u32[]{:S(2)}) collective-permute-start(f32[8,4,128]{2,1,0:T(4,128)S(1)} %get-tuple-element.76), channel_id=1, source_target_pairs={{32,64},{64,32},{96,128},{128,96},{160,192},{192,160},{224,256},{2... | collective-permute-start | bytes 49160 | tf_op jit(solution)/shard_map/ppermute | solution.py:388
  137.7 13.8 %collective-permute-start.18 = (f32[8,4,128]{2,1,0:T(4,128)S(1)}, f32[8,4,128]{2,1,0:T(4,128)S(1)}, u32[]{:S(2)}, u32[]{:S(2)}) collective-permute-start(f32[8,4,128]{2,1,0:T(4,128)S(1)} %get-tuple-element.76), channel_id=1, source_target_pairs={{0,32},{32,0},{64,96},{96,64},{128,160},{160,128},{192,224},{224,1... | collective-permute-start | bytes 49160 | tf_op jit(solution)/shard_map/ppermute | solution.py:387
  143.2 4.1 %collective-permute-start.17 = (f32[4,4,128]{2,1,0:T(4,128)S(1)}, f32[4,4,128]{2,1,0:T(4,128)S(1)}, u32[]{:S(2)}, u32[]{:S(2)}) collective-permute-start(f32[4,4,128]{2,1,0:T(4,128)S(1)} %get-tuple-element.74), channel_id=1, source_target_pairs={{0,1},{1,0},{2,3},{3,2},{4,5},{5,4},{6,7},{7,6},{8,9},{9,8},{10,11... | collective-permute-start | bytes 24584 | tf_op jit(solution)/shard_map/ppermute | solution.py:411
  151.6 15.2 %collective-permute-start.20 = (f32[4,24,128]{2,1,0:T(8,128)S(1)}, f32[4,24,128]{2,1,0:T(8,128)S(1)}, u32[]{:S(2)}, u32[]{:S(2)}) collective-permute-start(f32[4,24,128]{2,1,0:T(8,128)S(1)} %get-tuple-element.79), channel_id=1, source_target_pairs={{0,31},{1,2},{2,1},{3,4},{4,3},{5,6},{6,5},{7,8},{8,7},{9,10},{10,... | collective-permute-start | bytes 147464 | tf_op jit(solution)/shard_map/ppermute | solution.py:398
  167.0 15.1 %collective-permute-start.23 = (f32[8,4,128]{2,1,0:T(4,128)S(1)}, f32[8,4,128]{2,1,0:T(4,128)S(1)}, u32[]{:S(2)}, u32[]{:S(2)}) collective-permute-start(f32[8,4,128]{2,1,0:T(4,128)S(1)} %get-tuple-element.83), channel_id=1, source_target_pairs={{32,64},{64,32},{96,128},{128,96},{160,192},{192,160},{224,256},{2... | collective-permute-start | bytes 49160 | tf_op jit(solution)/shard_map/ppermute | solution.py:388
  167.7 14.4 %collective-permute-start.22 = (f32[8,4,128]{2,1,0:T(4,128)S(1)}, f32[8,4,128]{2,1,0:T(4,128)S(1)}, u32[]{:S(2)}, u32[]{:S(2)}) collective-permute-start(f32[8,4,128]{2,1,0:T(4,128)S(1)} %get-tuple-element.83), channel_id=1, source_target_pairs={{0,32},{32,0},{64,96},{96,64},{128,160},{160,128},{192,224},{224,1... | collective-permute-start | bytes 49160 | tf_op jit(solution)/shard_map/ppermute | solution.py:387
  173.8 4.1 %collective-permute-start.21 = (f32[4,4,128]{2,1,0:T(4,128)S(1)}, f32[4,4,128]{2,1,0:T(4,128)S(1)}, u32[]{:S(2)}, u32[]{:S(2)}) collective-permute-start(f32[4,4,128]{2,1,0:T(4,128)S(1)} %get-tuple-element.81), channel_id=1, source_target_pairs={{0,1},{1,0},{2,3},{3,2},{4,5},{5,4},{6,7},{7,6},{8,9},{9,8},{10,11... | collective-permute-start | bytes 24584 | tf_op jit(solution)/shard_map/ppermute | solution.py:411

commit v2 on v1

--- a/solution.py
+++ b/solution.py
@@ -66,7 +66,18 @@
     return 1 - (lax.axis_index("space") & 1)
 
 
-def pack_kernel(disp, live, cells, used, own, image_out, near_out, far_out):
+def pack_kernel(*refs):
+    own, image_out, near_out, far_out = refs[4:8]
+    done = refs[12]
+    copies = [
+        pltpu.make_async_copy(source, target, done.at[n])
+        for n, (source, target) in enumerate(zip(refs[:4], refs[8:12]))
+    ]
+    for copy in copies:
+        copy.start()
+    for copy in copies:
+        copy.wait()
+    disp, live, cells, used = refs[8:12]
     even = space_even()
     row = rows_iota()
     lane = lanes_iota()
@@ -96,10 +107,10 @@
 
 def force_kernel(first, *refs):
     if first:
-        wide, force, left, right, sums, slope_sums, powers, density = refs
+        wide, force, left, right, sums, slopes, tiles, density = refs
     else:
         base, own, near, far, force = refs[:5]
-        left, right, sums, slope_sums, powers, density, wide = refs[5:]
+        left, right, sums, slopes, tiles, density, wide = refs[5:]
         even = space_even()
         wide[pl.ds(HALO, CELLS)] = own[...]
         wide[pl.ds((1 - even) * (HALO + CELLS), HALO)] = far[...]
@@ -135,7 +146,7 @@
         sums[c] = tall([h, m, l, jnp.zeros_like(h)]).astype(bf16)
         return 0
 
-    lax.fori_loop(0, WIDE, prepare_left, 0, unroll=8)
+    lax.fori_loop(0, WIDE, prepare_left, 0, unroll=16)
 
     def prepare_right(c, _):
         p = placed(c)
@@ -148,14 +159,10 @@
             right[c, n] = tall([h, m, h, m, l, h]).astype(bf16)
         return 0
 
-    lax.fori_loop(DENSE.start, DENSE.stop, prepare_right, 0, unroll=4)
+    lax.fori_loop(DENSE.start, DENSE.stop, prepare_right, 0, unroll=12)
 
     def folded(t):
         return jnp.sum(t.reshape(SLOTS // 8, 8, SLOTS), axis=0)
-
-    def two_parts(v):
-        high = v.astype(bf16)
-        return high, (v - high.astype(f32)).astype(bf16)
 
     def cell_pair(c, owned):
         total = [jnp.zeros((8, SLOTS), f32), jnp.zeros((8, SLOTS), f32)]
@@ -166,14 +173,9 @@
             near = jnp.dot(left[c + dh], rhs, preferred_element_type=f32)
             for b, (i, n) in enumerate(sides):
                 t = jnp.maximum(near[:, b * SLOTS : (b + 1) * SLOTS], 0.0)
+                if owned:
+                    tiles[c - HALO + i, n] = t
                 square = t * t
-                if owned:
-                    for k, v in enumerate((square * t, square)):
-                        columns = slice(k * SLOTS, (k + 1) * SLOTS)
-                        high, low = two_parts(v)
-                        at = 2 * n * SLOTS
-                        powers[c - HALO + i, at : at + SLOTS, columns] = high
-                        powers[c - HALO + i, at + SLOTS : at + 2 * SLOTS, columns] = low
                 total[i] = total[i] + weight_of(c + i, n) * folded(square * square)
         for i in (0, 1):
             value = jnp.sum(total[i], axis=0, keepdims=True) - weight_of(c + i, 2)
@@ -189,48 +191,54 @@
         return 0
 
     lax.fori_loop(0, 2, rim_pair, 0, unroll=2)
-    lax.fori_loop(0, CELLS // 2, own_pair, 0)
+    lax.fori_loop(0, CELLS // 2, own_pair, 0, unroll=4)
 
     def prepare_slopes(c, _):
-        h, m, l = three_parts(partner_rows(c) * density[c])
-        slope_sums[c] = tall([h, m, l, jnp.zeros_like(h)]).astype(bf16)
-        return 0
-
-    lax.fori_loop(DENSE.start, DENSE.stop, prepare_slopes, 0, unroll=6)
-
-    tilt_row = lax.broadcasted_iota(jnp.int32, (64, SLOTS), 0) % 8 == 6
-
-    def force_cell(k, _):
-        c = HALO + k
-        parts = []
-        for n, o in enumerate(OFFSETS):
-            weight = weight_of(c, n)
-            factor = jnp.where(tilt_row, o * weight, weight).astype(bf16)
-            rows = tall([sums[c + o], slope_sums[c + o]]) * factor
-            parts += [rows, rows]
-        got = jnp.dot(
-            jnp.concatenate(parts, axis=1), powers[k], preferred_element_type=f32
-        )
-
-        def joined(at, columns):
-            x = got[at : at + 24, columns]
-            return x[0:8] + x[8:16] + x[16:24]
-
-        cubes, squared = slice(0, SLOTS), slice(SLOTS, 2 * SLOTS)
-        total = (
-            -4.0 * (density[c] * joined(0, cubes) + joined(32, cubes))
-            - 3.0 * pair_strength * joined(0, squared)
-        )
-        value = total - (2.0 / cutoff_sq) * placed(c) * total[4:5]
-        value = jnp.where(row == 0, value + (4.0 / cutoff_sq) * total[6:7], value)
-        force[k] = jnp.where(row < 3, value * wide[c, 3:4, :], 0.0)
-        return 0
-
-    lax.fori_loop(0, CELLS, force_cell, 0, unroll=4)
-
-
-def gaps_kernel(own, force, from_a, from_b, ends, packed, far_out, sums):
-    even = space_even()
+        slope = -4.0 * density[c]
+        high = slope.astype(bf16).astype(f32)
+        rest = (slope - high).astype(bf16).astype(f32)
+        lines = jnp.where(row == 0, high, jnp.where(row == 1, rest, 0.0))
+        column = tall([lines, jnp.zeros_like(lines)]).T.astype(bf16)
+        slopes[c] = jnp.dot(column, jnp.ones((16, SLOTS), bf16), preferred_element_type=f32)
+        return 0
+
+    lax.fori_loop(DENSE.start, DENSE.stop, prepare_slopes, 0, unroll=12)
+
+    def force_pair(k, _):
+        c = HALO + 2 * k
+        total = [jnp.zeros((8, SLOTS), f32), jnp.zeros((8, SLOTS), f32)]
+        tilt = [jnp.zeros((8, SLOTS), f32), jnp.zeros((8, SLOTS), f32)]
+        ours = [-4.0 * density[c], -4.0 * density[c + 1]]
+        for dh in range(-2, 4):
+            sides = [(i, dh - i + 2) for i in (0, 1) if 0 <= dh - i + 2 < 5]
+            highs, lows = [], []
+            for i, n in sides:
+                t = tiles[2 * k + i, n]
+                value = t * t * ((slopes[c + dh] + ours[i]) * t - 3.0 * pair_strength)
+                high = value.astype(bf16)
+                highs.append(high)
+                lows.append((value - high.astype(f32)).astype(bf16))
+            got = jnp.dot(
+                jnp.concatenate([sums[c + dh]] * 2, axis=1),
+                tall([jnp.concatenate(v, axis=1) if len(v) > 1 else v[0] for v in (highs, lows)]),
+                preferred_element_type=f32,
+            )
+            for b, (i, n) in enumerate(sides):
+                part = got[:, b * SLOTS : (b + 1) * SLOTS]
+                part = weight_of(c + i, n) * (part[0:8] + part[8:16] + part[16:24])
+                total[i] = total[i] + part
+                if OFFSETS[n]:
+                    tilt[i] = tilt[i] + (4.0 * OFFSETS[n] / cutoff_sq) * part
+        for i in (0, 1):
+            value = total[i] - (2.0 / cutoff_sq) * placed(c + i) * total[i][4:5]
+            value = jnp.where(row == 0, value + tilt[i][4:5], value)
+            force[2 * k + i] = jnp.where(row < 3, value * wide[c + i, 3:4, :], 0.0)
+        return 0
+
+    lax.fori_loop(0, CELLS // 2, force_pair, 0, unroll=4)
+
+
+def gaps_kernel(own, force, from_a, from_b, ends, packed, sums, far_out=None):
     image = lax.axis_index("image")
     image_even = 1 - (image & 1)
     edge = (image == 0) | (image == lax.axis_size("image") - 1)
@@ -264,7 +272,8 @@
         value = jnp.sum(jnp.sum(t, axis=0, keepdims=True), axis=1, keepdims=True)
         line = jnp.where(lane == n, value, line)
     sums[...] = jnp.broadcast_to(line[None], sums.shape)
-    far_out[...] = packed[pl.ds((1 - even) * HALO, HALO)]
+    if far_out is not None:
+        far_out[...] = packed[pl.ds((1 - space_even()) * HALO, HALO)]
 
 
 def band_terms(sums, spring):
@@ -348,12 +357,23 @@
     image_a, image_b = swap_pairs("image", False)
     space_a, space_b = swap_pairs("space", True)
 
-    own, image_out, near, far = call(
+    raw = (displacement.transpose(1, 0, 2), atom_live[None], partner_cells, partner_live)
+    outs = (
+        shape(CELLS, 8, SLOTS),
+        shape(CELLS, 4, SLOTS),
+        shape(HALO, 8, SLOTS),
+        shape(HALO, 8, SLOTS),
+    )
+    own, image_out, near, far = pl.pallas_call(
         pack_kernel,
-        (shape(CELLS, 8, SLOTS), shape(CELLS, 4, SLOTS), shape(HALO, 8, SLOTS), shape(HALO, 8, SLOTS)),
-        0,
-        4,
-    )(displacement.transpose(1, 0, 2), atom_live[None], partner_cells, partner_live)
+        out_shape=outs,
+        in_specs=[pl.BlockSpec(memory_space=pltpu.HBM)] * 4,
+        out_specs=tuple(vmem(4)),
+        scratch_shapes=[pltpu.VMEM(v.shape, v.dtype) for v in raw]
+        + [pltpu.SemaphoreType.DMA((4,))],
+        name="pack",
+        compiler_params=pltpu.CompilerParams(vmem_limit_bytes=62 << 20),
+    )(*raw)
     near = lax.ppermute(near, "space", space_a)
     far = lax.ppermute(far, "space", space_b)
     base = call(join_kernel, shape(WIDE, 8, SLOTS), 0, 3)(own, near, far)
@@ -364,8 +384,8 @@
             pltpu.VMEM((WIDE, SLOTS, 48), bf16),
             pltpu.VMEM((WIDE, 5, 48, SLOTS), bf16),
             pltpu.VMEM((WIDE, 32, SLOTS), bf16),
-            pltpu.VMEM((WIDE, 32, SLOTS), bf16),
-            pltpu.VMEM((CELLS, 10 * SLOTS, 2 * SLOTS), bf16),
+            pltpu.VMEM((WIDE, SLOTS, SLOTS), f32),
+            pltpu.VMEM((CELLS, 5, SLOTS, SLOTS), f32),
             pltpu.VMEM((WIDE, 1, SLOTS), f32),
         ]
         if not first:
@@ -387,16 +407,18 @@
         from_a = lax.ppermute(image_out, "image", image_a)
         from_b = lax.ppermute(image_out, "image", image_b)
         force = forces(*operands)
-        packed, far_packed, sums = call(
+        more = iteration < ITERATIONS - 1
+        packed, sums, *far_packed = call(
             gaps_kernel,
-            (shape(CELLS, 24, SLOTS), shape(HALO, 24, SLOTS), shape(parts, 1, SLOTS)),
+            (shape(CELLS, 24, SLOTS), shape(parts, 1, SLOTS))
+            + (shape(HALO, 24, SLOTS),) * more,
             0,
             5,
         )(own, force, from_a, from_b, end_states)
         sums = lax.all_to_all(sums, "space", 0, 0, tiled=True)
-        if iteration < ITERATIONS - 1:
-            far_packed = lax.ppermute(far_packed, "space", space_b)
-        if iteration < ITERATIONS - 1:
+        if more:
+            far_packed = lax.ppermute(far_packed[0], "space", space_b)
+        if more:
             own, far, image_out, near = call(
                 moved_kernel,
                 (

time: 196 us -> 183 us (0.934)
  Pallas kernels: 28.4 us -> 17.5 us
  local copies, waits for them, and re-layouts: 2.76 us -> 0.77 us
    pallas_call x6, Pallas kernels: 24.8 us -> 13 us  [forces(): call(functools.partial(force_kernel, first), shape(CELLS, 8, SLOTS), 0, 1...]
    unnamed x10 -> x6, local copies, waits for them, and re-layouts: 2.76 us -> 0.77 us
  transfers between devices with their start and end apart: 25 -> 25, of which waited for: 7 -> 7; matrix products, arithmetic and copies ran while one was open for 0% -> 0% of each run, Pallas kernels for 13% -> 7%
where the time goes in v2:
time: 183 us; the launch traced here: 182 us
  starting transfers between devices  87.9 us (48%)
  blocking collectives  61.9 us (34%)
  Pallas kernels  17.5 us (10%)
  waiting for transfers between devices  11.9 us (7%)
    all_to_all x5, blocking collectives, body(): sums = lax.all_to_all(sums, 'space', 0, 0, tiled=True)  61.9 us
    ppermute x6, starting transfers between devices, body(): from_a = lax.ppermute(image_out, 'image', image_a)  35.4 us
    ppermute x6, starting transfers between devices, body(): near = lax.ppermute(near, 'space', space_a)  25.3 us
    ppermute x5, starting transfers between devices, body(): far_packed = lax.ppermute(far_packed[0], 'space', space_b)  13.6 us
    pallas_call x6, Pallas kernels, forces(): call(functools.partial(force_kernel, first), shape(CELLS, 8, SLOTS), 0, 1...  13 us
    all_to_all x1, starting transfers between devices, body(): sums = lax.all_to_all(sums, 'space', 0, 0, tiled=True)  7.72 us
    all_to_all x1, waiting for transfers between devices, body(): sums = lax.all_to_all(sums, 'space', 0, 0, tiled=True)  7.24 us
    ppermute x6, starting transfers between devices, body(): from_b = lax.ppermute(image_out, 'image', image_b)  3.97 us
  transfers between devices with their start and end apart: 25, of which 7 were waited for; matrix products, arithmetic and copies ran while one was open for 0% of the time, Pallas kernels for 7%

profile of v2, /device:TPU:1, one launch (start us, length us, event | category | flops | bytes accessed | tf_op | source)
XLA Modules:
  0.0 181.7 jit_solution(15905429071329180009)
XLA Ops:
  0.6 1.5 pack.1
  2.1 8.7 %collective-permute-start = (f32[4,8,128]{2,1,0:T(8,128)}, f32[4,8,128]{2,1,0:T(8,128)S(1)}, u32[]{:S(2)}, u32[]{:S(2)}) collective-permute-start(f32[4,8,128]{2,1,0:T(8,128)} %get-tuple-element.46), channel_id=1, source_target_pairs={{0,1},{1,0},{2,3},{3,2},{4,5},{5,4},{6,7},{7,6},{8,9},{9,8},{10,11... | collective-permute-start | bytes 49160 | tf_op jit(solution)/shard_map/ppermute | solution.py:377
  10.9 1.9 %collective-permute-start.1 = (f32[4,8,128]{2,1,0:T(8,128)}, f32[4,8,128]{2,1,0:T(8,128)S(1)}, u32[]{:S(2)}, u32[]{:S(2)}) collective-permute-start(f32[4,8,128]{2,1,0:T(8,128)} %get-tuple-element.47), channel_id=1, source_target_pairs={{0,31},{1,2},{2,1},{3,4},{4,3},{5,6},{6,5},{7,8},{8,7},{9,10},{10,... | collective-permute-start | bytes 49160 | tf_op jit(solution)/shard_map/ppermute | solution.py:378
  12.8 0.7 collective-permute-start.3
  13.5 1.9 %collective-permute-start.2 = (f32[8,4,128]{2,1,0:T(4,128)}, f32[8,4,128]{2,1,0:T(4,128)S(1)}, u32[]{:S(2)}, u32[]{:S(2)}) collective-permute-start(f32[8,4,128]{2,1,0:T(4,128)} %get-tuple-element.48), channel_id=1, source_target_pairs={{0,32},{32,0},{64,96},{96,64},{128,160},{160,128},{192,224},{224,1... | collective-permute-start | bytes 49160 | tf_op jit(solution)/shard_map/ppermute | solution.py:407
  15.4 0.7 collective-permute-done.1.far.old_far
  16.2 0.8 copy-done.1
  16.9 2.2 %shard_map.78.force = f32[8,8,128]{2,1,0:T(8,128)S(1)} custom-call(f32[16,8,128]{2,1,0:T(8,128)S(1)} %shard_map.77.refs_0_), custom_call_target="tpu_custom_call" | custom-call | flops 20000000 | bytes 200000 | tf_op jit(solution)/shard_map/pallas_call | solution.py:393
  19.2 0.7 shard_map.79
  19.9 3.8 %collective-permute-start.4 = (f32[4,24,128]{2,1,0:T(8,128)S(1)}, f32[4,24,128]{2,1,0:T(8,128)S(1)}, u32[]{:S(2)}, u32[]{:S(2)}) collective-permute-start(f32[4,24,128]{2,1,0:T(8,128)S(1)} %get-tuple-element.51), channel_id=1, source_target_pairs={{0,31},{1,2},{2,1},{3,4},{4,3},{5,6},{6,5},{7,8},{8,7},{9,10},{10,... | collective-permute-start | bytes 147464 | tf_op jit(solution)/shard_map/ppermute | solution.py:420
  23.7 7.7 %all-to-all-start = ((f32[32,1,128]{2,1,0:T(1,128)}), f32[32,1,128]{2,1,0:T(1,128)S(1)}, u32[]{:S(2)}, u32[]{:S(2)}) async-start(f32[32,1,128]{2,1,0:T(1,128)} %get-tuple-element.49), calls=%async_computation | async-start | bytes 32768 | tf_op jit(solution)/shard_map/all_to_all | solution.py:418
  32.1 7.2 %all-to-all-done.sums = f32[32,1,128]{2,1,0:T(1,128)S(1)} async-done(((f32[32,1,128]{2,1,0:T(1,128)}), f32[32,1,128]{2,1,0:T(1,128)S(1)}, u32[]{:S(2)}, u32[]{:S(2)}) %all-to-all-start) | async-done | bytes 16416 | tf_op jit(solution)/shard_map/all_to_all | solution.py:418
  39.3 0.2 shard_map.80
  39.5 0.7 collective-permute-start.7
  40.2 7.9 %collective-permute-start.6 = (f32[8,4,128]{2,1,0:T(4,128)S(1)}, f32[8,4,128]{2,1,0:T(4,128)S(1)}, u32[]{:S(2)}, u32[]{:S(2)}) collective-permute-start(f32[8,4,128]{2,1,0:T(4,128)S(1)} %get-tuple-element.55), channel_id=1, source_target_pairs={{0,32},{32,0},{64,96},{96,64},{128,160},{160,128},{192,224},{224,1... | collective-permute-start | bytes 49160 | tf_op jit(solution)/shard_map/ppermute | solution.py:407
  48.1 3.3 %collective-permute-start.5 = (f32[4,4,128]{2,1,0:T(4,128)S(1)}, f32[4,4,128]{2,1,0:T(4,128)S(1)}, u32[]{:S(2)}, u32[]{:S(2)}) collective-permute-start(f32[4,4,128]{2,1,0:T(4,128)S(1)} %get-tuple-element.53), channel_id=1, source_target_pairs={{0,1},{1,0},{2,3},{3,2},{4,5},{5,4},{6,7},{7,6},{8,9},{9,8},{10,11... | collective-permute-start | bytes 24584 | tf_op jit(solution)/shard_map/ppermute | solution.py:433
  51.3 0.8 collective-permute-done.5.refs_2_
  52.1 2.2 %shard_map.81.force = f32[8,8,128]{2,1,0:T(8,128)S(1)} custom-call(f32[16,8,128]{2,1,0:T(8,128)S(1)} %shard_map.77.refs_0_, f32[8,8,128]{2,1,0:T(8,128)S(1)} %get-tuple-element.52.refs_1_.own.old, f32[4,4,128]{2,1,0:T(4,128)S(1)} %collective-permute-done.5.refs_2_, f32[4,8,128]{2,1,0:T(8,128)S(1)} %get-tuple-element.54.refs_3_.old_far), custom_call_target="tpu_custom_call" | custom-call | flops 20000000 | bytes 200000 | tf_op jit(solution)/shard_map/pallas_call | solution.py:393
  54.5 2.4 %collective-permute-start.8 = (f32[4,24,128]{2,1,0:T(8,128)S(1)}, f32[4,24,128]{2,1,0:T(8,128)S(1)}, u32[]{:S(2)}, u32[]{:S(2)}) collective-permute-start(f32[4,24,128]{2,1,0:T(8,128)S(1)} %get-tuple-element.58), channel_id=1, source_target_pairs={{0,31},{1,2},{2,1},{3,4},{4,3},{5,6},{6,5},{7,8},{8,7},{9,10},{10,... | collective-permute-start | bytes 147464 | tf_op jit(solution)/shard_map/ppermute | solution.py:420
  56.9 12.8 %all_to_all.30.sums = f32[32,1,128]{2,1,0:T(1,128)S(1)} all-to-all(f32[32,1,128]{2,1,0:T(1,128)S(1)} %get-tuple-element.56), channel_id=1, replica_groups=mesh['image'=16,'space'=32] {'space'}, dimensions={0} | all-to-all | bytes 32768 | tf_op jit(solution)/shard_map/all_to_all | solution.py:418
  69.8 0.7 collective-permute-start.11
  70.5 5.6 %collective-permute-start.10 = (f32[8,4,128]{2,1,0:T(4,128)S(1)}, f32[8,4,128]{2,1,0:T(4,128)S(1)}, u32[]{:S(2)}, u32[]{:S(2)}) collective-permute-start(f32[8,4,128]{2,1,0:T(4,128)S(1)} %get-tuple-element.62), channel_id=1, source_target_pairs={{0,32},{32,0},{64,96},{96,64},{128,160},{160,128},{192,224},{224,1... | collective-permute-start | bytes 49160 | tf_op jit(solution)/shard_map/ppermute | solution.py:407
  76.1 3.3 %collective-permute-start.9 = (f32[4,4,128]{2,1,0:T(4,128)S(1)}, f32[4,4,128]{2,1,0:T(4,128)S(1)}, u32[]{:S(2)}, u32[]{:S(2)}) collective-permute-start(f32[4,4,128]{2,1,0:T(4,128)S(1)} %get-tuple-element.60), channel_id=1, source_target_pairs={{0,1},{1,0},{2,3},{3,2},{4,5},{5,4},{6,7},{7,6},{8,9},{9,8},{10,11... | collective-permute-start | bytes 24584 | tf_op jit(solution)/shard_map/ppermute | solution.py:433
  79.4 0.8 collective-permute-done.9.refs_2_
  80.2 2.2 %shard_map.84.force = f32[8,8,128]{2,1,0:T(8,128)S(1)} custom-call(f32[16,8,128]{2,1,0:T(8,128)S(1)} %shard_map.77.refs_0_, f32[8,8,128]{2,1,0:T(8,128)S(1)} %get-tuple-element.59.refs_1_.own.old, f32[4,4,128]{2,1,0:T(4,128)S(1)} %collective-permute-done.9.refs_2_, f32[4,8,128]{2,1,0:T(8,128)S(1)} %get-tuple-element.61.refs_3_.old_far), custom_call_target="tpu_custom_call" | custom-call | flops 20000000 | bytes 200000 | tf_op jit(solution)/shard_map/pallas_call | solution.py:393
  82.5 2.5 %collective-permute-start.12 = (f32[4,24,128]{2,1,0:T(8,128)S(1)}, f32[4,24,128]{2,1,0:T(8,128)S(1)}, u32[]{:S(2)}, u32[]{:S(2)}) collective-permute-start(f32[4,24,128]{2,1,0:T(8,128)S(1)} %get-tuple-element.65), channel_id=1, source_target_pairs={{0,31},{1,2},{2,1},{3,4},{4,3},{5,6},{6,5},{7,8},{8,7},{9,10},{10,... | collective-permute-start | bytes 147464 | tf_op jit(solution)/shard_map/ppermute | solution.py:420
  85.0 12.7 %all_to_all.31.sums = f32[32,1,128]{2,1,0:T(1,128)S(1)} all-to-all(f32[32,1,128]{2,1,0:T(1,128)S(1)} %get-tuple-element.63), channel_id=1, replica_groups=mesh['image'=16,'space'=32] {'space'}, dimensions={0} | all-to-all | bytes 32768 | tf_op jit(solution)/shard_map/all_to_all | solution.py:418
  97.9 0.7 collective-permute-start.15
  98.6 8.2 %collective-permute-start.14 = (f32[8,4,128]{2,1,0:T(4,128)S(1)}, f32[8,4,128]{2,1,0:T(4,128)S(1)}, u32[]{:S(2)}, u32[]{:S(2)}) collective-permute-start(f32[8,4,128]{2,1,0:T(4,128)S(1)} %get-tuple-element.69), channel_id=1, source_target_pairs={{0,32},{32,0},{64,96},{96,64},{128,160},{160,128},{192,224},{224,1... | collective-permute-start | bytes 49160 | tf_op jit(solution)/shard_map/ppermute | solution.py:407
  106.8 3.3 %collective-permute-start.13 = (f32[4,4,128]{2,1,0:T(4,128)S(1)}, f32[4,4,128]{2,1,0:T(4,128)S(1)}, u32[]{:S(2)}, u32[]{:S(2)}) collective-permute-start(f32[4,4,128]{2,1,0:T(4,128)S(1)} %get-tuple-element.67), channel_id=1, source_target_pairs={{0,1},{1,0},{2,3},{3,2},{4,5},{5,4},{6,7},{7,6},{8,9},{9,8},{10,11... | collective-permute-start | bytes 24584 | tf_op jit(solution)/shard_map/ppermute | solution.py:433
  110.1 0.8 collective-permute-done.13.refs_2_
  110.9 2.2 %shard_map.87.force = f32[8,8,128]{2,1,0:T(8,128)S(1)} custom-call(f32[16,8,128]{2,1,0:T(8,128)S(1)} %shard_map.77.refs_0_, f32[8,8,128]{2,1,0:T(8,128)S(1)} %get-tuple-element.66.refs_1_.own.old, f32[4,4,128]{2,1,0:T(4,128)S(1)} %collective-permute-done.13.refs_2_, f32[4,8,128]{2,1,0:T(8,128)S(1)} %get-tuple-element.68.refs_3_.old_far), custom_call_target="tpu_custom_call" | custom-call | flops 20000000 | bytes 200000 | tf_op jit(solution)/shard_map/pallas_call | solution.py:393
  113.2 2.5 %collective-permute-start.16 = (f32[4,24,128]{2,1,0:T(8,128)S(1)}, f32[4,24,128]{2,1,0:T(8,128)S(1)}, u32[]{:S(2)}, u32[]{:S(2)}) collective-permute-start(f32[4,24,128]{2,1,0:T(8,128)S(1)} %get-tuple-element.72), channel_id=1, source_target_pairs={{0,31},{1,2},{2,1},{3,4},{4,3},{5,6},{6,5},{7,8},{8,7},{9,10},{10,... | collective-permute-start | bytes 147464 | tf_op jit(solution)/shard_map/ppermute | solution.py:420
  115.7 12.7 %all_to_all.32.sums = f32[32,1,128]{2,1,0:T(1,128)S(1)} all-to-all(f32[32,1,128]{2,1,0:T(1,128)S(1)} %get-tuple-element.70), channel_id=1, replica_groups=mesh['image'=16,'space'=32] {'space'}, dimensions={0} | all-to-all | bytes 32768 | tf_op jit(solution)/shard_map/all_to_all | solution.py:418
  128.6 0.7 collective-permute-start.19
  129.2 5.6 %collective-permute-start.18 = (f32[8,4,128]{2,1,0:T(4,128)S(1)}, f32[8,4,128]{2,1,0:T(4,128)S(1)}, u32[]{:S(2)}, u32[]{:S(2)}) collective-permute-start(f32[8,4,128]{2,1,0:T(4,128)S(1)} %get-tuple-element.76), channel_id=1, source_target_pairs={{0,32},{32,0},{64,96},{96,64},{128,160},{160,128},{192,224},{224,1... | collective-permute-start | bytes 49160 | tf_op jit(solution)/shard_map/ppermute | solution.py:407
  134.8 3.5 %collective-permute-start.17 = (f32[4,4,128]{2,1,0:T(4,128)S(1)}, f32[4,4,128]{2,1,0:T(4,128)S(1)}, u32[]{:S(2)}, u32[]{:S(2)}) collective-permute-start(f32[4,4,128]{2,1,0:T(4,128)S(1)} %get-tuple-element.74), channel_id=1, source_target_pairs={{0,1},{1,0},{2,3},{3,2},{4,5},{5,4},{6,7},{7,6},{8,9},{9,8},{10,11... | collective-permute-start | bytes 24584 | tf_op jit(solution)/shard_map/ppermute | solution.py:433
  138.3 0.6 collective-permute-done.17.refs_2_
  138.9 2.2 %shard_map.90.force = f32[8,8,128]{2,1,0:T(8,128)S(1)} custom-call(f32[16,8,128]{2,1,0:T(8,128)S(1)} %shard_map.77.refs_0_, f32[8,8,128]{2,1,0:T(8,128)S(1)} %get-tuple-element.73.refs_1_.own.old, f32[4,4,128]{2,1,0:T(4,128)S(1)} %collective-permute-done.17.refs_2_, f32[4,8,128]{2,1,0:T(8,128)S(1)} %get-tuple-element.75.refs_3_.old_far), custom_call_target="tpu_custom_call" | custom-call | flops 20000000 | bytes 200000 | tf_op jit(solution)/shard_map/pallas_call | solution.py:393
  141.3 2.5 %collective-permute-start.20 = (f32[4,24,128]{2,1,0:T(8,128)S(1)}, f32[4,24,128]{2,1,0:T(8,128)S(1)}, u32[]{:S(2)}, u32[]{:S(2)}) collective-permute-start(f32[4,24,128]{2,1,0:T(8,128)S(1)} %get-tuple-element.79), channel_id=1, source_target_pairs={{0,31},{1,2},{2,1},{3,4},{4,3},{5,6},{6,5},{7,8},{8,7},{9,10},{10,... | collective-permute-start | bytes 147464 | tf_op jit(solution)/shard_map/ppermute | solution.py:420
  143.7 12.7 %all_to_all.33.sums = f32[32,1,128]{2,1,0:T(1,128)S(1)} all-to-all(f32[32,1,128]{2,1,0:T(1,128)S(1)} %get-tuple-element.77), channel_id=1, replica_groups=mesh['image'=16,'space'=32] {'space'}, dimensions={0} | all-to-all | bytes 32768 | tf_op jit(solution)/shard_map/all_to_all | solution.py:418
  156.6 0.7 collective-permute-start.23
  157.3 6.2 %collective-permute-start.22 = (f32[8,4,128]{2,1,0:T(4,128)S(1)}, f32[8,4,128]{2,1,0:T(4,128)S(1)}, u32[]{:S(2)}, u32[]{:S(2)}) collective-permute-start(f32[8,4,128]{2,1,0:T(4,128)S(1)} %get-tuple-element.83), channel_id=1, source_target_pairs={{0,32},{32,0},{64,96},{96,64},{128,160},{160,128},{192,224},{224,1... | collective-permute-start | bytes 49160 | tf_op jit(solution)/shard_map/ppermute | solution.py:407
  163.5 3.3 %collective-permute-start.21 = (f32[4,4,128]{2,1,0:T(4,128)S(1)}, f32[4,4,128]{2,1,0:T(4,128)S(1)}, u32[]{:S(2)}, u32[]{:S(2)}) collective-permute-start(f32[4,4,128]{2,1,0:T(4,128)S(1)} %get-tuple-element.81), channel_id=1, source_target_pairs={{0,1},{1,0},{2,3},{3,2},{4,5},{5,4},{6,7},{7,6},{8,9},{9,8},{10,11... | collective-permute-start | bytes 24584 | tf_op jit(solution)/shard_map/ppermute | solution.py:433
  166.8 0.8 collective-permute-done.21.refs_2_
  167.6 2.2 %shard_map.93.force = f32[8,8,128]{2,1,0:T(8,128)S(1)} custom-call(f32[16,8,128]{2,1,0:T(8,128)S(1)} %shard_map.77.refs_0_, f32[8,8,128]{2,1,0:T(8,128)S(1)} %get-tuple-element.80.refs_1_.own, f32[4,4,128]{2,1,0:T(4,128)S(1)} %collective-permute-done.21.refs_2_, f32[4,8,128]{2,1,0:T(8,128)S(1)} %get-tuple-element.82.refs_3_), custom_call_target="tpu_custom_call" | custom-call | flops 20000000 | bytes 200000 | tf_op jit(solution)/shard_map/pallas_call | solution.py:393
  170.0 10.9 %all_to_all.34.sums = f32[32,1,128]{2,1,0:T(1,128)S(1)} all-to-all(f32[32,1,128]{2,1,0:T(1,128)S(1)} %get-tuple-element.84), channel_id=1, replica_groups=mesh['image'=16,'space'=32] {'space'}, dimensions={0} | all-to-all | bytes 32768 | tf_op jit(solution)/shard_map/all_to_all | solution.py:418
  180.9 0.8 shard_map.95
  (33 shorter events, 1.4 us)
Async XLA Ops:
  2.1 13.3 %collective-permute-start = (f32[4,8,128]{2,1,0:T(8,128)}, f32[4,8,128]{2,1,0:T(8,128)S(1)}, u32[]{:S(2)}, u32[]{:S(2)}) collective-permute-start(f32[4,8,128]{2,1,0:T(8,128)} %get-tuple-element.46), channel_id=1, source_target_pairs={{0,1},{1,0},{2,3},{3,2},{4,5},{5,4},{6,7},{7,6},{8,9},{9,8},{10,11... | collective-permute-start | bytes 49160 | tf_op jit(solution)/shard_map/ppermute | solution.py:377
  10.9 5.3 %collective-permute-start.1 = (f32[4,8,128]{2,1,0:T(8,128)}, f32[4,8,128]{2,1,0:T(8,128)S(1)}, u32[]{:S(2)}, u32[]{:S(2)}) collective-permute-start(f32[4,8,128]{2,1,0:T(8,128)} %get-tuple-element.47), channel_id=1, source_target_pairs={{0,31},{1,2},{2,1},{3,4},{4,3},{5,6},{6,5},{7,8},{8,7},{9,10},{10,... | collective-permute-start | bytes 49160 | tf_op jit(solution)/shard_map/ppermute | solution.py:378
  12.8 6.3 %collective-permute-start.3 = (f32[8,4,128]{2,1,0:T(4,128)}, f32[8,4,128]{2,1,0:T(4,128)S(1)}, u32[]{:S(2)}, u32[]{:S(2)}) collective-permute-start(f32[8,4,128]{2,1,0:T(4,128)} %get-tuple-element.48), channel_id=1, source_target_pairs={{32,64},{64,32},{96,128},{128,96},{160,192},{192,160},{224,256},{2... | collective-permute-start | bytes 49160 | tf_op jit(solution)/shard_map/ppermute | solution.py:408
  13.5 5.6 %collective-permute-start.2 = (f32[8,4,128]{2,1,0:T(4,128)}, f32[8,4,128]{2,1,0:T(4,128)S(1)}, u32[]{:S(2)}, u32[]{:S(2)}) collective-permute-start(f32[8,4,128]{2,1,0:T(4,128)} %get-tuple-element.48), channel_id=1, source_target_pairs={{0,32},{32,0},{64,96},{96,64},{128,160},{160,128},{192,224},{224,1... | collective-permute-start | bytes 49160 | tf_op jit(solution)/shard_map/ppermute | solution.py:407
  16.2 0.8 copy-start.1
  16.9 2.2 %copy-start = (f32[2,3,1024]{2,0,1:T(2,128)S(1)}, f32[2,3,1024]{2,0,1:T(2,128)}, u32[]{:S(2)}) copy-start(f32[2,3,1024]{2,0,1:T(2,128)} %param.7) | copy-start | bytes 73732
  16.9 2.2 %copy-start.2 = (f32[8,8,128]{2,1,0:T(8,128)S(1)}, f32[8,8,128]{2,1,0:T(8,128)}, u32[]{:S(2)}) copy-start(f32[8,8,128]{2,1,0:T(8,128)} %get-tuple-element.45.own.old) | copy-start | bytes 98308
  19.9 19.4 %collective-permute-start.4 = (f32[4,24,128]{2,1,0:T(8,128)S(1)}, f32[4,24,128]{2,1,0:T(8,128)S(1)}, u32[]{:S(2)}, u32[]{:S(2)}) collective-permute-start(f32[4,24,128]{2,1,0:T(8,128)S(1)} %get-tuple-element.51), channel_id=1, source_target_pairs={{0,31},{1,2},{2,1},{3,4},{4,3},{5,6},{6,5},{7,8},{8,7},{9,10},{10,... | collective-permute-start | bytes 147464 | tf_op jit(solution)/shard_map/ppermute | solution.py:420
  23.7 15.6 %all-to-all-start = ((f32[32,1,128]{2,1,0:T(1,128)}), f32[32,1,128]{2,1,0:T(1,128)S(1)}, u32[]{:S(2)}, u32[]{:S(2)}) async-start(f32[32,1,128]{2,1,0:T(1,128)} %get-tuple-element.49), calls=%async_computation | async-start | bytes 32768 | tf_op jit(solution)/shard_map/all_to_all | solution.py:418
  39.5 14.8 %collective-permute-start.7 = (f32[8,4,128]{2,1,0:T(4,128)S(1)}, f32[8,4,128]{2,1,0:T(4,128)S(1)}, u32[]{:S(2)}, u32[]{:S(2)}) collective-permute-start(f32[8,4,128]{2,1,0:T(4,128)S(1)} %get-tuple-element.55), channel_id=1, source_target_pairs={{32,64},{64,32},{96,128},{128,96},{160,192},{192,160},{224,256},{2... | collective-permute-start | bytes 49160 | tf_op jit(solution)/shard_map/ppermute | solution.py:408
  40.2 14.2 %collective-permute-start.6 = (f32[8,4,128]{2,1,0:T(4,128)S(1)}, f32[8,4,128]{2,1,0:T(4,128)S(1)}, u32[]{:S(2)}, u32[]{:S(2)}) collective-permute-start(f32[8,4,128]{2,1,0:T(4,128)S(1)} %get-tuple-element.55), channel_id=1, source_target_pairs={{0,32},{32,0},{64,96},{96,64},{128,160},{160,128},{192,224},{224,1... | collective-permute-start | bytes 49160 | tf_op jit(solution)/shard_map/ppermute | solution.py:407
  48.1 4.1 %collective-permute-start.5 = (f32[4,4,128]{2,1,0:T(4,128)S(1)}, f32[4,4,128]{2,1,0:T(4,128)S(1)}, u32[]{:S(2)}, u32[]{:S(2)}) collective-permute-start(f32[4,4,128]{2,1,0:T(4,128)S(1)} %get-tuple-element.53), channel_id=1, source_target_pairs={{0,1},{1,0},{2,3},{3,2},{4,5},{5,4},{6,7},{7,6},{8,9},{9,8},{10,11... | collective-permute-start | bytes 24584 | tf_op jit(solution)/shard_map/ppermute | solution.py:433
  54.5 15.2 %collective-permute-start.8 = (f32[4,24,128]{2,1,0:T(8,128)S(1)}, f32[4,24,128]{2,1,0:T(8,128)S(1)}, u32[]{:S(2)}, u32[]{:S(2)}) collective-permute-start(f32[4,24,128]{2,1,0:T(8,128)S(1)} %get-tuple-element.58), channel_id=1, source_target_pairs={{0,31},{1,2},{2,1},{3,4},{4,3},{5,6},{6,5},{7,8},{8,7},{9,10},{10,... | collective-permute-start | bytes 147464 | tf_op jit(solution)/shard_map/ppermute | solution.py:420
  69.8 12.5 %collective-permute-start.11 = (f32[8,4,128]{2,1,0:T(4,128)S(1)}, f32[8,4,128]{2,1,0:T(4,128)S(1)}, u32[]{:S(2)}, u32[]{:S(2)}) collective-permute-start(f32[8,4,128]{2,1,0:T(4,128)S(1)} %get-tuple-element.62), channel_id=1, source_target_pairs={{32,64},{64,32},{96,128},{128,96},{160,192},{192,160},{224,256},{2... | collective-permute-start | bytes 49160 | tf_op jit(solution)/shard_map/ppermute | solution.py:408
  70.5 11.9 %collective-permute-start.10 = (f32[8,4,128]{2,1,0:T(4,128)S(1)}, f32[8,4,128]{2,1,0:T(4,128)S(1)}, u32[]{:S(2)}, u32[]{:S(2)}) collective-permute-start(f32[8,4,128]{2,1,0:T(4,128)S(1)} %get-tuple-element.62), channel_id=1, source_target_pairs={{0,32},{32,0},{64,96},{96,64},{128,160},{160,128},{192,224},{224,1... | collective-permute-start | bytes 49160 | tf_op jit(solution)/shard_map/ppermute | solution.py:407
  76.1 4.1 %collective-permute-start.9 = (f32[4,4,128]{2,1,0:T(4,128)S(1)}, f32[4,4,128]{2,1,0:T(4,128)S(1)}, u32[]{:S(2)}, u32[]{:S(2)}) collective-permute-start(f32[4,4,128]{2,1,0:T(4,128)S(1)} %get-tuple-element.60), channel_id=1, source_target_pairs={{0,1},{1,0},{2,3},{3,2},{4,5},{5,4},{6,7},{7,6},{8,9},{9,8},{10,11... | collective-permute-start | bytes 24584 | tf_op jit(solution)/shard_map/ppermute | solution.py:433
  82.5 15.2 %collective-permute-start.12 = (f32[4,24,128]{2,1,0:T(8,128)S(1)}, f32[4,24,128]{2,1,0:T(8,128)S(1)}, u32[]{:S(2)}, u32[]{:S(2)}) collective-permute-start(f32[4,24,128]{2,1,0:T(8,128)S(1)} %get-tuple-element.65), channel_id=1, source_target_pairs={{0,31},{1,2},{2,1},{3,4},{4,3},{5,6},{6,5},{7,8},{8,7},{9,10},{10,... | collective-permute-start | bytes 147464 | tf_op jit(solution)/shard_map/ppermute | solution.py:420
  97.9 15.2 %collective-permute-start.15 = (f32[8,4,128]{2,1,0:T(4,128)S(1)}, f32[8,4,128]{2,1,0:T(4,128)S(1)}, u32[]{:S(2)}, u32[]{:S(2)}) collective-permute-start(f32[8,4,128]{2,1,0:T(4,128)S(1)} %get-tuple-element.69), channel_id=1, source_target_pairs={{32,64},{64,32},{96,128},{128,96},{160,192},{192,160},{224,256},{2... | collective-permute-start | bytes 49160 | tf_op jit(solution)/shard_map/ppermute | solution.py:408
  98.6 14.5 %collective-permute-start.14 = (f32[8,4,128]{2,1,0:T(4,128)S(1)}, f32[8,4,128]{2,1,0:T(4,128)S(1)}, u32[]{:S(2)}, u32[]{:S(2)}) collective-permute-start(f32[8,4,128]{2,1,0:T(4,128)S(1)} %get-tuple-element.69), channel_id=1, source_target_pairs={{0,32},{32,0},{64,96},{96,64},{128,160},{160,128},{192,224},{224,1... | collective-permute-start | bytes 49160 | tf_op jit(solution)/shard_map/ppermute | solution.py:407
  106.8 4.1 %collective-permute-start.13 = (f32[4,4,128]{2,1,0:T(4,128)S(1)}, f32[4,4,128]{2,1,0:T(4,128)S(1)}, u32[]{:S(2)}, u32[]{:S(2)}) collective-permute-start(f32[4,4,128]{2,1,0:T(4,128)S(1)} %get-tuple-element.67), channel_id=1, source_target_pairs={{0,1},{1,0},{2,3},{3,2},{4,5},{5,4},{6,7},{7,6},{8,9},{9,8},{10,11... | collective-permute-start | bytes 24584 | tf_op jit(solution)/shard_map/ppermute | solution.py:433
  113.2 15.2 %collective-permute-start.16 = (f32[4,24,128]{2,1,0:T(8,128)S(1)}, f32[4,24,128]{2,1,0:T(8,128)S(1)}, u32[]{:S(2)}, u32[]{:S(2)}) collective-permute-start(f32[4,24,128]{2,1,0:T(8,128)S(1)} %get-tuple-element.72), channel_id=1, source_target_pairs={{0,31},{1,2},{2,1},{3,4},{4,3},{5,6},{6,5},{7,8},{8,7},{9,10},{10,... | collective-permute-start | bytes 147464 | tf_op jit(solution)/shard_map/ppermute | solution.py:420
  128.6 12.5 %collective-permute-start.19 = (f32[8,4,128]{2,1,0:T(4,128)S(1)}, f32[8,4,128]{2,1,0:T(4,128)S(1)}, u32[]{:S(2)}, u32[]{:S(2)}) collective-permute-start(f32[8,4,128]{2,1,0:T(4,128)S(1)} %get-tuple-element.76), channel_id=1, source_target_pairs={{32,64},{64,32},{96,128},{128,96},{160,192},{192,160},{224,256},{2... | collective-permute-start | bytes 49160 | tf_op jit(solution)/shard_map/ppermute | solution.py:408
  129.2 11.9 %collective-permute-start.18 = (f32[8,4,128]{2,1,0:T(4,128)S(1)}, f32[8,4,128]{2,1,0:T(4,128)S(1)}, u32[]{:S(2)}, u32[]{:S(2)}) collective-permute-start(f32[8,4,128]{2,1,0:T(4,128)S(1)} %get-tuple-element.76), channel_id=1, source_target_pairs={{0,32},{32,0},{64,96},{96,64},{128,160},{160,128},{192,224},{224,1... | collective-permute-start | bytes 49160 | tf_op jit(solution)/shard_map/ppermute | solution.py:407
  134.8 4.1 %collective-permute-start.17 = (f32[4,4,128]{2,1,0:T(4,128)S(1)}, f32[4,4,128]{2,1,0:T(4,128)S(1)}, u32[]{:S(2)}, u32[]{:S(2)}) collective-permute-start(f32[4,4,128]{2,1,0:T(4,128)S(1)} %get-tuple-element.74), channel_id=1, source_target_pairs={{0,1},{1,0},{2,3},{3,2},{4,5},{5,4},{6,7},{7,6},{8,9},{9,8},{10,11... | collective-permute-start | bytes 24584 | tf_op jit(solution)/shard_map/ppermute | solution.py:433
  141.3 15.2 %collective-permute-start.20 = (f32[4,24,128]{2,1,0:T(8,128)S(1)}, f32[4,24,128]{2,1,0:T(8,128)S(1)}, u32[]{:S(2)}, u32[]{:S(2)}) collective-permute-start(f32[4,24,128]{2,1,0:T(8,128)S(1)} %get-tuple-element.79), channel_id=1, source_target_pairs={{0,31},{1,2},{2,1},{3,4},{4,3},{5,6},{6,5},{7,8},{8,7},{9,10},{10,... | collective-permute-start | bytes 147464 | tf_op jit(solution)/shard_map/ppermute | solution.py:420
  156.6 13.2 %collective-permute-start.23 = (f32[8,4,128]{2,1,0:T(4,128)S(1)}, f32[8,4,128]{2,1,0:T(4,128)S(1)}, u32[]{:S(2)}, u32[]{:S(2)}) collective-permute-start(f32[8,4,128]{2,1,0:T(4,128)S(1)} %get-tuple-element.83), channel_id=1, source_target_pairs={{32,64},{64,32},{96,128},{128,96},{160,192},{192,160},{224,256},{2... | collective-permute-start | bytes 49160 | tf_op jit(solution)/shard_map/ppermute | solution.py:408
  157.3 12.5 %collective-permute-start.22 = (f32[8,4,128]{2,1,0:T(4,128)S(1)}, f32[8,4,128]{2,1,0:T(4,128)S(1)}, u32[]{:S(2)}, u32[]{:S(2)}) collective-permute-start(f32[8,4,128]{2,1,0:T(4,128)S(1)} %get-tuple-element.83), channel_id=1, source_target_pairs={{0,32},{32,0},{64,96},{96,64},{128,160},{160,128},{192,224},{224,1... | collective-permute-start | bytes 49160 | tf_op jit(solution)/shard_map/ppermute | solution.py:407
  163.5 4.1 %collective-permute-start.21 = (f32[4,4,128]{2,1,0:T(4,128)S(1)}, f32[4,4,128]{2,1,0:T(4,128)S(1)}, u32[]{:S(2)}, u32[]{:S(2)}) collective-permute-start(f32[4,4,128]{2,1,0:T(4,128)S(1)} %get-tuple-element.81), channel_id=1, source_target_pairs={{0,1},{1,0},{2,3},{3,2},{4,5},{5,4},{6,7},{7,6},{8,9},{9,8},{10,11... | collective-permute-start | bytes 24584 | tf_op jit(solution)/shard_map/ppermute | solution.py:433

commit v3 on v2

--- a/solution.py
+++ b/solution.py
@@ -273,7 +273,10 @@
         line = jnp.where(lane == n, value, line)
     sums[...] = jnp.broadcast_to(line[None], sums.shape)
     if far_out is not None:
-        far_out[...] = packed[pl.ds((1 - space_even()) * HALO, HALO)]
+        start = (1 - space_even()) * HALO
+        for c in range(HALO):
+            for n in range(3):
+                far_out[c, n] = packed[start + c, 8 * n : 8 * n + 4]
 
 
 def band_terms(sums, spring):
@@ -305,16 +308,17 @@
     even = space_even()
     _, _, _, ahead, behind = band_terms(sums, spring[0])
 
-    def shifted(state, g):
-        return state + step_size * (g[0:8] + ahead * g[8:16] + behind * g[16:24])
+    def shifted(state, f, forward, backward):
+        return state + step_size * (f + ahead * forward + behind * backward)
 
     for c in range(CELLS):
-        state = shifted(old[c], packed[c])
+        state = shifted(old[c], *[packed[c, 8 * n : 8 * n + 8] for n in range(3)])
         own[c] = state
         image_out[c] = state[0:4]
     near_out[...] = image_out[pl.ds(even * HALO, HALO)]
     for c in range(HALO):
-        far[c] = shifted(old_far[c], far_packed[c])
+        rim = [far_packed[c, n] for n in range(3)]
+        far[c] = jnp.concatenate([shifted(old_far[c, 0:4], *rim), old_far[c, 4:8]], axis=0)
 
 
 def final_kernel(spring, sums, packed, band, stats):
@@ -372,8 +376,8 @@
         scratch_shapes=[pltpu.VMEM(v.shape, v.dtype) for v in raw]
         + [pltpu.SemaphoreType.DMA((4,))],
         name="pack",
-        compiler_params=pltpu.CompilerParams(vmem_limit_bytes=62 << 20),
-    )(*raw)
+        compiler_params=pltpu.CompilerParams(vmem_limit_bytes=2 << 20),
+    )(*[pltpu.with_memory_space_constraint(v, pltpu.HBM) for v in raw])
     near = lax.ppermute(near, "space", space_a)
     far = lax.ppermute(far, "space", space_b)
     base = call(join_kernel, shape(WIDE, 8, SLOTS), 0, 3)(own, near, far)
@@ -411,7 +415,7 @@
         packed, sums, *far_packed = call(
             gaps_kernel,
             (shape(CELLS, 24, SLOTS), shape(parts, 1, SLOTS))
-            + (shape(HALO, 24, SLOTS),) * more,
+            + (shape(HALO, 3, 4, SLOTS),) * more,
             0,
             5,
         )(own, force, from_a, from_b, end_states)

time: 183 us -> 180 us (0.984)
  blocking collectives: 61.9 us -> 14 us
  starting transfers between devices: 87.9 us -> 119 us
  waiting for transfers between devices: 11.9 us -> 25.4 us
    all_to_all x5 -> x1, blocking collectives: 61.9 us -> 14 us  [body(): sums = lax.all_to_all(sums, 'space', 0, 0, tiled=True)]
    all_to_all x1 -> x5, starting transfers between devices: 7.72 us -> 33.3 us  [body(): sums = lax.all_to_all(sums, 'space', 0, 0, tiled=True)]
    ppermute x5, waiting for transfers between devices: 0.01 us -> 8.82 us  [body(): far_packed = lax.ppermute(far_packed[0], 'space', space_b)]
    all_to_all x1 -> x5, waiting for transfers between devices: 7.24 us -> 12.2 us  [body(): sums = lax.all_to_all(sums, 'space', 0, 0, tiled=True)]
    ppermute x5, starting transfers between devices: 13.6 us -> 17.7 us  [body(): far_packed = lax.ppermute(far_packed[0], 'space', space_b)]
    pallas_call x6, Pallas kernels: 1.44 us -> 3.87 us  [body(): call(gaps_kernel, (shape(CELLS, 24, SLOTS), shape(parts, 1, SLOTS)) + (sh...]
  transfers between devices with their start and end apart: 25 -> 29, of which waited for: 7 -> 16; matrix products, arithmetic and copies ran while one was open for 0% -> 0% of each run, Pallas kernels for 7% -> 7%
where the time goes in v3:
time: 180 us; the launch traced here: 179 us
  starting transfers between devices  119 us (66%)
  waiting for transfers between devices  25.4 us (14%)
  Pallas kernels  19.3 us (11%)
  blocking collectives  14 us (8%)
    ppermute x6, starting transfers between devices, body(): from_a = lax.ppermute(image_out, 'image', image_a)  36.5 us
    all_to_all x5, starting transfers between devices, body(): sums = lax.all_to_all(sums, 'space', 0, 0, tiled=True)  33.3 us
    ppermute x6, starting transfers between devices, body(): near = lax.ppermute(near, 'space', space_a)  25.3 us
    ppermute x5, starting transfers between devices, body(): far_packed = lax.ppermute(far_packed[0], 'space', space_b)  17.7 us
    all_to_all x1, blocking collectives, body(): sums = lax.all_to_all(sums, 'space', 0, 0, tiled=True)  14 us
    pallas_call x6, Pallas kernels, forces(): call(functools.partial(force_kernel, first), shape(CELLS, 8, SLOTS), 0, 1...  13 us
    all_to_all x5, waiting for transfers between devices, body(): sums = lax.all_to_all(sums, 'space', 0, 0, tiled=True)  12.2 us
    ppermute x5, waiting for transfers between devices, body(): far_packed = lax.ppermute(far_packed[0], 'space', space_b)  8.82 us
  transfers between devices with their start and end apart: 29, of which 16 were waited for; matrix products, arithmetic and copies ran while one was open for 0% of the time, Pallas kernels for 7%

profile of v3, /device:TPU:1, one launch (start us, length us, event | category | flops | bytes accessed | tf_op | source)
XLA Modules:
  0.0 179.2 jit_solution(62026403311693483)
XLA Ops:
  0.6 0.9 pack.1
  1.5 8.7 %collective-permute-start = (f32[4,8,128]{2,1,0:T(8,128)S(1)}, f32[4,8,128]{2,1,0:T(8,128)S(1)}, u32[]{:S(2)}, u32[]{:S(2)}) collective-permute-start(f32[4,8,128]{2,1,0:T(8,128)S(1)} %get-tuple-element.46), channel_id=1, source_target_pairs={{0,1},{1,0},{2,3},{3,2},{4,5},{5,4},{6,7},{7,6},{8,9},{9,8},{10,11... | collective-permute-start | bytes 49160 | tf_op jit(solution)/shard_map/ppermute | solution.py:381
  10.3 1.9 %collective-permute-start.1 = (f32[4,8,128]{2,1,0:T(8,128)S(1)}, f32[4,8,128]{2,1,0:T(8,128)S(1)}, u32[]{:S(2)}, u32[]{:S(2)}) collective-permute-start(f32[4,8,128]{2,1,0:T(8,128)S(1)} %get-tuple-element.47), channel_id=1, source_target_pairs={{0,31},{1,2},{2,1},{3,4},{4,3},{5,6},{6,5},{7,8},{8,7},{9,10},{10,... | collective-permute-start | bytes 49160 | tf_op jit(solution)/shard_map/ppermute | solution.py:382
  12.9 1.9 %collective-permute-start.2 = (f32[8,4,128]{2,1,0:T(4,128)S(1)}, f32[8,4,128]{2,1,0:T(4,128)S(1)}, u32[]{:S(2)}, u32[]{:S(2)}) collective-permute-start(f32[8,4,128]{2,1,0:T(4,128)S(1)} %get-tuple-element.48), channel_id=1, source_target_pairs={{0,32},{32,0},{64,96},{96,64},{128,160},{160,128},{192,224},{224,1... | collective-permute-start | bytes 49160 | tf_op jit(solution)/shard_map/ppermute | solution.py:411
  15.3 2.2 %shard_map.78.force = f32[8,8,128]{2,1,0:T(8,128)S(1)} custom-call(f32[16,8,128]{2,1,0:T(8,128)S(1)} %shard_map.77.refs_0_), custom_call_target="tpu_custom_call" | custom-call | flops 20000000 | bytes 200000 | tf_op jit(solution)/shard_map/pallas_call | solution.py:397
  18.3 8.1 %all-to-all-start = ((f32[32,1,128]{2,1,0:T(1,128)}), f32[32,1,128]{2,1,0:T(1,128)S(1)}, u32[]{:S(2)}, u32[]{:S(2)}) async-start(f32[32,1,128]{2,1,0:T(1,128)} %get-tuple-element.49), calls=%async_computation | async-start | bytes 32768 | tf_op jit(solution)/shard_map/all_to_all | solution.py:422
  26.4 3.5 %collective-permute-start.4 = (f32[4,3,4,128]{3,2,1,0:T(4,128)S(1)}, f32[4,3,4,128]{3,2,1,0:T(4,128)S(1)}, u32[]{:S(2)}, u32[]{:S(2)}) collective-permute-start(f32[4,3,4,128]{3,2,1,0:T(4,128)S(1)} %get-tuple-element.51), channel_id=1, source_target_pairs={{0,31},{1,2},{2,1},{3,4},{4,3},{5,6},{6,5},{7,8},{8,7},{9,10},{10,... | collective-permute-start | bytes 73736 | tf_op jit(solution)/shard_map/ppermute | solution.py:424
  30.6 1.2 collective-permute-done.4.far_packed
  31.9 2.4 %all-to-all-done.sums = f32[32,1,128]{2,1,0:T(1,128)S(1)} async-done(((f32[32,1,128]{2,1,0:T(1,128)}), f32[32,1,128]{2,1,0:T(1,128)S(1)}, u32[]{:S(2)}, u32[]{:S(2)}) %all-to-all-start) | async-done | bytes 16416 | tf_op jit(solution)/shard_map/all_to_all | solution.py:422
  35.1 7.9 %collective-permute-start.6 = (f32[8,4,128]{2,1,0:T(4,128)S(1)}, f32[8,4,128]{2,1,0:T(4,128)S(1)}, u32[]{:S(2)}, u32[]{:S(2)}) collective-permute-start(f32[8,4,128]{2,1,0:T(4,128)S(1)} %get-tuple-element.55), channel_id=1, source_target_pairs={{0,32},{32,0},{64,96},{96,64},{128,160},{160,128},{192,224},{224,1... | collective-permute-start | bytes 49160 | tf_op jit(solution)/shard_map/ppermute | solution.py:411
  43.0 3.3 %collective-permute-start.5 = (f32[4,4,128]{2,1,0:T(4,128)S(1)}, f32[4,4,128]{2,1,0:T(4,128)S(1)}, u32[]{:S(2)}, u32[]{:S(2)}) collective-permute-start(f32[4,4,128]{2,1,0:T(4,128)S(1)} %get-tuple-element.53), channel_id=1, source_target_pairs={{0,1},{1,0},{2,3},{3,2},{4,5},{5,4},{6,7},{7,6},{8,9},{9,8},{10,11... | collective-permute-start | bytes 24584 | tf_op jit(solution)/shard_map/ppermute | solution.py:437
  46.3 0.8 collective-permute-done.5.refs_2_
  47.1 2.2 %shard_map.81.force = f32[8,8,128]{2,1,0:T(8,128)S(1)} custom-call(f32[16,8,128]{2,1,0:T(8,128)S(1)} %shard_map.77.refs_0_, f32[8,8,128]{2,1,0:T(8,128)S(1)} %get-tuple-element.52.refs_1_.own.old, f32[4,4,128]{2,1,0:T(4,128)S(1)} %collective-permute-done.5.refs_2_, f32[4,8,128]{2,1,0:T(8,128)S(1)} %get-tuple-element.54.refs_3_.old_far), custom_call_target="tpu_custom_call" | custom-call | flops 20000000 | bytes 200000 | tf_op jit(solution)/shard_map/pallas_call | solution.py:397
  49.3 0.7 shard_map.82
  50.1 6.3 %all-to-all-start.1 = ((f32[32,1,128]{2,1,0:T(1,128)}), f32[32,1,128]{2,1,0:T(1,128)S(1)}, u32[]{:S(2)}, u32[]{:S(2)}) async-start(f32[32,1,128]{2,1,0:T(1,128)} %get-tuple-element.56), calls=%async_computation.1 | async-start | bytes 32768 | tf_op jit(solution)/shard_map/all_to_all | solution.py:422
  56.4 3.5 %collective-permute-start.8 = (f32[4,3,4,128]{3,2,1,0:T(4,128)S(1)}, f32[4,3,4,128]{3,2,1,0:T(4,128)S(1)}, u32[]{:S(2)}, u32[]{:S(2)}) collective-permute-start(f32[4,3,4,128]{3,2,1,0:T(4,128)S(1)} %get-tuple-element.58), channel_id=1, source_target_pairs={{0,31},{1,2},{2,1},{3,4},{4,3},{5,6},{6,5},{7,8},{8,7},{9,10},{10,... | collective-permute-start | bytes 73736 | tf_op jit(solution)/shard_map/ppermute | solution.py:424
  59.9 1.9 %collective-permute-done.8.far_packed = f32[4,3,4,128]{3,2,1,0:T(4,128)S(1)} collective-permute-done((f32[4,3,4,128]{3,2,1,0:T(4,128)S(1)}, f32[4,3,4,128]{3,2,1,0:T(4,128)S(1)}, u32[]{:S(2)}, u32[]{:S(2)}) %collective-permute-start.8) | collective-permute-done | bytes 24608 | tf_op jit(solution)/shard_map/ppermute | solution.py:424
  61.8 2.4 %all-to-all-done.1.sums = f32[32,1,128]{2,1,0:T(1,128)S(1)} async-done(((f32[32,1,128]{2,1,0:T(1,128)}), f32[32,1,128]{2,1,0:T(1,128)S(1)}, u32[]{:S(2)}, u32[]{:S(2)}) %all-to-all-start.1) | async-done | bytes 16416 | tf_op jit(solution)/shard_map/all_to_all | solution.py:422
  65.1 5.6 %collective-permute-start.10 = (f32[8,4,128]{2,1,0:T(4,128)S(1)}, f32[8,4,128]{2,1,0:T(4,128)S(1)}, u32[]{:S(2)}, u32[]{:S(2)}) collective-permute-start(f32[8,4,128]{2,1,0:T(4,128)S(1)} %get-tuple-element.62), channel_id=1, source_target_pairs={{0,32},{32,0},{64,96},{96,64},{128,160},{160,128},{192,224},{224,1... | collective-permute-start | bytes 49160 | tf_op jit(solution)/shard_map/ppermute | solution.py:411
  70.7 3.3 %collective-permute-start.9 = (f32[4,4,128]{2,1,0:T(4,128)S(1)}, f32[4,4,128]{2,1,0:T(4,128)S(1)}, u32[]{:S(2)}, u32[]{:S(2)}) collective-permute-start(f32[4,4,128]{2,1,0:T(4,128)S(1)} %get-tuple-element.60), channel_id=1, source_target_pairs={{0,1},{1,0},{2,3},{3,2},{4,5},{5,4},{6,7},{7,6},{8,9},{9,8},{10,11... | collective-permute-start | bytes 24584 | tf_op jit(solution)/shard_map/ppermute | solution.py:437
  74.0 0.8 collective-permute-done.9.refs_2_
  74.8 2.2 %shard_map.84.force = f32[8,8,128]{2,1,0:T(8,128)S(1)} custom-call(f32[16,8,128]{2,1,0:T(8,128)S(1)} %shard_map.77.refs_0_, f32[8,8,128]{2,1,0:T(8,128)S(1)} %get-tuple-element.59.refs_1_.own.old, f32[4,4,128]{2,1,0:T(4,128)S(1)} %collective-permute-done.9.refs_2_, f32[4,8,128]{2,1,0:T(8,128)S(1)} %get-tuple-element.61.refs_3_.old_far), custom_call_target="tpu_custom_call" | custom-call | flops 20000000 | bytes 200000 | tf_op jit(solution)/shard_map/pallas_call | solution.py:397
  77.7 6.3 %all-to-all-start.2 = ((f32[32,1,128]{2,1,0:T(1,128)}), f32[32,1,128]{2,1,0:T(1,128)S(1)}, u32[]{:S(2)}, u32[]{:S(2)}) async-start(f32[32,1,128]{2,1,0:T(1,128)} %get-tuple-element.63), calls=%async_computation.2 | async-start | bytes 32768 | tf_op jit(solution)/shard_map/all_to_all | solution.py:422
  84.0 3.5 %collective-permute-start.12 = (f32[4,3,4,128]{3,2,1,0:T(4,128)S(1)}, f32[4,3,4,128]{3,2,1,0:T(4,128)S(1)}, u32[]{:S(2)}, u32[]{:S(2)}) collective-permute-start(f32[4,3,4,128]{3,2,1,0:T(4,128)S(1)} %get-tuple-element.65), channel_id=1, source_target_pairs={{0,31},{1,2},{2,1},{3,4},{4,3},{5,6},{6,5},{7,8},{8,7},{9,10},{10,... | collective-permute-start | bytes 73736 | tf_op jit(solution)/shard_map/ppermute | solution.py:424
  87.6 1.9 %collective-permute-done.12.far_packed = f32[4,3,4,128]{3,2,1,0:T(4,128)S(1)} collective-permute-done((f32[4,3,4,128]{3,2,1,0:T(4,128)S(1)}, f32[4,3,4,128]{3,2,1,0:T(4,128)S(1)}, u32[]{:S(2)}, u32[]{:S(2)}) %collective-permute-start.12) | collective-permute-done | bytes 24608 | tf_op jit(solution)/shard_map/ppermute | solution.py:424
  89.5 2.4 %all-to-all-done.2.sums = f32[32,1,128]{2,1,0:T(1,128)S(1)} async-done(((f32[32,1,128]{2,1,0:T(1,128)}), f32[32,1,128]{2,1,0:T(1,128)S(1)}, u32[]{:S(2)}, u32[]{:S(2)}) %all-to-all-start.2) | async-done | bytes 16416 | tf_op jit(solution)/shard_map/all_to_all | solution.py:422
  92.8 8.2 %collective-permute-start.14 = (f32[8,4,128]{2,1,0:T(4,128)S(1)}, f32[8,4,128]{2,1,0:T(4,128)S(1)}, u32[]{:S(2)}, u32[]{:S(2)}) collective-permute-start(f32[8,4,128]{2,1,0:T(4,128)S(1)} %get-tuple-element.69), channel_id=1, source_target_pairs={{0,32},{32,0},{64,96},{96,64},{128,160},{160,128},{192,224},{224,1... | collective-permute-start | bytes 49160 | tf_op jit(solution)/shard_map/ppermute | solution.py:411
  101.0 3.3 %collective-permute-start.13 = (f32[4,4,128]{2,1,0:T(4,128)S(1)}, f32[4,4,128]{2,1,0:T(4,128)S(1)}, u32[]{:S(2)}, u32[]{:S(2)}) collective-permute-start(f32[4,4,128]{2,1,0:T(4,128)S(1)} %get-tuple-element.67), channel_id=1, source_target_pairs={{0,1},{1,0},{2,3},{3,2},{4,5},{5,4},{6,7},{7,6},{8,9},{9,8},{10,11... | collective-permute-start | bytes 24584 | tf_op jit(solution)/shard_map/ppermute | solution.py:437
  104.3 0.8 collective-permute-done.13.refs_2_
  105.1 2.2 %shard_map.87.force = f32[8,8,128]{2,1,0:T(8,128)S(1)} custom-call(f32[16,8,128]{2,1,0:T(8,128)S(1)} %shard_map.77.refs_0_, f32[8,8,128]{2,1,0:T(8,128)S(1)} %get-tuple-element.66.refs_1_.own.old, f32[4,4,128]{2,1,0:T(4,128)S(1)} %collective-permute-done.13.refs_2_, f32[4,8,128]{2,1,0:T(8,128)S(1)} %get-tuple-element.68.refs_3_.old_far), custom_call_target="tpu_custom_call" | custom-call | flops 20000000 | bytes 200000 | tf_op jit(solution)/shard_map/pallas_call | solution.py:397
  107.3 0.7 shard_map.88
  108.0 6.3 %all-to-all-start.3 = ((f32[32,1,128]{2,1,0:T(1,128)}), f32[32,1,128]{2,1,0:T(1,128)S(1)}, u32[]{:S(2)}, u32[]{:S(2)}) async-start(f32[32,1,128]{2,1,0:T(1,128)} %get-tuple-element.70), calls=%async_computation.3 | async-start | bytes 32768 | tf_op jit(solution)/shard_map/all_to_all | solution.py:422
  114.3 3.5 %collective-permute-start.16 = (f32[4,3,4,128]{3,2,1,0:T(4,128)S(1)}, f32[4,3,4,128]{3,2,1,0:T(4,128)S(1)}, u32[]{:S(2)}, u32[]{:S(2)}) collective-permute-start(f32[4,3,4,128]{3,2,1,0:T(4,128)S(1)} %get-tuple-element.72), channel_id=1, source_target_pairs={{0,31},{1,2},{2,1},{3,4},{4,3},{5,6},{6,5},{7,8},{8,7},{9,10},{10,... | collective-permute-start | bytes 73736 | tf_op jit(solution)/shard_map/ppermute | solution.py:424
  117.9 1.9 %collective-permute-done.16.far_packed = f32[4,3,4,128]{3,2,1,0:T(4,128)S(1)} collective-permute-done((f32[4,3,4,128]{3,2,1,0:T(4,128)S(1)}, f32[4,3,4,128]{3,2,1,0:T(4,128)S(1)}, u32[]{:S(2)}, u32[]{:S(2)}) %collective-permute-start.16) | collective-permute-done | bytes 24608 | tf_op jit(solution)/shard_map/ppermute | solution.py:424
  119.8 2.4 %all-to-all-done.3.sums = f32[32,1,128]{2,1,0:T(1,128)S(1)} async-done(((f32[32,1,128]{2,1,0:T(1,128)}), f32[32,1,128]{2,1,0:T(1,128)S(1)}, u32[]{:S(2)}, u32[]{:S(2)}) %all-to-all-start.3) | async-done | bytes 16416 | tf_op jit(solution)/shard_map/all_to_all | solution.py:422
  123.0 6.5 %collective-permute-start.18 = (f32[8,4,128]{2,1,0:T(4,128)S(1)}, f32[8,4,128]{2,1,0:T(4,128)S(1)}, u32[]{:S(2)}, u32[]{:S(2)}) collective-permute-start(f32[8,4,128]{2,1,0:T(4,128)S(1)} %get-tuple-element.76), channel_id=1, source_target_pairs={{0,32},{32,0},{64,96},{96,64},{128,160},{160,128},{192,224},{224,1... | collective-permute-start | bytes 49160 | tf_op jit(solution)/shard_map/ppermute | solution.py:411
  129.6 3.5 %collective-permute-start.17 = (f32[4,4,128]{2,1,0:T(4,128)S(1)}, f32[4,4,128]{2,1,0:T(4,128)S(1)}, u32[]{:S(2)}, u32[]{:S(2)}) collective-permute-start(f32[4,4,128]{2,1,0:T(4,128)S(1)} %get-tuple-element.74), channel_id=1, source_target_pairs={{0,1},{1,0},{2,3},{3,2},{4,5},{5,4},{6,7},{7,6},{8,9},{9,8},{10,11... | collective-permute-start | bytes 24584 | tf_op jit(solution)/shard_map/ppermute | solution.py:437
  133.7 2.2 %shard_map.90.force = f32[8,8,128]{2,1,0:T(8,128)S(1)} custom-call(f32[16,8,128]{2,1,0:T(8,128)S(1)} %shard_map.77.refs_0_, f32[8,8,128]{2,1,0:T(8,128)S(1)} %get-tuple-element.73.refs_1_.own.old, f32[4,4,128]{2,1,0:T(4,128)S(1)} %collective-permute-done.17.refs_2_, f32[4,8,128]{2,1,0:T(8,128)S(1)} %get-tuple-element.75.refs_3_.old_far), custom_call_target="tpu_custom_call" | custom-call | flops 20000000 | bytes 200000 | tf_op jit(solution)/shard_map/pallas_call | solution.py:397
  136.6 6.3 %all-to-all-start.4 = ((f32[32,1,128]{2,1,0:T(1,128)}), f32[32,1,128]{2,1,0:T(1,128)S(1)}, u32[]{:S(2)}, u32[]{:S(2)}) async-start(f32[32,1,128]{2,1,0:T(1,128)} %get-tuple-element.77), calls=%async_computation.4 | async-start | bytes 32768 | tf_op jit(solution)/shard_map/all_to_all | solution.py:422
  142.9 3.5 %collective-permute-start.20 = (f32[4,3,4,128]{3,2,1,0:T(4,128)S(1)}, f32[4,3,4,128]{3,2,1,0:T(4,128)S(1)}, u32[]{:S(2)}, u32[]{:S(2)}) collective-permute-start(f32[4,3,4,128]{3,2,1,0:T(4,128)S(1)} %get-tuple-element.79), channel_id=1, source_target_pairs={{0,31},{1,2},{2,1},{3,4},{4,3},{5,6},{6,5},{7,8},{8,7},{9,10},{10,... | collective-permute-start | bytes 73736 | tf_op jit(solution)/shard_map/ppermute | solution.py:424
  146.5 1.9 %collective-permute-done.20.far_packed = f32[4,3,4,128]{3,2,1,0:T(4,128)S(1)} collective-permute-done((f32[4,3,4,128]{3,2,1,0:T(4,128)S(1)}, f32[4,3,4,128]{3,2,1,0:T(4,128)S(1)}, u32[]{:S(2)}, u32[]{:S(2)}) %collective-permute-start.20) | collective-permute-done | bytes 24608 | tf_op jit(solution)/shard_map/ppermute | solution.py:424
  148.4 2.4 %all-to-all-done.4.sums = f32[32,1,128]{2,1,0:T(1,128)S(1)} async-done(((f32[32,1,128]{2,1,0:T(1,128)}), f32[32,1,128]{2,1,0:T(1,128)S(1)}, u32[]{:S(2)}, u32[]{:S(2)}) %all-to-all-start.4) | async-done | bytes 16416 | tf_op jit(solution)/shard_map/all_to_all | solution.py:422
  151.6 6.4 %collective-permute-start.22 = (f32[8,4,128]{2,1,0:T(4,128)S(1)}, f32[8,4,128]{2,1,0:T(4,128)S(1)}, u32[]{:S(2)}, u32[]{:S(2)}) collective-permute-start(f32[8,4,128]{2,1,0:T(4,128)S(1)} %get-tuple-element.83), channel_id=1, source_target_pairs={{0,32},{32,0},{64,96},{96,64},{128,160},{160,128},{192,224},{224,1... | collective-permute-start | bytes 49160 | tf_op jit(solution)/shard_map/ppermute | solution.py:411
  158.0 3.3 %collective-permute-start.21 = (f32[4,4,128]{2,1,0:T(4,128)S(1)}, f32[4,4,128]{2,1,0:T(4,128)S(1)}, u32[]{:S(2)}, u32[]{:S(2)}) collective-permute-start(f32[4,4,128]{2,1,0:T(4,128)S(1)} %get-tuple-element.81), channel_id=1, source_target_pairs={{0,1},{1,0},{2,3},{3,2},{4,5},{5,4},{6,7},{7,6},{8,9},{9,8},{10,11... | collective-permute-start | bytes 24584 | tf_op jit(solution)/shard_map/ppermute | solution.py:437
  161.3 0.8 collective-permute-done.21.refs_2_
  162.1 2.2 %shard_map.93.force = f32[8,8,128]{2,1,0:T(8,128)S(1)} custom-call(f32[16,8,128]{2,1,0:T(8,128)S(1)} %shard_map.77.refs_0_, f32[8,8,128]{2,1,0:T(8,128)S(1)} %get-tuple-element.80.refs_1_.own, f32[4,4,128]{2,1,0:T(4,128)S(1)} %collective-permute-done.21.refs_2_, f32[4,8,128]{2,1,0:T(8,128)S(1)} %get-tuple-element.82.refs_3_), custom_call_target="tpu_custom_call" | custom-call | flops 20000000 | bytes 200000 | tf_op jit(solution)/shard_map/pallas_call | solution.py:397
  164.5 14.0 %all_to_all.30.sums = f32[32,1,128]{2,1,0:T(1,128)S(1)} all-to-all(f32[32,1,128]{2,1,0:T(1,128)S(1)} %get-tuple-element.84), channel_id=1, replica_groups=mesh['image'=16,'space'=32] {'space'}, dimensions={0} | all-to-all | bytes 32768 | tf_op jit(solution)/shard_map/all_to_all | solution.py:422
  178.4 0.8 shard_map.95
  (33 shorter events, 8.3 us)
Async XLA Ops:
  1.5 13.3 %collective-permute-start = (f32[4,8,128]{2,1,0:T(8,128)S(1)}, f32[4,8,128]{2,1,0:T(8,128)S(1)}, u32[]{:S(2)}, u32[]{:S(2)}) collective-permute-start(f32[4,8,128]{2,1,0:T(8,128)S(1)} %get-tuple-element.46), channel_id=1, source_target_pairs={{0,1},{1,0},{2,3},{3,2},{4,5},{5,4},{6,7},{7,6},{8,9},{9,8},{10,11... | collective-permute-start | bytes 49160 | tf_op jit(solution)/shard_map/ppermute | solution.py:381
  10.3 5.1 %collective-permute-start.1 = (f32[4,8,128]{2,1,0:T(8,128)S(1)}, f32[4,8,128]{2,1,0:T(8,128)S(1)}, u32[]{:S(2)}, u32[]{:S(2)}) collective-permute-start(f32[4,8,128]{2,1,0:T(8,128)S(1)} %get-tuple-element.47), channel_id=1, source_target_pairs={{0,31},{1,2},{2,1},{3,4},{4,3},{5,6},{6,5},{7,8},{8,7},{9,10},{10,... | collective-permute-start | bytes 49160 | tf_op jit(solution)/shard_map/ppermute | solution.py:382
  12.2 5.3 %collective-permute-start.3 = (f32[8,4,128]{2,1,0:T(4,128)S(1)}, f32[8,4,128]{2,1,0:T(4,128)S(1)}, u32[]{:S(2)}, u32[]{:S(2)}) collective-permute-start(f32[8,4,128]{2,1,0:T(4,128)S(1)} %get-tuple-element.48), channel_id=1, source_target_pairs={{32,64},{64,32},{96,128},{128,96},{160,192},{192,160},{224,256},{2... | collective-permute-start | bytes 49160 | tf_op jit(solution)/shard_map/ppermute | solution.py:412
  12.9 4.7 %collective-permute-start.2 = (f32[8,4,128]{2,1,0:T(4,128)S(1)}, f32[8,4,128]{2,1,0:T(4,128)S(1)}, u32[]{:S(2)}, u32[]{:S(2)}) collective-permute-start(f32[8,4,128]{2,1,0:T(4,128)S(1)} %get-tuple-element.48), channel_id=1, source_target_pairs={{0,32},{32,0},{64,96},{96,64},{128,160},{160,128},{192,224},{224,1... | collective-permute-start | bytes 49160 | tf_op jit(solution)/shard_map/ppermute | solution.py:411
  15.3 2.2 %copy-start = (f32[2,3,1024]{2,0,1:T(2,128)S(1)}, f32[2,3,1024]{2,0,1:T(2,128)}, u32[]{:S(2)}) copy-start(f32[2,3,1024]{2,0,1:T(2,128)} %param.7) | copy-start | bytes 73732
  18.3 16.0 %all-to-all-start = ((f32[32,1,128]{2,1,0:T(1,128)}), f32[32,1,128]{2,1,0:T(1,128)S(1)}, u32[]{:S(2)}, u32[]{:S(2)}) async-start(f32[32,1,128]{2,1,0:T(1,128)} %get-tuple-element.49), calls=%async_computation | async-start | bytes 32768 | tf_op jit(solution)/shard_map/all_to_all | solution.py:422
  26.4 5.4 %collective-permute-start.4 = (f32[4,3,4,128]{3,2,1,0:T(4,128)S(1)}, f32[4,3,4,128]{3,2,1,0:T(4,128)S(1)}, u32[]{:S(2)}, u32[]{:S(2)}) collective-permute-start(f32[4,3,4,128]{3,2,1,0:T(4,128)S(1)} %get-tuple-element.51), channel_id=1, source_target_pairs={{0,31},{1,2},{2,1},{3,4},{4,3},{5,6},{6,5},{7,8},{8,7},{9,10},{10,... | collective-permute-start | bytes 73736 | tf_op jit(solution)/shard_map/ppermute | solution.py:424
  34.5 14.8 %collective-permute-start.7 = (f32[8,4,128]{2,1,0:T(4,128)S(1)}, f32[8,4,128]{2,1,0:T(4,128)S(1)}, u32[]{:S(2)}, u32[]{:S(2)}) collective-permute-start(f32[8,4,128]{2,1,0:T(4,128)S(1)} %get-tuple-element.55), channel_id=1, source_target_pairs={{32,64},{64,32},{96,128},{128,96},{160,192},{192,160},{224,256},{2... | collective-permute-start | bytes 49160 | tf_op jit(solution)/shard_map/ppermute | solution.py:412
  35.1 14.2 %collective-permute-start.6 = (f32[8,4,128]{2,1,0:T(4,128)S(1)}, f32[8,4,128]{2,1,0:T(4,128)S(1)}, u32[]{:S(2)}, u32[]{:S(2)}) collective-permute-start(f32[8,4,128]{2,1,0:T(4,128)S(1)} %get-tuple-element.55), channel_id=1, source_target_pairs={{0,32},{32,0},{64,96},{96,64},{128,160},{160,128},{192,224},{224,1... | collective-permute-start | bytes 49160 | tf_op jit(solution)/shard_map/ppermute | solution.py:411
  43.0 4.1 %collective-permute-start.5 = (f32[4,4,128]{2,1,0:T(4,128)S(1)}, f32[4,4,128]{2,1,0:T(4,128)S(1)}, u32[]{:S(2)}, u32[]{:S(2)}) collective-permute-start(f32[4,4,128]{2,1,0:T(4,128)S(1)} %get-tuple-element.53), channel_id=1, source_target_pairs={{0,1},{1,0},{2,3},{3,2},{4,5},{5,4},{6,7},{7,6},{8,9},{9,8},{10,11... | collective-permute-start | bytes 24584 | tf_op jit(solution)/shard_map/ppermute | solution.py:437
  50.1 14.2 %all-to-all-start.1 = ((f32[32,1,128]{2,1,0:T(1,128)}), f32[32,1,128]{2,1,0:T(1,128)S(1)}, u32[]{:S(2)}, u32[]{:S(2)}) async-start(f32[32,1,128]{2,1,0:T(1,128)} %get-tuple-element.56), calls=%async_computation.1 | async-start | bytes 32768 | tf_op jit(solution)/shard_map/all_to_all | solution.py:422
  56.4 5.4 %collective-permute-start.8 = (f32[4,3,4,128]{3,2,1,0:T(4,128)S(1)}, f32[4,3,4,128]{3,2,1,0:T(4,128)S(1)}, u32[]{:S(2)}, u32[]{:S(2)}) collective-permute-start(f32[4,3,4,128]{3,2,1,0:T(4,128)S(1)} %get-tuple-element.58), channel_id=1, source_target_pairs={{0,31},{1,2},{2,1},{3,4},{4,3},{5,6},{6,5},{7,8},{8,7},{9,10},{10,... | collective-permute-start | bytes 73736 | tf_op jit(solution)/shard_map/ppermute | solution.py:424
  64.4 12.5 %collective-permute-start.11 = (f32[8,4,128]{2,1,0:T(4,128)S(1)}, f32[8,4,128]{2,1,0:T(4,128)S(1)}, u32[]{:S(2)}, u32[]{:S(2)}) collective-permute-start(f32[8,4,128]{2,1,0:T(4,128)S(1)} %get-tuple-element.62), channel_id=1, source_target_pairs={{32,64},{64,32},{96,128},{128,96},{160,192},{192,160},{224,256},{2... | collective-permute-start | bytes 49160 | tf_op jit(solution)/shard_map/ppermute | solution.py:412
  65.1 11.9 %collective-permute-start.10 = (f32[8,4,128]{2,1,0:T(4,128)S(1)}, f32[8,4,128]{2,1,0:T(4,128)S(1)}, u32[]{:S(2)}, u32[]{:S(2)}) collective-permute-start(f32[8,4,128]{2,1,0:T(4,128)S(1)} %get-tuple-element.62), channel_id=1, source_target_pairs={{0,32},{32,0},{64,96},{96,64},{128,160},{160,128},{192,224},{224,1... | collective-permute-start | bytes 49160 | tf_op jit(solution)/shard_map/ppermute | solution.py:411
  70.7 4.1 %collective-permute-start.9 = (f32[4,4,128]{2,1,0:T(4,128)S(1)}, f32[4,4,128]{2,1,0:T(4,128)S(1)}, u32[]{:S(2)}, u32[]{:S(2)}) collective-permute-start(f32[4,4,128]{2,1,0:T(4,128)S(1)} %get-tuple-element.60), channel_id=1, source_target_pairs={{0,1},{1,0},{2,3},{3,2},{4,5},{5,4},{6,7},{7,6},{8,9},{9,8},{10,11... | collective-permute-start | bytes 24584 | tf_op jit(solution)/shard_map/ppermute | solution.py:437
  77.7 14.2 %all-to-all-start.2 = ((f32[32,1,128]{2,1,0:T(1,128)}), f32[32,1,128]{2,1,0:T(1,128)S(1)}, u32[]{:S(2)}, u32[]{:S(2)}) async-start(f32[32,1,128]{2,1,0:T(1,128)} %get-tuple-element.63), calls=%async_computation.2 | async-start | bytes 32768 | tf_op jit(solution)/shard_map/all_to_all | solution.py:422
  84.0 5.4 %collective-permute-start.12 = (f32[4,3,4,128]{3,2,1,0:T(4,128)S(1)}, f32[4,3,4,128]{3,2,1,0:T(4,128)S(1)}, u32[]{:S(2)}, u32[]{:S(2)}) collective-permute-start(f32[4,3,4,128]{3,2,1,0:T(4,128)S(1)} %get-tuple-element.65), channel_id=1, source_target_pairs={{0,31},{1,2},{2,1},{3,4},{4,3},{5,6},{6,5},{7,8},{8,7},{9,10},{10,... | collective-permute-start | bytes 73736 | tf_op jit(solution)/shard_map/ppermute | solution.py:424
  92.1 15.2 %collective-permute-start.15 = (f32[8,4,128]{2,1,0:T(4,128)S(1)}, f32[8,4,128]{2,1,0:T(4,128)S(1)}, u32[]{:S(2)}, u32[]{:S(2)}) collective-permute-start(f32[8,4,128]{2,1,0:T(4,128)S(1)} %get-tuple-element.69), channel_id=1, source_target_pairs={{32,64},{64,32},{96,128},{128,96},{160,192},{192,160},{224,256},{2... | collective-permute-start | bytes 49160 | tf_op jit(solution)/shard_map/ppermute | solution.py:412
  92.8 14.5 %collective-permute-start.14 = (f32[8,4,128]{2,1,0:T(4,128)S(1)}, f32[8,4,128]{2,1,0:T(4,128)S(1)}, u32[]{:S(2)}, u32[]{:S(2)}) collective-permute-start(f32[8,4,128]{2,1,0:T(4,128)S(1)} %get-tuple-element.69), channel_id=1, source_target_pairs={{0,32},{32,0},{64,96},{96,64},{128,160},{160,128},{192,224},{224,1... | collective-permute-start | bytes 49160 | tf_op jit(solution)/shard_map/ppermute | solution.py:411
  101.0 4.1 %collective-permute-start.13 = (f32[4,4,128]{2,1,0:T(4,128)S(1)}, f32[4,4,128]{2,1,0:T(4,128)S(1)}, u32[]{:S(2)}, u32[]{:S(2)}) collective-permute-start(f32[4,4,128]{2,1,0:T(4,128)S(1)} %get-tuple-element.67), channel_id=1, source_target_pairs={{0,1},{1,0},{2,3},{3,2},{4,5},{5,4},{6,7},{7,6},{8,9},{9,8},{10,11... | collective-permute-start | bytes 24584 | tf_op jit(solution)/shard_map/ppermute | solution.py:437
  108.0 14.2 %all-to-all-start.3 = ((f32[32,1,128]{2,1,0:T(1,128)}), f32[32,1,128]{2,1,0:T(1,128)S(1)}, u32[]{:S(2)}, u32[]{:S(2)}) async-start(f32[32,1,128]{2,1,0:T(1,128)} %get-tuple-element.70), calls=%async_computation.3 | async-start | bytes 32768 | tf_op jit(solution)/shard_map/all_to_all | solution.py:422
  114.3 5.4 %collective-permute-start.16 = (f32[4,3,4,128]{3,2,1,0:T(4,128)S(1)}, f32[4,3,4,128]{3,2,1,0:T(4,128)S(1)}, u32[]{:S(2)}, u32[]{:S(2)}) collective-permute-start(f32[4,3,4,128]{3,2,1,0:T(4,128)S(1)} %get-tuple-element.72), channel_id=1, source_target_pairs={{0,31},{1,2},{2,1},{3,4},{4,3},{5,6},{6,5},{7,8},{8,7},{9,10},{10,... | collective-permute-start | bytes 73736 | tf_op jit(solution)/shard_map/ppermute | solution.py:424
  122.4 13.5 %collective-permute-start.19 = (f32[8,4,128]{2,1,0:T(4,128)S(1)}, f32[8,4,128]{2,1,0:T(4,128)S(1)}, u32[]{:S(2)}, u32[]{:S(2)}) collective-permute-start(f32[8,4,128]{2,1,0:T(4,128)S(1)} %get-tuple-element.76), channel_id=1, source_target_pairs={{32,64},{64,32},{96,128},{128,96},{160,192},{192,160},{224,256},{2... | collective-permute-start | bytes 49160 | tf_op jit(solution)/shard_map/ppermute | solution.py:412
  123.0 12.8 %collective-permute-start.18 = (f32[8,4,128]{2,1,0:T(4,128)S(1)}, f32[8,4,128]{2,1,0:T(4,128)S(1)}, u32[]{:S(2)}, u32[]{:S(2)}) collective-permute-start(f32[8,4,128]{2,1,0:T(4,128)S(1)} %get-tuple-element.76), channel_id=1, source_target_pairs={{0,32},{32,0},{64,96},{96,64},{128,160},{160,128},{192,224},{224,1... | collective-permute-start | bytes 49160 | tf_op jit(solution)/shard_map/ppermute | solution.py:411
  129.6 4.1 %collective-permute-start.17 = (f32[4,4,128]{2,1,0:T(4,128)S(1)}, f32[4,4,128]{2,1,0:T(4,128)S(1)}, u32[]{:S(2)}, u32[]{:S(2)}) collective-permute-start(f32[4,4,128]{2,1,0:T(4,128)S(1)} %get-tuple-element.74), channel_id=1, source_target_pairs={{0,1},{1,0},{2,3},{3,2},{4,5},{5,4},{6,7},{7,6},{8,9},{9,8},{10,11... | collective-permute-start | bytes 24584 | tf_op jit(solution)/shard_map/ppermute | solution.py:437
  136.6 14.2 %all-to-all-start.4 = ((f32[32,1,128]{2,1,0:T(1,128)}), f32[32,1,128]{2,1,0:T(1,128)S(1)}, u32[]{:S(2)}, u32[]{:S(2)}) async-start(f32[32,1,128]{2,1,0:T(1,128)} %get-tuple-element.77), calls=%async_computation.4 | async-start | bytes 32768 | tf_op jit(solution)/shard_map/all_to_all | solution.py:422
  142.9 5.4 %collective-permute-start.20 = (f32[4,3,4,128]{3,2,1,0:T(4,128)S(1)}, f32[4,3,4,128]{3,2,1,0:T(4,128)S(1)}, u32[]{:S(2)}, u32[]{:S(2)}) collective-permute-start(f32[4,3,4,128]{3,2,1,0:T(4,128)S(1)} %get-tuple-element.79), channel_id=1, source_target_pairs={{0,31},{1,2},{2,1},{3,4},{4,3},{5,6},{6,5},{7,8},{8,7},{9,10},{10,... | collective-permute-start | bytes 73736 | tf_op jit(solution)/shard_map/ppermute | solution.py:424
  151.0 13.3 %collective-permute-start.23 = (f32[8,4,128]{2,1,0:T(4,128)S(1)}, f32[8,4,128]{2,1,0:T(4,128)S(1)}, u32[]{:S(2)}, u32[]{:S(2)}) collective-permute-start(f32[8,4,128]{2,1,0:T(4,128)S(1)} %get-tuple-element.83), channel_id=1, source_target_pairs={{32,64},{64,32},{96,128},{128,96},{160,192},{192,160},{224,256},{2... | collective-permute-start | bytes 49160 | tf_op jit(solution)/shard_map/ppermute | solution.py:412
  151.6 12.7 %collective-permute-start.22 = (f32[8,4,128]{2,1,0:T(4,128)S(1)}, f32[8,4,128]{2,1,0:T(4,128)S(1)}, u32[]{:S(2)}, u32[]{:S(2)}) collective-permute-start(f32[8,4,128]{2,1,0:T(4,128)S(1)} %get-tuple-element.83), channel_id=1, source_target_pairs={{0,32},{32,0},{64,96},{96,64},{128,160},{160,128},{192,224},{224,1... | collective-permute-start | bytes 49160 | tf_op jit(solution)/shard_map/ppermute | solution.py:411
  158.0 4.1 %collective-permute-start.21 = (f32[4,4,128]{2,1,0:T(4,128)S(1)}, f32[4,4,128]{2,1,0:T(4,128)S(1)}, u32[]{:S(2)}, u32[]{:S(2)}) collective-permute-start(f32[4,4,128]{2,1,0:T(4,128)S(1)} %get-tuple-element.81), channel_id=1, source_target_pairs={{0,1},{1,0},{2,3},{3,2},{4,5},{5,4},{6,7},{7,6},{8,9},{9,8},{10,11... | collective-permute-start | bytes 24584 | tf_op jit(solution)/shard_map/ppermute | solution.py:437

commit v4 on v3

--- a/solution.py
+++ b/solution.py
@@ -109,14 +109,12 @@
     if first:
         wide, force, left, right, sums, slopes, tiles, density = refs
     else:
-        base, own, near, far, force = refs[:5]
-        left, right, sums, slopes, tiles, density, wide = refs[5:]
+        own, near, far, force = refs[:4]
+        left, right, sums, slopes, tiles, density, wide = refs[4:]
         even = space_even()
         wide[pl.ds(HALO, CELLS)] = own[...]
+        wide[pl.ds(even * (HALO + CELLS), HALO)] = near[...]
         wide[pl.ds((1 - even) * (HALO + CELLS), HALO)] = far[...]
-        for c in range(HALO):
-            at = even * (HALO + CELLS) + c
-            wide[at] = jnp.concatenate([near[c], base[at, 4:8]], axis=0)
     row = rows_iota()
     site = centred_sites()
 
@@ -238,7 +236,7 @@
     lax.fori_loop(0, CELLS // 2, force_pair, 0, unroll=4)
 
 
-def gaps_kernel(own, force, from_a, from_b, ends, packed, sums, far_out=None):
+def gaps_kernel(own, force, from_a, from_b, ends, packed, sums, near_out=None, far_out=None):
     image = lax.axis_index("image")
     image_even = 1 - (image & 1)
     edge = (image == 0) | (image == lax.axis_size("image") - 1)
@@ -273,10 +271,11 @@
         line = jnp.where(lane == n, value, line)
     sums[...] = jnp.broadcast_to(line[None], sums.shape)
     if far_out is not None:
-        start = (1 - space_even()) * HALO
+        start = space_even() * HALO
         for c in range(HALO):
             for n in range(3):
-                far_out[c, n] = packed[start + c, 8 * n : 8 * n + 4]
+                near_out[c, n] = packed[start + c, 8 * n : 8 * n + 4]
+                far_out[c, n] = packed[HALO - start + c, 8 * n : 8 * n + 4]
 
 
 def band_terms(sums, spring):
@@ -304,8 +303,8 @@
     return parallel, spring_term, cosine, pull / length_ahead, pull / length_behind
 
 
-def moved_kernel(spring, sums, old, old_far, packed, far_packed, own, far, image_out, near_out):
-    even = space_even()
+def moved_kernel(spring, sums, old, old_near, old_far, packed, near_packed, far_packed, *outs):
+    own, near, far, image_out = outs
     _, _, _, ahead, behind = band_terms(sums, spring[0])
 
     def shifted(state, f, forward, backward):
@@ -315,10 +314,11 @@
         state = shifted(old[c], *[packed[c, 8 * n : 8 * n + 8] for n in range(3)])
         own[c] = state
         image_out[c] = state[0:4]
-    near_out[...] = image_out[pl.ds(even * HALO, HALO)]
-    for c in range(HALO):
-        rim = [far_packed[c, n] for n in range(3)]
-        far[c] = jnp.concatenate([shifted(old_far[c, 0:4], *rim), old_far[c, 4:8]], axis=0)
+    for halo, old_halo, halo_packed in ((near, old_near, near_packed), (far, old_far, far_packed)):
+        for c in range(HALO):
+            rim = [halo_packed[c, n] for n in range(3)]
+            state = old_halo[c]
+            halo[c] = jnp.concatenate([shifted(state[0:4], *rim), state[4:8]], axis=0)
 
 
 def final_kernel(spring, sums, packed, band, stats):
@@ -398,7 +398,7 @@
             functools.partial(force_kernel, first),
             shape(CELLS, 8, SLOTS),
             0,
-            1 if first else 4,
+            1 if first else 3,
             room=12,
             scratch_shapes=scratch,
             cost_estimate=pl.CostEstimate(
@@ -412,30 +412,30 @@
         from_b = lax.ppermute(image_out, "image", image_b)
         force = forces(*operands)
         more = iteration < ITERATIONS - 1
-        packed, sums, *far_packed = call(
+        packed, sums, *rims = call(
             gaps_kernel,
             (shape(CELLS, 24, SLOTS), shape(parts, 1, SLOTS))
-            + (shape(HALO, 3, 4, SLOTS),) * more,
+            + (shape(HALO, 3, 4, SLOTS),) * (2 * more),
             0,
             5,
         )(own, force, from_a, from_b, end_states)
         sums = lax.all_to_all(sums, "space", 0, 0, tiled=True)
         if more:
-            far_packed = lax.ppermute(far_packed[0], "space", space_b)
+            near_packed = lax.ppermute(rims[0], "space", space_a)
+            far_packed = lax.ppermute(rims[1], "space", space_b)
         if more:
-            own, far, image_out, near = call(
+            own, near, far, image_out = call(
                 moved_kernel,
                 (
                     shape(CELLS, 8, SLOTS),
                     shape(HALO, 8, SLOTS),
+                    shape(HALO, 8, SLOTS),
                     shape(CELLS, 4, SLOTS),
-                    shape(HALO, 4, SLOTS),
                 ),
                 1,
-                5,
-            )(spring_const, sums, own, far, packed, far_packed)
-            near = lax.ppermute(near, "space", space_a)
-            operands = (base, own, near, far)
+                7,
+            )(spring_const, sums, own, near, far, packed, near_packed, far_packed)
+            operands = (own, near, far)
     band, stats = call(final_kernel, (shape(3, 1, CELLS * SLOTS), shape(1, 3)), 1, 2)(
         spring_const, sums, packed
     )

time: 180 us -> 178 us (0.989)
  the two profiles are of different devices: /device:TPU:1 before, /device:TPU:134 now
where the time goes in v4:
time: 178 us; the launch traced here: 177 us
  starting transfers between devices  125 us (70%)
  Pallas kernels  19.3 us (11%)
  waiting for transfers between devices  15.8 us (9%)
  blocking collectives  15.5 us (9%)
    all_to_all x5, starting transfers between devices, body(): sums = lax.all_to_all(sums, 'space', 0, 0, tiled=True)  33.6 us
    ppermute x6, starting transfers between devices, body(): from_b = lax.ppermute(image_out, 'image', image_b)  30.8 us
    ppermute x5, starting transfers between devices, body(): far_packed = lax.ppermute(rims[1], 'space', space_b)  28.7 us
    all_to_all x1, blocking collectives, body(): sums = lax.all_to_all(sums, 'space', 0, 0, tiled=True)  15.5 us
    pallas_call x6, Pallas kernels, forces(): call(functools.partial(force_kernel, first), shape(CELLS, 8, SLOTS), 0, 1...  13 us
    ppermute x6, starting transfers between devices, body(): from_a = lax.ppermute(image_out, 'image', image_a)  11.7 us
    ppermute x5, starting transfers between devices, body(): near_packed = lax.ppermute(rims[0], 'space', space_a)  10.9 us
    ppermute x1, starting transfers between devices, body(): far = lax.ppermute(far, 'space', space_b)  7.29 us
  transfers between devices with their start and end apart: 29, of which 15 were waited for; matrix products, arithmetic and copies ran while one was open for 0% of the time, Pallas kernels for 7%

profile of v4, /device:TPU:134, one launch (start us, length us, event | category | flops | bytes accessed | tf_op | source)
XLA Modules:
  0.0 177.2 jit_solution(16149942536299604648)
XLA Ops:
  0.6 0.9 pack.1
  1.5 1.9 %collective-permute-start = (f32[4,8,128]{2,1,0:T(8,128)S(1)}, f32[4,8,128]{2,1,0:T(8,128)S(1)}, u32[]{:S(2)}, u32[]{:S(2)}) collective-permute-start(f32[4,8,128]{2,1,0:T(8,128)S(1)} %get-tuple-element.51), channel_id=1, source_target_pairs={{0,1},{1,0},{2,3},{3,2},{4,5},{5,4},{6,7},{7,6},{8,9},{9,8},{10,11... | collective-permute-start | bytes 49160 | tf_op jit(solution)/shard_map/ppermute | solution.py:381
  3.4 7.3 %collective-permute-start.1 = (f32[4,8,128]{2,1,0:T(8,128)S(1)}, f32[4,8,128]{2,1,0:T(8,128)S(1)}, u32[]{:S(2)}, u32[]{:S(2)}) collective-permute-start(f32[4,8,128]{2,1,0:T(8,128)S(1)} %get-tuple-element.52), channel_id=1, source_target_pairs={{0,31},{1,2},{2,1},{3,4},{4,3},{5,6},{6,5},{7,8},{8,7},{9,10},{10,... | collective-permute-start | bytes 49160 | tf_op jit(solution)/shard_map/ppermute | solution.py:382
  10.7 6.3 %collective-permute-start.3 = (f32[8,4,128]{2,1,0:T(4,128)S(1)}, f32[8,4,128]{2,1,0:T(4,128)S(1)}, u32[]{:S(2)}, u32[]{:S(2)}) collective-permute-start(f32[8,4,128]{2,1,0:T(4,128)S(1)} %get-tuple-element.53), channel_id=1, source_target_pairs={{32,64},{64,32},{96,128},{128,96},{160,192},{192,160},{224,256},{2... | collective-permute-start | bytes 49160 | tf_op jit(solution)/shard_map/ppermute | solution.py:412
  17.1 1.9 %collective-permute-start.2 = (f32[8,4,128]{2,1,0:T(4,128)S(1)}, f32[8,4,128]{2,1,0:T(4,128)S(1)}, u32[]{:S(2)}, u32[]{:S(2)}) collective-permute-start(f32[8,4,128]{2,1,0:T(4,128)S(1)} %get-tuple-element.53), channel_id=1, source_target_pairs={{0,32},{32,0},{64,96},{96,64},{128,160},{160,128},{192,224},{224,1... | collective-permute-start | bytes 49160 | tf_op jit(solution)/shard_map/ppermute | solution.py:411
  19.0 2.2 %shard_map.78.force = f32[8,8,128]{2,1,0:T(8,128)S(1)} custom-call(f32[16,8,128]{2,1,0:T(8,128)S(1)} %shard_map.77.refs_0_), custom_call_target="tpu_custom_call" | custom-call | flops 20000000 | bytes 200000 | tf_op jit(solution)/shard_map/pallas_call | solution.py:397
  21.2 1.5 collective-permute-done.2.from_a
  23.4 4.6 %all-to-all-start = ((f32[32,1,128]{2,1,0:T(1,128)}), f32[32,1,128]{2,1,0:T(1,128)S(1)}, u32[]{:S(2)}, u32[]{:S(2)}) async-start(f32[32,1,128]{2,1,0:T(1,128)} %get-tuple-element.54), calls=%async_computation | async-start | bytes 32768 | tf_op jit(solution)/shard_map/all_to_all | solution.py:422
  28.0 2.2 %collective-permute-start.4 = (f32[4,3,4,128]{3,2,1,0:T(4,128)S(1)}, f32[4,3,4,128]{3,2,1,0:T(4,128)S(1)}, u32[]{:S(2)}, u32[]{:S(2)}) collective-permute-start(f32[4,3,4,128]{3,2,1,0:T(4,128)S(1)} %get-tuple-element.56), channel_id=1, source_target_pairs={{0,1},{1,0},{2,3},{3,2},{4,5},{5,4},{6,7},{7,6},{8,9},{9,8},{10,11... | collective-permute-start | bytes 73736 | tf_op jit(solution)/shard_map/ppermute | solution.py:424
  30.2 5.7 %collective-permute-start.5 = (f32[4,3,4,128]{3,2,1,0:T(4,128)S(1)}, f32[4,3,4,128]{3,2,1,0:T(4,128)S(1)}, u32[]{:S(2)}, u32[]{:S(2)}) collective-permute-start(f32[4,3,4,128]{3,2,1,0:T(4,128)S(1)} %get-tuple-element.57), channel_id=1, source_target_pairs={{0,31},{1,2},{2,1},{3,4},{4,3},{5,6},{6,5},{7,8},{8,7},{9,10},{10,... | collective-permute-start | bytes 73736 | tf_op jit(solution)/shard_map/ppermute | solution.py:425
  36.6 0.9 collective-permute-done.5.far_packed
  37.6 4.4 %collective-permute-start.7 = (f32[8,4,128]{2,1,0:T(4,128)S(1)}, f32[8,4,128]{2,1,0:T(4,128)S(1)}, u32[]{:S(2)}, u32[]{:S(2)}) collective-permute-start(f32[8,4,128]{2,1,0:T(4,128)S(1)} %get-tuple-element.61), channel_id=1, source_target_pairs={{32,64},{64,32},{96,128},{128,96},{160,192},{192,160},{224,256},{2... | collective-permute-start | bytes 49160 | tf_op jit(solution)/shard_map/ppermute | solution.py:412
  42.0 1.9 %collective-permute-start.6 = (f32[8,4,128]{2,1,0:T(4,128)S(1)}, f32[8,4,128]{2,1,0:T(4,128)S(1)}, u32[]{:S(2)}, u32[]{:S(2)}) collective-permute-start(f32[8,4,128]{2,1,0:T(4,128)S(1)} %get-tuple-element.61), channel_id=1, source_target_pairs={{0,32},{32,0},{64,96},{96,64},{128,160},{160,128},{192,224},{224,1... | collective-permute-start | bytes 49160 | tf_op jit(solution)/shard_map/ppermute | solution.py:411
  44.0 2.2 %shard_map.81.force = f32[8,8,128]{2,1,0:T(8,128)S(1)} custom-call(f32[8,8,128]{2,1,0:T(8,128)S(1)} %get-tuple-element.58.refs_0_.own.old, f32[4,8,128]{2,1,0:T(8,128)S(1)} %get-tuple-element.59.refs_1_.old_near, f32[4,8,128]{2,1,0:T(8,128)S(1)} %get-tuple-element.60.refs_2_.old_far), custom_call_target="tpu_custom_call" | custom-call | flops 20000000 | bytes 200000 | tf_op jit(solution)/shard_map/pallas_call | solution.py:397
  46.1 1.4 collective-permute-done.7.from_b
  48.4 7.3 %all-to-all-start.1 = ((f32[32,1,128]{2,1,0:T(1,128)}), f32[32,1,128]{2,1,0:T(1,128)S(1)}, u32[]{:S(2)}, u32[]{:S(2)}) async-start(f32[32,1,128]{2,1,0:T(1,128)} %get-tuple-element.62), calls=%async_computation.1 | async-start | bytes 32768 | tf_op jit(solution)/shard_map/all_to_all | solution.py:422
  55.7 2.2 %collective-permute-start.8 = (f32[4,3,4,128]{3,2,1,0:T(4,128)S(1)}, f32[4,3,4,128]{3,2,1,0:T(4,128)S(1)}, u32[]{:S(2)}, u32[]{:S(2)}) collective-permute-start(f32[4,3,4,128]{3,2,1,0:T(4,128)S(1)} %get-tuple-element.64), channel_id=1, source_target_pairs={{0,1},{1,0},{2,3},{3,2},{4,5},{5,4},{6,7},{7,6},{8,9},{9,8},{10,11... | collective-permute-start | bytes 73736 | tf_op jit(solution)/shard_map/ppermute | solution.py:424
  57.9 5.7 %collective-permute-start.9 = (f32[4,3,4,128]{3,2,1,0:T(4,128)S(1)}, f32[4,3,4,128]{3,2,1,0:T(4,128)S(1)}, u32[]{:S(2)}, u32[]{:S(2)}) collective-permute-start(f32[4,3,4,128]{3,2,1,0:T(4,128)S(1)} %get-tuple-element.65), channel_id=1, source_target_pairs={{0,31},{1,2},{2,1},{3,4},{4,3},{5,6},{6,5},{7,8},{8,7},{9,10},{10,... | collective-permute-start | bytes 73736 | tf_op jit(solution)/shard_map/ppermute | solution.py:425
  63.6 1.5 collective-permute-done.9.far_packed
  65.3 5.7 %collective-permute-start.11 = (f32[8,4,128]{2,1,0:T(4,128)S(1)}, f32[8,4,128]{2,1,0:T(4,128)S(1)}, u32[]{:S(2)}, u32[]{:S(2)}) collective-permute-start(f32[8,4,128]{2,1,0:T(4,128)S(1)} %get-tuple-element.69), channel_id=1, source_target_pairs={{32,64},{64,32},{96,128},{128,96},{160,192},{192,160},{224,256},{2... | collective-permute-start | bytes 49160 | tf_op jit(solution)/shard_map/ppermute | solution.py:412
  71.0 1.9 %collective-permute-start.10 = (f32[8,4,128]{2,1,0:T(4,128)S(1)}, f32[8,4,128]{2,1,0:T(4,128)S(1)}, u32[]{:S(2)}, u32[]{:S(2)}) collective-permute-start(f32[8,4,128]{2,1,0:T(4,128)S(1)} %get-tuple-element.69), channel_id=1, source_target_pairs={{0,32},{32,0},{64,96},{96,64},{128,160},{160,128},{192,224},{224,1... | collective-permute-start | bytes 49160 | tf_op jit(solution)/shard_map/ppermute | solution.py:411
  72.9 2.2 %shard_map.84.force = f32[8,8,128]{2,1,0:T(8,128)S(1)} custom-call(f32[8,8,128]{2,1,0:T(8,128)S(1)} %get-tuple-element.66.refs_0_.own.old, f32[4,8,128]{2,1,0:T(8,128)S(1)} %get-tuple-element.67.refs_1_.old_near, f32[4,8,128]{2,1,0:T(8,128)S(1)} %get-tuple-element.68.refs_2_.old_far), custom_call_target="tpu_custom_call" | custom-call | flops 20000000 | bytes 200000 | tf_op jit(solution)/shard_map/pallas_call | solution.py:397
  75.1 1.5 collective-permute-done.10.from_a
  77.4 7.3 %all-to-all-start.2 = ((f32[32,1,128]{2,1,0:T(1,128)}), f32[32,1,128]{2,1,0:T(1,128)S(1)}, u32[]{:S(2)}, u32[]{:S(2)}) async-start(f32[32,1,128]{2,1,0:T(1,128)} %get-tuple-element.70), calls=%async_computation.2 | async-start | bytes 32768 | tf_op jit(solution)/shard_map/all_to_all | solution.py:422
  84.6 2.2 %collective-permute-start.12 = (f32[4,3,4,128]{3,2,1,0:T(4,128)S(1)}, f32[4,3,4,128]{3,2,1,0:T(4,128)S(1)}, u32[]{:S(2)}, u32[]{:S(2)}) collective-permute-start(f32[4,3,4,128]{3,2,1,0:T(4,128)S(1)} %get-tuple-element.72), channel_id=1, source_target_pairs={{0,1},{1,0},{2,3},{3,2},{4,5},{5,4},{6,7},{7,6},{8,9},{9,8},{10,11... | collective-permute-start | bytes 73736 | tf_op jit(solution)/shard_map/ppermute | solution.py:424
  86.8 5.7 %collective-permute-start.13 = (f32[4,3,4,128]{3,2,1,0:T(4,128)S(1)}, f32[4,3,4,128]{3,2,1,0:T(4,128)S(1)}, u32[]{:S(2)}, u32[]{:S(2)}) collective-permute-start(f32[4,3,4,128]{3,2,1,0:T(4,128)S(1)} %get-tuple-element.73), channel_id=1, source_target_pairs={{0,31},{1,2},{2,1},{3,4},{4,3},{5,6},{6,5},{7,8},{8,7},{9,10},{10,... | collective-permute-start | bytes 73736 | tf_op jit(solution)/shard_map/ppermute | solution.py:425
  92.6 1.5 collective-permute-done.13.far_packed
  94.2 4.4 %collective-permute-start.15 = (f32[8,4,128]{2,1,0:T(4,128)S(1)}, f32[8,4,128]{2,1,0:T(4,128)S(1)}, u32[]{:S(2)}, u32[]{:S(2)}) collective-permute-start(f32[8,4,128]{2,1,0:T(4,128)S(1)} %get-tuple-element.77), channel_id=1, source_target_pairs={{32,64},{64,32},{96,128},{128,96},{160,192},{192,160},{224,256},{2... | collective-permute-start | bytes 49160 | tf_op jit(solution)/shard_map/ppermute | solution.py:412
  98.6 1.9 %collective-permute-start.14 = (f32[8,4,128]{2,1,0:T(4,128)S(1)}, f32[8,4,128]{2,1,0:T(4,128)S(1)}, u32[]{:S(2)}, u32[]{:S(2)}) collective-permute-start(f32[8,4,128]{2,1,0:T(4,128)S(1)} %get-tuple-element.77), channel_id=1, source_target_pairs={{0,32},{32,0},{64,96},{96,64},{128,160},{160,128},{192,224},{224,1... | collective-permute-start | bytes 49160 | tf_op jit(solution)/shard_map/ppermute | solution.py:411
  100.6 2.2 %shard_map.87.force = f32[8,8,128]{2,1,0:T(8,128)S(1)} custom-call(f32[8,8,128]{2,1,0:T(8,128)S(1)} %get-tuple-element.74.refs_0_.own.old, f32[4,8,128]{2,1,0:T(8,128)S(1)} %get-tuple-element.75.refs_1_.old_near, f32[4,8,128]{2,1,0:T(8,128)S(1)} %get-tuple-element.76.refs_2_.old_far), custom_call_target="tpu_custom_call" | custom-call | flops 20000000 | bytes 200000 | tf_op jit(solution)/shard_map/pallas_call | solution.py:397
  102.7 1.4 collective-permute-done.15.from_b
  105.0 7.3 %all-to-all-start.3 = ((f32[32,1,128]{2,1,0:T(1,128)}), f32[32,1,128]{2,1,0:T(1,128)S(1)}, u32[]{:S(2)}, u32[]{:S(2)}) async-start(f32[32,1,128]{2,1,0:T(1,128)} %get-tuple-element.78), calls=%async_computation.3 | async-start | bytes 32768 | tf_op jit(solution)/shard_map/all_to_all | solution.py:422
  112.3 2.2 %collective-permute-start.16 = (f32[4,3,4,128]{3,2,1,0:T(4,128)S(1)}, f32[4,3,4,128]{3,2,1,0:T(4,128)S(1)}, u32[]{:S(2)}, u32[]{:S(2)}) collective-permute-start(f32[4,3,4,128]{3,2,1,0:T(4,128)S(1)} %get-tuple-element.80), channel_id=1, source_target_pairs={{0,1},{1,0},{2,3},{3,2},{4,5},{5,4},{6,7},{7,6},{8,9},{9,8},{10,11... | collective-permute-start | bytes 73736 | tf_op jit(solution)/shard_map/ppermute | solution.py:424
  114.5 5.7 %collective-permute-start.17 = (f32[4,3,4,128]{3,2,1,0:T(4,128)S(1)}, f32[4,3,4,128]{3,2,1,0:T(4,128)S(1)}, u32[]{:S(2)}, u32[]{:S(2)}) collective-permute-start(f32[4,3,4,128]{3,2,1,0:T(4,128)S(1)} %get-tuple-element.81), channel_id=1, source_target_pairs={{0,31},{1,2},{2,1},{3,4},{4,3},{5,6},{6,5},{7,8},{8,7},{9,10},{10,... | collective-permute-start | bytes 73736 | tf_op jit(solution)/shard_map/ppermute | solution.py:425
  120.2 1.5 collective-permute-done.17.far_packed
  121.9 5.7 %collective-permute-start.19 = (f32[8,4,128]{2,1,0:T(4,128)S(1)}, f32[8,4,128]{2,1,0:T(4,128)S(1)}, u32[]{:S(2)}, u32[]{:S(2)}) collective-permute-start(f32[8,4,128]{2,1,0:T(4,128)S(1)} %get-tuple-element.85), channel_id=1, source_target_pairs={{32,64},{64,32},{96,128},{128,96},{160,192},{192,160},{224,256},{2... | collective-permute-start | bytes 49160 | tf_op jit(solution)/shard_map/ppermute | solution.py:412
  127.6 2.1 %collective-permute-start.18 = (f32[8,4,128]{2,1,0:T(4,128)S(1)}, f32[8,4,128]{2,1,0:T(4,128)S(1)}, u32[]{:S(2)}, u32[]{:S(2)}) collective-permute-start(f32[8,4,128]{2,1,0:T(4,128)S(1)} %get-tuple-element.85), channel_id=1, source_target_pairs={{0,32},{32,0},{64,96},{96,64},{128,160},{160,128},{192,224},{224,1... | collective-permute-start | bytes 49160 | tf_op jit(solution)/shard_map/ppermute | solution.py:411
  129.7 2.2 %shard_map.90.force = f32[8,8,128]{2,1,0:T(8,128)S(1)} custom-call(f32[8,8,128]{2,1,0:T(8,128)S(1)} %get-tuple-element.82.refs_0_.own.old, f32[4,8,128]{2,1,0:T(8,128)S(1)} %get-tuple-element.83.refs_1_.old_near, f32[4,8,128]{2,1,0:T(8,128)S(1)} %get-tuple-element.84.refs_2_.old_far), custom_call_target="tpu_custom_call" | custom-call | flops 20000000 | bytes 200000 | tf_op jit(solution)/shard_map/pallas_call | solution.py:397
  131.9 1.3 collective-permute-done.18.from_a
  134.0 7.3 %all-to-all-start.4 = ((f32[32,1,128]{2,1,0:T(1,128)}), f32[32,1,128]{2,1,0:T(1,128)S(1)}, u32[]{:S(2)}, u32[]{:S(2)}) async-start(f32[32,1,128]{2,1,0:T(1,128)} %get-tuple-element.86), calls=%async_computation.4 | async-start | bytes 32768 | tf_op jit(solution)/shard_map/all_to_all | solution.py:422
  141.2 2.2 %collective-permute-start.20 = (f32[4,3,4,128]{3,2,1,0:T(4,128)S(1)}, f32[4,3,4,128]{3,2,1,0:T(4,128)S(1)}, u32[]{:S(2)}, u32[]{:S(2)}) collective-permute-start(f32[4,3,4,128]{3,2,1,0:T(4,128)S(1)} %get-tuple-element.88), channel_id=1, source_target_pairs={{0,1},{1,0},{2,3},{3,2},{4,5},{5,4},{6,7},{7,6},{8,9},{9,8},{10,11... | collective-permute-start | bytes 73736 | tf_op jit(solution)/shard_map/ppermute | solution.py:424
  143.4 5.7 %collective-permute-start.21 = (f32[4,3,4,128]{3,2,1,0:T(4,128)S(1)}, f32[4,3,4,128]{3,2,1,0:T(4,128)S(1)}, u32[]{:S(2)}, u32[]{:S(2)}) collective-permute-start(f32[4,3,4,128]{3,2,1,0:T(4,128)S(1)} %get-tuple-element.89), channel_id=1, source_target_pairs={{0,31},{1,2},{2,1},{3,4},{4,3},{5,6},{6,5},{7,8},{8,7},{9,10},{10,... | collective-permute-start | bytes 73736 | tf_op jit(solution)/shard_map/ppermute | solution.py:425
  149.2 1.5 collective-permute-done.21.far_packed
  150.8 4.4 %collective-permute-start.23 = (f32[8,4,128]{2,1,0:T(4,128)S(1)}, f32[8,4,128]{2,1,0:T(4,128)S(1)}, u32[]{:S(2)}, u32[]{:S(2)}) collective-permute-start(f32[8,4,128]{2,1,0:T(4,128)S(1)} %get-tuple-element.93), channel_id=1, source_target_pairs={{32,64},{64,32},{96,128},{128,96},{160,192},{192,160},{224,256},{2... | collective-permute-start | bytes 49160 | tf_op jit(solution)/shard_map/ppermute | solution.py:412
  155.2 1.9 %collective-permute-start.22 = (f32[8,4,128]{2,1,0:T(4,128)S(1)}, f32[8,4,128]{2,1,0:T(4,128)S(1)}, u32[]{:S(2)}, u32[]{:S(2)}) collective-permute-start(f32[8,4,128]{2,1,0:T(4,128)S(1)} %get-tuple-element.93), channel_id=1, source_target_pairs={{0,32},{32,0},{64,96},{96,64},{128,160},{160,128},{192,224},{224,1... | collective-permute-start | bytes 49160 | tf_op jit(solution)/shard_map/ppermute | solution.py:411
  157.2 2.2 %shard_map.93.force = f32[8,8,128]{2,1,0:T(8,128)S(1)} custom-call(f32[8,8,128]{2,1,0:T(8,128)S(1)} %get-tuple-element.90.refs_0_.own, f32[4,8,128]{2,1,0:T(8,128)S(1)} %get-tuple-element.91.refs_1_, f32[4,8,128]{2,1,0:T(8,128)S(1)} %get-tuple-element.92.refs_2_), custom_call_target="tpu_custom_call" | custom-call | flops 20000000 | bytes 200000 | tf_op jit(solution)/shard_map/pallas_call | solution.py:397
  159.3 1.4 collective-permute-done.23.from_b
  161.0 15.5 %all_to_all.30.sums = f32[32,1,128]{2,1,0:T(1,128)S(1)} all-to-all(f32[32,1,128]{2,1,0:T(1,128)S(1)} %get-tuple-element.94), channel_id=1, replica_groups=mesh['image'=16,'space'=32] {'space'}, dimensions={0} | all-to-all | bytes 32768 | tf_op jit(solution)/shard_map/all_to_all | solution.py:422
  (33 shorter events, 6.0 us)
Async XLA Ops:
  1.5 17.5 %collective-permute-start = (f32[4,8,128]{2,1,0:T(8,128)S(1)}, f32[4,8,128]{2,1,0:T(8,128)S(1)}, u32[]{:S(2)}, u32[]{:S(2)}) collective-permute-start(f32[4,8,128]{2,1,0:T(8,128)S(1)} %get-tuple-element.51), channel_id=1, source_target_pairs={{0,1},{1,0},{2,3},{3,2},{4,5},{5,4},{6,7},{7,6},{8,9},{9,8},{10,11... | collective-permute-start | bytes 49160 | tf_op jit(solution)/shard_map/ppermute | solution.py:381
  3.4 15.6 %collective-permute-start.1 = (f32[4,8,128]{2,1,0:T(8,128)S(1)}, f32[4,8,128]{2,1,0:T(8,128)S(1)}, u32[]{:S(2)}, u32[]{:S(2)}) collective-permute-start(f32[4,8,128]{2,1,0:T(8,128)S(1)} %get-tuple-element.52), channel_id=1, source_target_pairs={{0,31},{1,2},{2,1},{3,4},{4,3},{5,6},{6,5},{7,8},{8,7},{9,10},{10,... | collective-permute-start | bytes 49160 | tf_op jit(solution)/shard_map/ppermute | solution.py:382
  10.7 10.5 %collective-permute-start.3 = (f32[8,4,128]{2,1,0:T(4,128)S(1)}, f32[8,4,128]{2,1,0:T(4,128)S(1)}, u32[]{:S(2)}, u32[]{:S(2)}) collective-permute-start(f32[8,4,128]{2,1,0:T(4,128)S(1)} %get-tuple-element.53), channel_id=1, source_target_pairs={{32,64},{64,32},{96,128},{128,96},{160,192},{192,160},{224,256},{2... | collective-permute-start | bytes 49160 | tf_op jit(solution)/shard_map/ppermute | solution.py:412
  17.1 5.6 %collective-permute-start.2 = (f32[8,4,128]{2,1,0:T(4,128)S(1)}, f32[8,4,128]{2,1,0:T(4,128)S(1)}, u32[]{:S(2)}, u32[]{:S(2)}) collective-permute-start(f32[8,4,128]{2,1,0:T(4,128)S(1)} %get-tuple-element.53), channel_id=1, source_target_pairs={{0,32},{32,0},{64,96},{96,64},{128,160},{160,128},{192,224},{224,1... | collective-permute-start | bytes 49160 | tf_op jit(solution)/shard_map/ppermute | solution.py:411
  19.0 3.7 %copy-start = (f32[2,3,1024]{2,0,1:T(2,128)S(1)}, f32[2,3,1024]{2,0,1:T(2,128)}, u32[]{:S(2)}) copy-start(f32[2,3,1024]{2,0,1:T(2,128)} %param.7) | copy-start | bytes 73732
  23.4 14.0 %all-to-all-start = ((f32[32,1,128]{2,1,0:T(1,128)}), f32[32,1,128]{2,1,0:T(1,128)S(1)}, u32[]{:S(2)}, u32[]{:S(2)}) async-start(f32[32,1,128]{2,1,0:T(1,128)} %get-tuple-element.54), calls=%async_computation | async-start | bytes 32768 | tf_op jit(solution)/shard_map/all_to_all | solution.py:422
  28.0 8.6 %collective-permute-start.4 = (f32[4,3,4,128]{3,2,1,0:T(4,128)S(1)}, f32[4,3,4,128]{3,2,1,0:T(4,128)S(1)}, u32[]{:S(2)}, u32[]{:S(2)}) collective-permute-start(f32[4,3,4,128]{3,2,1,0:T(4,128)S(1)} %get-tuple-element.56), channel_id=1, source_target_pairs={{0,1},{1,0},{2,3},{3,2},{4,5},{5,4},{6,7},{7,6},{8,9},{9,8},{10,11... | collective-permute-start | bytes 73736 | tf_op jit(solution)/shard_map/ppermute | solution.py:424
  30.2 7.3 %collective-permute-start.5 = (f32[4,3,4,128]{3,2,1,0:T(4,128)S(1)}, f32[4,3,4,128]{3,2,1,0:T(4,128)S(1)}, u32[]{:S(2)}, u32[]{:S(2)}) collective-permute-start(f32[4,3,4,128]{3,2,1,0:T(4,128)S(1)} %get-tuple-element.57), channel_id=1, source_target_pairs={{0,31},{1,2},{2,1},{3,4},{4,3},{5,6},{6,5},{7,8},{8,7},{9,10},{10,... | collective-permute-start | bytes 73736 | tf_op jit(solution)/shard_map/ppermute | solution.py:425
  37.6 9.9 %collective-permute-start.7 = (f32[8,4,128]{2,1,0:T(4,128)S(1)}, f32[8,4,128]{2,1,0:T(4,128)S(1)}, u32[]{:S(2)}, u32[]{:S(2)}) collective-permute-start(f32[8,4,128]{2,1,0:T(4,128)S(1)} %get-tuple-element.61), channel_id=1, source_target_pairs={{32,64},{64,32},{96,128},{128,96},{160,192},{192,160},{224,256},{2... | collective-permute-start | bytes 49160 | tf_op jit(solution)/shard_map/ppermute | solution.py:412
  42.0 5.6 %collective-permute-start.6 = (f32[8,4,128]{2,1,0:T(4,128)S(1)}, f32[8,4,128]{2,1,0:T(4,128)S(1)}, u32[]{:S(2)}, u32[]{:S(2)}) collective-permute-start(f32[8,4,128]{2,1,0:T(4,128)S(1)} %get-tuple-element.61), channel_id=1, source_target_pairs={{0,32},{32,0},{64,96},{96,64},{128,160},{160,128},{192,224},{224,1... | collective-permute-start | bytes 49160 | tf_op jit(solution)/shard_map/ppermute | solution.py:411
  48.4 16.7 %all-to-all-start.1 = ((f32[32,1,128]{2,1,0:T(1,128)}), f32[32,1,128]{2,1,0:T(1,128)S(1)}, u32[]{:S(2)}, u32[]{:S(2)}) async-start(f32[32,1,128]{2,1,0:T(1,128)} %get-tuple-element.62), calls=%async_computation.1 | async-start | bytes 32768 | tf_op jit(solution)/shard_map/all_to_all | solution.py:422
  55.7 7.9 %collective-permute-start.8 = (f32[4,3,4,128]{3,2,1,0:T(4,128)S(1)}, f32[4,3,4,128]{3,2,1,0:T(4,128)S(1)}, u32[]{:S(2)}, u32[]{:S(2)}) collective-permute-start(f32[4,3,4,128]{3,2,1,0:T(4,128)S(1)} %get-tuple-element.64), channel_id=1, source_target_pairs={{0,1},{1,0},{2,3},{3,2},{4,5},{5,4},{6,7},{7,6},{8,9},{9,8},{10,11... | collective-permute-start | bytes 73736 | tf_op jit(solution)/shard_map/ppermute | solution.py:424
  57.9 7.3 %collective-permute-start.9 = (f32[4,3,4,128]{3,2,1,0:T(4,128)S(1)}, f32[4,3,4,128]{3,2,1,0:T(4,128)S(1)}, u32[]{:S(2)}, u32[]{:S(2)}) collective-permute-start(f32[4,3,4,128]{3,2,1,0:T(4,128)S(1)} %get-tuple-element.65), channel_id=1, source_target_pairs={{0,31},{1,2},{2,1},{3,4},{4,3},{5,6},{6,5},{7,8},{8,7},{9,10},{10,... | collective-permute-start | bytes 73736 | tf_op jit(solution)/shard_map/ppermute | solution.py:425
  65.3 9.9 %collective-permute-start.11 = (f32[8,4,128]{2,1,0:T(4,128)S(1)}, f32[8,4,128]{2,1,0:T(4,128)S(1)}, u32[]{:S(2)}, u32[]{:S(2)}) collective-permute-start(f32[8,4,128]{2,1,0:T(4,128)S(1)} %get-tuple-element.69), channel_id=1, source_target_pairs={{32,64},{64,32},{96,128},{128,96},{160,192},{192,160},{224,256},{2... | collective-permute-start | bytes 49160 | tf_op jit(solution)/shard_map/ppermute | solution.py:412
  71.0 5.6 %collective-permute-start.10 = (f32[8,4,128]{2,1,0:T(4,128)S(1)}, f32[8,4,128]{2,1,0:T(4,128)S(1)}, u32[]{:S(2)}, u32[]{:S(2)}) collective-permute-start(f32[8,4,128]{2,1,0:T(4,128)S(1)} %get-tuple-element.69), channel_id=1, source_target_pairs={{0,32},{32,0},{64,96},{96,64},{128,160},{160,128},{192,224},{224,1... | collective-permute-start | bytes 49160 | tf_op jit(solution)/shard_map/ppermute | solution.py:411
  77.4 16.7 %all-to-all-start.2 = ((f32[32,1,128]{2,1,0:T(1,128)}), f32[32,1,128]{2,1,0:T(1,128)S(1)}, u32[]{:S(2)}, u32[]{:S(2)}) async-start(f32[32,1,128]{2,1,0:T(1,128)} %get-tuple-element.70), calls=%async_computation.2 | async-start | bytes 32768 | tf_op jit(solution)/shard_map/all_to_all | solution.py:422
  84.6 7.9 %collective-permute-start.12 = (f32[4,3,4,128]{3,2,1,0:T(4,128)S(1)}, f32[4,3,4,128]{3,2,1,0:T(4,128)S(1)}, u32[]{:S(2)}, u32[]{:S(2)}) collective-permute-start(f32[4,3,4,128]{3,2,1,0:T(4,128)S(1)} %get-tuple-element.72), channel_id=1, source_target_pairs={{0,1},{1,0},{2,3},{3,2},{4,5},{5,4},{6,7},{7,6},{8,9},{9,8},{10,11... | collective-permute-start | bytes 73736 | tf_op jit(solution)/shard_map/ppermute | solution.py:424
  86.8 7.3 %collective-permute-start.13 = (f32[4,3,4,128]{3,2,1,0:T(4,128)S(1)}, f32[4,3,4,128]{3,2,1,0:T(4,128)S(1)}, u32[]{:S(2)}, u32[]{:S(2)}) collective-permute-start(f32[4,3,4,128]{3,2,1,0:T(4,128)S(1)} %get-tuple-element.73), channel_id=1, source_target_pairs={{0,31},{1,2},{2,1},{3,4},{4,3},{5,6},{6,5},{7,8},{8,7},{9,10},{10,... | collective-permute-start | bytes 73736 | tf_op jit(solution)/shard_map/ppermute | solution.py:425
  94.2 9.9 %collective-permute-start.15 = (f32[8,4,128]{2,1,0:T(4,128)S(1)}, f32[8,4,128]{2,1,0:T(4,128)S(1)}, u32[]{:S(2)}, u32[]{:S(2)}) collective-permute-start(f32[8,4,128]{2,1,0:T(4,128)S(1)} %get-tuple-element.77), channel_id=1, source_target_pairs={{32,64},{64,32},{96,128},{128,96},{160,192},{192,160},{224,256},{2... | collective-permute-start | bytes 49160 | tf_op jit(solution)/shard_map/ppermute | solution.py:412
  98.6 5.6 %collective-permute-start.14 = (f32[8,4,128]{2,1,0:T(4,128)S(1)}, f32[8,4,128]{2,1,0:T(4,128)S(1)}, u32[]{:S(2)}, u32[]{:S(2)}) collective-permute-start(f32[8,4,128]{2,1,0:T(4,128)S(1)} %get-tuple-element.77), channel_id=1, source_target_pairs={{0,32},{32,0},{64,96},{96,64},{128,160},{160,128},{192,224},{224,1... | collective-permute-start | bytes 49160 | tf_op jit(solution)/shard_map/ppermute | solution.py:411
  105.0 16.7 %all-to-all-start.3 = ((f32[32,1,128]{2,1,0:T(1,128)}), f32[32,1,128]{2,1,0:T(1,128)S(1)}, u32[]{:S(2)}, u32[]{:S(2)}) async-start(f32[32,1,128]{2,1,0:T(1,128)} %get-tuple-element.78), calls=%async_computation.3 | async-start | bytes 32768 | tf_op jit(solution)/shard_map/all_to_all | solution.py:422
  112.3 7.9 %collective-permute-start.16 = (f32[4,3,4,128]{3,2,1,0:T(4,128)S(1)}, f32[4,3,4,128]{3,2,1,0:T(4,128)S(1)}, u32[]{:S(2)}, u32[]{:S(2)}) collective-permute-start(f32[4,3,4,128]{3,2,1,0:T(4,128)S(1)} %get-tuple-element.80), channel_id=1, source_target_pairs={{0,1},{1,0},{2,3},{3,2},{4,5},{5,4},{6,7},{7,6},{8,9},{9,8},{10,11... | collective-permute-start | bytes 73736 | tf_op jit(solution)/shard_map/ppermute | solution.py:424
  114.5 7.3 %collective-permute-start.17 = (f32[4,3,4,128]{3,2,1,0:T(4,128)S(1)}, f32[4,3,4,128]{3,2,1,0:T(4,128)S(1)}, u32[]{:S(2)}, u32[]{:S(2)}) collective-permute-start(f32[4,3,4,128]{3,2,1,0:T(4,128)S(1)} %get-tuple-element.81), channel_id=1, source_target_pairs={{0,31},{1,2},{2,1},{3,4},{4,3},{5,6},{6,5},{7,8},{8,7},{9,10},{10,... | collective-permute-start | bytes 73736 | tf_op jit(solution)/shard_map/ppermute | solution.py:425
  121.9 10.0 %collective-permute-start.19 = (f32[8,4,128]{2,1,0:T(4,128)S(1)}, f32[8,4,128]{2,1,0:T(4,128)S(1)}, u32[]{:S(2)}, u32[]{:S(2)}) collective-permute-start(f32[8,4,128]{2,1,0:T(4,128)S(1)} %get-tuple-element.85), channel_id=1, source_target_pairs={{32,64},{64,32},{96,128},{128,96},{160,192},{192,160},{224,256},{2... | collective-permute-start | bytes 49160 | tf_op jit(solution)/shard_map/ppermute | solution.py:412
  127.6 5.6 %collective-permute-start.18 = (f32[8,4,128]{2,1,0:T(4,128)S(1)}, f32[8,4,128]{2,1,0:T(4,128)S(1)}, u32[]{:S(2)}, u32[]{:S(2)}) collective-permute-start(f32[8,4,128]{2,1,0:T(4,128)S(1)} %get-tuple-element.85), channel_id=1, source_target_pairs={{0,32},{32,0},{64,96},{96,64},{128,160},{160,128},{192,224},{224,1... | collective-permute-start | bytes 49160 | tf_op jit(solution)/shard_map/ppermute | solution.py:411
  134.0 16.7 %all-to-all-start.4 = ((f32[32,1,128]{2,1,0:T(1,128)}), f32[32,1,128]{2,1,0:T(1,128)S(1)}, u32[]{:S(2)}, u32[]{:S(2)}) async-start(f32[32,1,128]{2,1,0:T(1,128)} %get-tuple-element.86), calls=%async_computation.4 | async-start | bytes 32768 | tf_op jit(solution)/shard_map/all_to_all | solution.py:422
  141.2 7.9 %collective-permute-start.20 = (f32[4,3,4,128]{3,2,1,0:T(4,128)S(1)}, f32[4,3,4,128]{3,2,1,0:T(4,128)S(1)}, u32[]{:S(2)}, u32[]{:S(2)}) collective-permute-start(f32[4,3,4,128]{3,2,1,0:T(4,128)S(1)} %get-tuple-element.88), channel_id=1, source_target_pairs={{0,1},{1,0},{2,3},{3,2},{4,5},{5,4},{6,7},{7,6},{8,9},{9,8},{10,11... | collective-permute-start | bytes 73736 | tf_op jit(solution)/shard_map/ppermute | solution.py:424
  143.4 7.3 %collective-permute-start.21 = (f32[4,3,4,128]{3,2,1,0:T(4,128)S(1)}, f32[4,3,4,128]{3,2,1,0:T(4,128)S(1)}, u32[]{:S(2)}, u32[]{:S(2)}) collective-permute-start(f32[4,3,4,128]{3,2,1,0:T(4,128)S(1)} %get-tuple-element.89), channel_id=1, source_target_pairs={{0,31},{1,2},{2,1},{3,4},{4,3},{5,6},{6,5},{7,8},{8,7},{9,10},{10,... | collective-permute-start | bytes 73736 | tf_op jit(solution)/shard_map/ppermute | solution.py:425
  150.8 9.9 %collective-permute-start.23 = (f32[8,4,128]{2,1,0:T(4,128)S(1)}, f32[8,4,128]{2,1,0:T(4,128)S(1)}, u32[]{:S(2)}, u32[]{:S(2)}) collective-permute-start(f32[8,4,128]{2,1,0:T(4,128)S(1)} %get-tuple-element.93), channel_id=1, source_target_pairs={{32,64},{64,32},{96,128},{128,96},{160,192},{192,160},{224,256},{2... | collective-permute-start | bytes 49160 | tf_op jit(solution)/shard_map/ppermute | solution.py:412
  155.2 5.6 %collective-permute-start.22 = (f32[8,4,128]{2,1,0:T(4,128)S(1)}, f32[8,4,128]{2,1,0:T(4,128)S(1)}, u32[]{:S(2)}, u32[]{:S(2)}) collective-permute-start(f32[8,4,128]{2,1,0:T(4,128)S(1)} %get-tuple-element.93), channel_id=1, source_target_pairs={{0,32},{32,0},{64,96},{96,64},{128,160},{160,128},{192,224},{224,1... | collective-permute-start | bytes 49160 | tf_op jit(solution)/shard_map/ppermute | solution.py:411
